TPU v7x, 128 devices: a whole 4x4x4 slice. The times are simulated.
128 devices in a mesh: row: 16 (over z_lo, y, core), col: 8 (over z_hi, x).
Axes of the slice: x: 4, y: 4, z: 4 (z_hi: 2, z_lo: 2; z = z_hi * 2 + z_lo), core: 2. Of those that a mesh axis runs over, the one named last changes fastest.
Arguments:
- activations: bfloat16 [3072, 16384], P(('row', 'col')), may hold values from -14 to 14
- tenant_ids: int32 [3072], P(('row', 'col')), may hold values from 0 to 63
- concept_labels: int32 [3072], P(('row', 'col')), may hold values from 0 to 1
Outputs:
- covariance: float32 [16384, 16384], P('row', 'col')
- cross: float32 [128, 16384], P(None, ('row', 'col'))
All inputs are finite; a program needn't handle non-finite values.
Results may differ from a plain program's by a relative error of at most 0.0003.
Values may be sent and summed in bfloat16 or wider, within the bound.
A program may use at most 128 MiB of HBM per device.

v0:
```python
import jax
import jax.numpy as jnp
from jax import lax
from jax.sharding import PartitionSpec as P

TENANTS = 64
LABELS = 2


def shards(activations, tenant_ids, concept_labels):
    local_tokens = activations.shape[0]
    width = activations.shape[1]
    row_count = lax.axis_size("row")
    col_count = lax.axis_size("col")
    groups = TENANTS * LABELS
    codes = tenant_ids * LABELS + concept_labels
    codes_rows = lax.all_gather(codes, "row", axis=0, tiled=True)
    row_piece = lax.all_to_all(activations, "row", split_axis=1, concat_axis=0, tiled=True)
    row_panel, codes_all = (
        lax.all_gather(row_piece, "col", axis=0, tiled=True),
        lax.all_gather(codes_rows, "col", axis=0, tiled=True),
    )
    total = row_panel.shape[0]
    row_width = row_panel.shape[1]
    row_view = row_panel.reshape(col_count, row_count, local_tokens, row_width)
    col_piece = lax.all_to_all(activations, "col", split_axis=1, concat_axis=0, tiled=True)
    col_panel = lax.all_gather(col_piece, "row", axis=0, tiled=True)
    col_view = col_panel.reshape(row_count, col_count, local_tokens, col_panel.shape[1])
    gram = jnp.einsum("abtf,batg->fg", row_view, col_view, preferred_element_type=jnp.float32)
    mean_row = jnp.sum(row_panel, axis=0, dtype=jnp.float32) / total
    mean_col = jnp.sum(col_panel, axis=0, dtype=jnp.float32) / total
    covariance = gram / total - mean_row[:, None] * mean_col[None, :]
    slice_width = width // (row_count * col_count)
    slice_start = lax.axis_index("col") * slice_width
    mean_slice = lax.dynamic_slice_in_dim(mean_row, slice_start, slice_width)
    group_ids = jnp.arange(groups, dtype=jnp.int32)
    onehot_all = codes_all[:, None] == group_ids[None, :]
    counts = jnp.sum(onehot_all.astype(jnp.float32), axis=0)
    panel_slice = lax.dynamic_slice_in_dim(row_panel, slice_start, slice_width, 1)
    sums = lax.dot_general(
        onehot_all.astype(jnp.bfloat16),
        panel_slice,
        (((0,), (0,)), ((), ())),
        preferred_element_type=jnp.float32,
    )
    cross = groups / total * (sums - counts[:, None] * mean_slice[None, :])
    return (covariance, cross)


def solution(mesh):
    placed = (P(("row", "col"), None), P(("row", "col")), P(("row", "col")))
    return jax.shard_map(
        shards,
        mesh=mesh,
        in_specs=placed,
        out_specs=(P("row", "col"), P(None, ("row", "col"))),
        check_vma=False,
    )
```

profile of v0, /device:TPU:1, one launch (start us, length us, event | category | flops | bytes accessed | tf_op | source)
XLA Modules:
  0.0 226.1 jit_solution(3943468472371128695)
XLA Ops:
  7.2 0.0 all-gather.4.cloned.1.call-start
  7.2 1.2 copy.29
  8.4 20.0 %all_to_all.38 = bf16[24,16,1024]{2,0,1:T(8,128)(2,1)} all-to-all(bf16[24,16,1024]{2,0,1:T(8,128)(2,1)S(1)} %bitcast.31), channel_id=1, replica_groups=mesh['row'=16,'col'=8] {'row'}, dimensions={1} | all-to-all | bytes 1572864 | tf_op jit(solution)/shard_map/all_to_all | solution.py:18
  28.4 0.0 all-gather.4.cloned.1.call-update
  28.5 0.0 all-gather.6.cloned.1.call-start
  28.5 1.2 copy.28
  29.7 22.4 %all_to_all.39 = bf16[24,8,2048]{2,0,1:T(8,128)(2,1)} all-to-all(bf16[24,8,2048]{2,0,1:T(8,128)(2,1)S(1)} %bitcast.32), channel_id=1, replica_groups=mesh['row'=16,'col'=8] {'col'}, dimensions={1} | all-to-all | bytes 1572864 | tf_op jit(solution)/shard_map/all_to_all | solution.py:26
  52.1 0.0 all-gather.6.cloned.1.call-update
  52.1 1.2 dynamic-slice
  54.0 0.8 add_dynamic-update-slice_fusion
  54.8 10.8 %all-reduce = s32[384]{0:T(512)S(1)} all-reduce(s32[384]{0:T(512)S(1)} %add_dynamic-update-slice_fusion), channel_id=1, replica_groups=mesh['row'=16,'col'=8] {'row'}, use_global_device_ids=true, to_apply=%add | all-reduce | flops 384 | bytes 3072
  65.6 26.1 %all-gather = s32[8,1,384]{2,1,0:T(1,128)S(1)} all-gather(s32[1,1,384]{2,1,0:T(1,128)S(1)} %reshape.30), channel_id=1, replica_groups=mesh['row'=16,'col'=8] {'col'}, dimensions={0}, use_global_device_ids=true | all-gather | bytes 13824 | tf_op jit(solution)/shard_map/all_gather | solution.py:21
  91.7 1.4 convert_reduce_fusion.2
  93.1 28.6 %all-gather.4.cloned.1.call-done = bf16[3072,1024]{1,0:T(8,128)(2,1)} async-done(((bf16[384,1024]{1,0:T(8,128)(2,1)}), bf16[3072,1024]{1,0:T(8,128)(2,1)}) %all-gather.4.cloned.1.call-update) | async-done | bytes 6291472 | tf_op jit(solution)/shard_map/all_gather | solution.py:20
  121.7 3.7 %convert_reduce_fusion.1 = f32[1024]{0:T(1024)S(1)} fusion(bf16[3072,1024]{1,0:T(8,128)(2,1)} %all-gather.4.cloned.1.call-done), kind=kLoop, calls=%fused_computation.3 | loop fusion | flops 6290432 | bytes 6295552 | tf_op jit(solution)/shard_map/reduce_sum | solution.py:30
  125.4 0.1 dynamic_slice.7
  125.5 2.8 %fusion.7 = f32[128,128]{1,0:T(8,128)} fusion(bf16[3072,1024]{1,0:T(8,128)(2,1)} %all-gather.4.cloned.1.call-done, s32[]{:T(128)S(6)} %select_n.4, s32[3072]{0:T(1024)S(1)} %bitcast.34, f32[128]{0:T(128)S(1)} %dynamic_slice.7, f32[128]{0:T(128)S(1)} %convert_reduce_fusion.2), kind=kOutput, calls=%fused_computation.10 | convolution fusion | flops 101105664 | bytes 865284 | tf_op jit(solution)/shard_map/dot_general | solution.py:40
  128.4 65.5 %all-gather.6.cloned.1.call-done = bf16[3072,2048]{1,0:T(8,128)(2,1)} async-done(((bf16[192,2048]{1,0:T(8,128)(2,1)}), bf16[3072,2048]{1,0:T(8,128)(2,1)}) %all-gather.6.cloned.1.call-update) | async-done | bytes 12582928 | tf_op jit(solution)/shard_map/all_gather | solution.py:27
  193.9 6.5 %convert_reduce_fusion = f32[2048]{0:T(1024)S(1)} fusion(bf16[3072,2048]{1,0:T(8,128)(2,1)} %all-gather.6.cloned.1.call-done), kind=kLoop, calls=%fused_computation | loop fusion | flops 12580864 | bytes 12591104 | tf_op jit(solution)/shard_map/reduce_sum | solution.py:31
  200.4 18.9 %fusion.2 = f32[1024,2048]{1,0:T(8,128)} fusion(bf16[8,16,24,1024]{3,2,1,0:T(8,128)(2,1)} %bitcast.26, bf16[16,8,24,2048]{3,2,1,0:T(8,128)(2,1)} %bitcast.25, f32[2048]{0:T(1024)S(1)} %broadcast_multiply_fusion, f32[1024]{0:T(1024)S(1)} %broadcast_multiply_fusion.1), kind=kOutput, calls=%fused_computation.5 | convolution fusion | flops 12891193344 | bytes 27275264 | tf_op jit(solution)/shard_map/abtf,batg->fg/dot_general | solution.py:29
  (4 shorter events, 0.0 us)
Async XLA Ops:
  7.2 114.5 %all-gather.4.cloned.1.call-start = ((), (), s32[]{:S(2)}) async-start(), calls=%async_computation.2 | async-start | bytes 7077888 | tf_op jit(solution)/shard_map/all_gather | solution.py:20
  28.5 165.4 %all-gather.6.cloned.1.call-start = ((), (), s32[]{:S(2)}) async-start(), calls=%async_computation.3 | async-start | bytes 13369344 | tf_op jit(solution)/shard_map/all_gather | solution.py:27
Sparse Core Ops, SparseCore 0:
  28.6 93.0 all-gather.3
  123.4 70.4 all-gather.5
where the time goes:
time: 227 us; the launch traced here: 226 us
  waiting for transfers between devices  94.2 us (41%)
  blocking collectives  79.3 us (35%)
  matrix products  21.8 us (10%)
  between operations  14.7 us (6%)
  other arithmetic  12.3 us (5%)
  local copies, waits for them, and re-layouts  3.72 us (2%)
    all_gather x1, waiting for transfers between devices, shards(): col_panel = lax.all_gather(col_piece, 'row', axis=0, tiled=True)  65.5 us
    all_gather x1, waiting for transfers between devices, shards(): lax.all_gather(row_piece, 'col', axis=0, tiled=True)  28.6 us
    all_gather x1, blocking collectives, shards(): lax.all_gather(codes_rows, 'col', axis=0, tiled=True)  26.1 us
    all_to_all x1, blocking collectives, shards(): lax.all_to_all(activations, 'col', split_axis=1, concat_axis=0, tiled=True)  22.4 us
    all_to_all x1, blocking collectives, shards(): lax.all_to_all(activations, 'row', split_axis=1, concat_axis=0, tiled=True)  20 us
    dot_general x1, matrix products, shards(): jnp.einsum('abtf,batg->fg', row_view, col_view, preferred_element_type=jn...  18.9 us
    unnamed x1, blocking collectives  10.8 us
    reduce_sum x1, other arithmetic, shards(): mean_col = jnp.sum(col_panel, axis=0, dtype=jnp.float32) / total  6.45 us
  transfers between devices with their start and end apart: 2, of which 2 were waited for; matrix products, arithmetic and copies ran while one was open for 5% of the time, Pallas kernels for 0%

commit v1 on v0

--- a/solution.py
+++ b/solution.py
@@ -1,10 +1,115 @@
+import functools
+
 import jax
 import jax.numpy as jnp
 from jax import lax
+from jax.experimental import pallas as pl
+from jax.experimental.pallas import tpu as pltpu
 from jax.sharding import PartitionSpec as P
 
 TENANTS = 64
 LABELS = 2
+MESH = pl.DeviceIdType.MESH
+
+
+def _row_panel_kernel(n_row, n_col, x_ref, code_ref, p_ref, pc_ref,
+                      sa, ra, sac, rac, sb, rb, sbc, rbc, lsem):
+    r = lax.axis_index("row")
+    c = lax.axis_index("col")
+    width = p_ref.shape[-1]
+
+    barrier = pltpu.get_barrier_semaphore()
+    for k in range(1, n_row):
+        pl.semaphore_signal(barrier, 1, device_id=(lax.rem(r + k, n_row), c), device_id_type=MESH)
+    for k in range(1, n_col):
+        pl.semaphore_signal(barrier, 1, device_id=(r, lax.rem(c + k, n_col)), device_id_type=MESH)
+    pl.semaphore_wait(barrier, (n_row - 1) + (n_col - 1))
+
+    own = pltpu.make_async_copy(
+        x_ref.at[:, pl.ds(pl.multiple_of(r * width, width), width)], p_ref.at[c, r], lsem.at[0])
+    own_codes = pltpu.make_async_copy(code_ref, pc_ref.at[c, r], lsem.at[1])
+    own.start()
+    own_codes.start()
+    phase_a = []
+    for k in range(1, n_row):
+        dst = lax.rem(r + k, n_row)
+        cp = pltpu.make_async_remote_copy(
+            src_ref=x_ref.at[:, pl.ds(pl.multiple_of(dst * width, width), width)],
+            dst_ref=p_ref.at[c, r],
+            send_sem=sa.at[k - 1],
+            recv_sem=ra.at[k - 1],
+            device_id=(dst, c),
+            device_id_type=MESH,
+        )
+        cc = pltpu.make_async_remote_copy(
+            src_ref=code_ref,
+            dst_ref=pc_ref.at[c, r],
+            send_sem=sac.at[k - 1],
+            recv_sem=rac.at[k - 1],
+            device_id=(dst, c),
+            device_id_type=MESH,
+        )
+        cp.start()
+        cc.start()
+        phase_a.append(cp)
+        phase_a.append(cc)
+    own.wait()
+    own_codes.wait()
+    for cp in phase_a:
+        cp.wait()
+
+    phase_b = []
+    for k in range(1, n_col):
+        dst = lax.rem(c + k, n_col)
+        cp = pltpu.make_async_remote_copy(
+            src_ref=p_ref.at[c],
+            dst_ref=p_ref.at[c],
+            send_sem=sb.at[k - 1],
+            recv_sem=rb.at[k - 1],
+            device_id=(r, dst),
+            device_id_type=MESH,
+        )
+        cc = pltpu.make_async_remote_copy(
+            src_ref=pc_ref.at[c],
+            dst_ref=pc_ref.at[c],
+            send_sem=sbc.at[k - 1],
+            recv_sem=rbc.at[k - 1],
+            device_id=(r, dst),
+            device_id_type=MESH,
+        )
+        cp.start()
+        cc.start()
+        phase_b.append(cp)
+        phase_b.append(cc)
+    for cp in phase_b:
+        cp.wait()
+
+
+def _row_panel(activations, codes, n_row, n_col):
+    tokens = activations.shape[0]
+    width = activations.shape[1] // n_row
+    any_spec = pl.BlockSpec(memory_space=pl.ANY)
+    return pl.pallas_call(
+        functools.partial(_row_panel_kernel, n_row, n_col),
+        out_shape=(
+            jax.ShapeDtypeStruct((n_col, n_row, tokens, width), activations.dtype),
+            jax.ShapeDtypeStruct((n_col, n_row, 1, tokens), jnp.int32),
+        ),
+        in_specs=[any_spec, any_spec],
+        out_specs=(any_spec, any_spec),
+        scratch_shapes=[
+            pltpu.SemaphoreType.DMA((n_row - 1,)),
+            pltpu.SemaphoreType.DMA((n_row - 1,)),
+            pltpu.SemaphoreType.DMA((n_row - 1,)),
+            pltpu.SemaphoreType.DMA((n_row - 1,)),
+            pltpu.SemaphoreType.DMA((n_col - 1,)),
+            pltpu.SemaphoreType.DMA((n_col - 1,)),
+            pltpu.SemaphoreType.DMA((n_col - 1,)),
+            pltpu.SemaphoreType.DMA((n_col - 1,)),
+            pltpu.SemaphoreType.DMA((2,)),
+        ],
+        compiler_params=pltpu.CompilerParams(collective_id=0, has_side_effects=True),
+    )(activations, codes.reshape(1, tokens))
 
 
 def shards(activations, tenant_ids, concept_labels):
@@ -14,17 +119,14 @@
     col_count = lax.axis_size("col")
     groups = TENANTS * LABELS
     codes = tenant_ids * LABELS + concept_labels
-    codes_rows = lax.all_gather(codes, "row", axis=0, tiled=True)
-    row_piece = lax.all_to_all(activations, "row", split_axis=1, concat_axis=0, tiled=True)
-    row_panel, codes_all = (
-        lax.all_gather(row_piece, "col", axis=0, tiled=True),
-        lax.all_gather(codes_rows, "col", axis=0, tiled=True),
-    )
-    total = row_panel.shape[0]
-    row_width = row_panel.shape[1]
-    row_view = row_panel.reshape(col_count, row_count, local_tokens, row_width)
     col_piece = lax.all_to_all(activations, "col", split_axis=1, concat_axis=0, tiled=True)
     col_panel = lax.all_gather(col_piece, "row", axis=0, tiled=True)
+    row_slots, code_slots = _row_panel(activations, codes, row_count, col_count)
+    total = col_panel.shape[0]
+    row_width = row_slots.shape[-1]
+    row_panel = row_slots.reshape(total, row_width)
+    codes_all = code_slots.reshape(total)
+    row_view = row_slots
     col_view = col_panel.reshape(row_count, col_count, local_tokens, col_panel.shape[1])
     gram = jnp.einsum("abtf,batg->fg", row_view, col_view, preferred_element_type=jnp.float32)
     mean_row = jnp.sum(row_panel, axis=0, dtype=jnp.float32) / total

time: 227 us -> 209 us (0.921)
  Pallas kernels: 0 us -> 124 us
  waiting for transfers between devices: 94.2 us -> 10.9 us
  blocking collectives: 79.3 us -> 21.6 us
    pallas_call x0 -> x1, Pallas kernels: none -> 124 us  [_row_panel(): pl.pallas_call(functools.partial(_row_panel_kernel, n_row, n_col), out_sh...]
    all_gather x1, waiting for transfers between devices: 65.5 us -> 10.9 us  [shards(): col_panel = lax.all_gather(col_piece, 'row', axis=0, tiled=True)]
    all_gather x1 -> x0, waiting for transfers between devices: 28.6 us -> none  [shards(): lax.all_gather(row_piece, 'col', axis=0, tiled=True)]
    all_gather x1 -> x0, blocking collectives: 26.1 us -> none  [shards(): lax.all_gather(codes_rows, 'col', axis=0, tiled=True)]
    all_to_all x1 -> x0, blocking collectives: 20 us -> none  [shards(): lax.all_to_all(activations, 'row', split_axis=1, concat_axis=0, tiled=True)]
    unnamed x1 -> x0, blocking collectives: 10.8 us -> none
  transfers between devices with their start and end apart: 2 -> 1, of which waited for: 2 -> 1; matrix products, arithmetic and copies ran while one was open for 5% -> 6% of each run, Pallas kernels for 0% -> 59%
where the time goes in v1:
time: 209 us; the launch traced here: 208 us
  Pallas kernels  124 us (59%)
  matrix products  21.8 us (10%)
  blocking collectives  21.6 us (10%)
  other arithmetic  14.5 us (7%)
  between operations  14.1 us (7%)
  waiting for transfers between devices  10.9 us (5%)
    pallas_call x1, Pallas kernels, _row_panel(): pl.pallas_call(functools.partial(_row_panel_kernel, n_row, n_col), out_sh...  124 us
    all_to_all x1, blocking collectives, shards(): lax.all_to_all(activations, 'col', split_axis=1, concat_axis=0, tiled=True)  21.6 us
    dot_general x1, matrix products, shards(): jnp.einsum('abtf,batg->fg', row_view, col_view, preferred_element_type=jn...  18.9 us
    all_gather x1, waiting for transfers between devices, shards(): col_panel = lax.all_gather(col_piece, 'row', axis=0, tiled=True)  10.9 us
    reduce_sum x1, other arithmetic, shards(): mean_col = jnp.sum(col_panel, axis=0, dtype=jnp.float32) / total  6.45 us
  transfers between devices with their start and end apart: 1, of which 1 were waited for; matrix products, arithmetic and copies ran while one was open for 6% of the time, Pallas kernels for 59%

profile of v1, /device:TPU:1, one launch (start us, length us, event | category | flops | bytes accessed | tf_op | source)
XLA Modules:
  0.0 208.3 jit_solution(15885143959336049545)
XLA Ops:
  7.2 0.0 all-gather.2.cloned.1.call-start
  7.2 1.2 copy.19
  8.4 21.6 %all_to_all.19 = bf16[24,8,2048]{2,0,1:T(8,128)(2,1)} all-to-all(bf16[24,8,2048]{2,0,1:T(8,128)(2,1)S(1)} %bitcast.22), channel_id=1, replica_groups=mesh['row'=16,'col'=8] {'col'}, dimensions={1} | all-to-all | bytes 1572864 | tf_op jit(solution)/shard_map/all_to_all | solution.py:122
  30.0 0.0 all-gather.2.cloned.1.call-update
  30.0 1.2 add_bitcast_fusion.code_ref
  31.2 123.5 %shard_map.50 = (bf16[8,16,24,1024]{3,2,1,0:T(8,128)(2,1)}, s32[8,16,1,24]{3,2,1,0:T(1,128)}) custom-call(bf16[24,16384]{1,0:T(8,128)(2,1)} %x_ref.1, s32[1,24]{1,0:T(1,128)} %add_bitcast_fusion.code_ref), custom_call_target="tpu_custom_call" | custom-call | tf_op jit(solution)/shard_map/pallas_call | solution.py:92
  154.7 0.5 broadcast.21
  155.2 1.7 reduce.4
  156.9 0.1 eq.15
  157.0 3.9 %convert_reduce_fusion.1 = f32[1024]{0:T(1024)S(1)} fusion(bf16[8,16,24,1024]{3,2,1,0:T(8,128)(2,1)} %get-tuple-element.4), kind=kLoop, calls=%fused_computation.3 | loop fusion | flops 6290432 | bytes 6295552 | tf_op jit(solution)/shard_map/reduce_sum | solution.py:132
  160.9 0.1 dynamic_slice.7
  160.9 1.4 convert_reduce_fusion.2
  162.3 2.9 %fusion.7 = f32[128,128]{1,0:T(8,128)} fusion(bf16[3072,1024]{1,0:T(8,128)(2,1)} %bitcast.19, s32[]{:T(128)S(6)} %select_n.4, s32[3072]{0:T(1024)S(1)} %eq.15, f32[128]{0:T(128)S(1)} %dynamic_slice.7, f32[128]{0:T(128)S(1)} %convert_reduce_fusion.2), kind=kOutput, calls=%fused_computation.10 | convolution fusion | flops 101105664 | bytes 865284 | tf_op jit(solution)/shard_map/dot_general | solution.py:142
  165.2 10.9 %all-gather.2.cloned.1.call-done = bf16[3072,2048]{1,0:T(8,128)(2,1)} async-done(((bf16[192,2048]{1,0:T(8,128)(2,1)}), bf16[3072,2048]{1,0:T(8,128)(2,1)}) %all-gather.2.cloned.1.call-update) | async-done | bytes 12582928 | tf_op jit(solution)/shard_map/all_gather | solution.py:123
  176.1 6.5 %convert_reduce_fusion = f32[2048]{0:T(1024)S(1)} fusion(bf16[3072,2048]{1,0:T(8,128)(2,1)} %all-gather.2.cloned.1.call-done), kind=kLoop, calls=%fused_computation | loop fusion | flops 12580864 | bytes 12591104 | tf_op jit(solution)/shard_map/reduce_sum | solution.py:133
  182.5 18.9 %fusion.2 = f32[1024,2048]{1,0:T(8,128)} fusion(bf16[8,16,24,1024]{3,2,1,0:T(8,128)(2,1)} %get-tuple-element.4, bf16[16,8,24,2048]{3,2,1,0:T(8,128)(2,1)} %bitcast.18, f32[2048]{0:T(1024)S(1)} %broadcast_multiply_fusion, f32[1024]{0:T(1024)S(1)} %broadcast_multiply_fusion.1), kind=kOutput, calls=%fused_computation.5 | convolution fusion | flops 12891193344 | bytes 27275264 | tf_op jit(solution)/shard_map/abtf,batg->fg/dot_general | solution.py:131
  (2 shorter events, 0.0 us)
Async XLA Ops:
  7.2 168.9 %all-gather.2.cloned.1.call-start = ((), (), s32[]{:S(2)}) async-start(), calls=%async_computation.1 | async-start | bytes 13369344 | tf_op jit(solution)/shard_map/all_gather | solution.py:123
Sparse Core Ops, SparseCore 0:
  30.1 145.9 all-gather.1

commit v2 on v0

--- a/solution.py
+++ b/solution.py
@@ -1,10 +1,175 @@
+import functools
+
 import jax
 import jax.numpy as jnp
 from jax import lax
+from jax.experimental import pallas as pl
+from jax.experimental.pallas import tpu as pltpu
 from jax.sharding import PartitionSpec as P
 
 TENANTS = 64
 LABELS = 2
+MESH = pl.DeviceIdType.MESH
+Z_HI = 2
+
+
+def _row_panel_kernel(n_row, n_x, x_ref, code_ref, p_ref, pc_ref,
+                      s1, r1, s1c, r1c, s2, r2, s2c, r2c, lsem):
+    r = lax.axis_index("row")
+    c = lax.axis_index("col")
+    zh = c // n_x
+    x = lax.rem(c, n_x)
+    width = p_ref.shape[-1]
+    group = Z_HI * n_row
+    me_q = zh * n_row + r
+    left = zh * n_x + lax.rem(x + n_x - 1, n_x)
+    right = zh * n_x + lax.rem(x + 1, n_x)
+
+    def peer(j):
+        q = lax.rem(me_q + j, group)
+        return q % n_row, (q // n_row) * n_x + x
+
+    barrier = pltpu.get_barrier_semaphore()
+    for j in range(1, group):
+        pl.semaphore_signal(barrier, 1, device_id=peer(j), device_id_type=MESH)
+    pl.semaphore_signal(barrier, 1, device_id=(r, left), device_id_type=MESH)
+    pl.semaphore_signal(barrier, 1, device_id=(r, right), device_id_type=MESH)
+    pl.semaphore_wait(barrier, group + 1)
+
+    own = pltpu.make_async_copy(
+        x_ref.at[:, pl.ds(pl.multiple_of(r * width, width), width)], p_ref.at[x, zh, r], lsem.at[0])
+    own_codes = pltpu.make_async_copy(code_ref, pc_ref.at[x, zh, r], lsem.at[1])
+    own.start()
+    own_codes.start()
+    stage1 = []
+    for j in range(1, group):
+        pr, pc = peer(j)
+        cp = pltpu.make_async_remote_copy(
+            src_ref=x_ref.at[:, pl.ds(pl.multiple_of(pr * width, width), width)],
+            dst_ref=p_ref.at[x, zh, r],
+            send_sem=s1.at[j - 1],
+            recv_sem=r1.at[j - 1],
+            device_id=(pr, pc),
+            device_id_type=MESH,
+        )
+        cc = pltpu.make_async_remote_copy(
+            src_ref=code_ref,
+            dst_ref=pc_ref.at[x, zh, r],
+            send_sem=s1c.at[j - 1],
+            recv_sem=r1c.at[j - 1],
+            device_id=(pr, pc),
+            device_id_type=MESH,
+        )
+        cp.start()
+        cc.start()
+        stage1.append(cp)
+        stage1.append(cc)
+    own.wait()
+    own_codes.wait()
+    for cp in stage1:
+        cp.wait()
+
+    def send(src, dst, sems, idx, target):
+        return pltpu.make_async_remote_copy(
+            src_ref=src, dst_ref=dst, send_sem=sems[0].at[idx], recv_sem=sems[1].at[idx],
+            device_id=(r, target), device_id_type=MESH)
+
+    a_right = send(p_ref.at[x], p_ref.at[x], (s2, r2), 0, right)
+    a_left = send(p_ref.at[x], p_ref.at[x], (s2, r2), 1, left)
+    ac_right = send(pc_ref.at[x], pc_ref.at[x], (s2c, r2c), 0, right)
+    ac_left = send(pc_ref.at[x], pc_ref.at[x], (s2c, r2c), 1, left)
+    for cp in (a_right, a_left, ac_right, ac_left):
+        cp.start()
+    for cp in (a_right, a_left, ac_right, ac_left):
+        cp.wait()
+
+    from_left = lax.rem(x + n_x - 1, n_x)
+    from_right = lax.rem(x + 1, n_x)
+    b_right = send(p_ref.at[from_left, 0], p_ref.at[from_left, 0], (s2, r2), 2, right)
+    b_left = send(p_ref.at[from_right, 1], p_ref.at[from_right, 1], (s2, r2), 3, left)
+    bc_right = send(pc_ref.at[from_left, 0], pc_ref.at[from_left, 0], (s2c, r2c), 2, right)
+    bc_left = send(pc_ref.at[from_right, 1], pc_ref.at[from_right, 1], (s2c, r2c), 3, left)
+    for cp in (b_right, b_left, bc_right, bc_left):
+        cp.start()
+    for cp in (b_right, b_left, bc_right, bc_left):
+        cp.wait()
+
+
+def _row_panel(activations, codes, n_row, n_col):
+    tokens = activations.shape[0]
+    width = activations.shape[1] // n_row
+    n_x = n_col // Z_HI
+    assert n_x == 4
+    group = Z_HI * n_row
+    any_spec = pl.BlockSpec(memory_space=pl.ANY)
+    return pl.pallas_call(
+        functools.partial(_row_panel_kernel, n_row, n_x),
+        out_shape=(
+            jax.ShapeDtypeStruct((n_x, Z_HI, n_row, tokens, width), activations.dtype),
+            jax.ShapeDtypeStruct((n_x, Z_HI, n_row, 1, tokens), jnp.int32),
+        ),
+        in_specs=[any_spec, any_spec],
+        out_specs=(any_spec, any_spec),
+        scratch_shapes=[
+            pltpu.SemaphoreType.DMA((group - 1,)),
+            pltpu.SemaphoreType.DMA((group - 1,)),
+            pltpu.SemaphoreType.DMA((group - 1,)),
+            pltpu.SemaphoreType.DMA((group - 1,)),
+            pltpu.SemaphoreType.DMA((4,)),
+            pltpu.SemaphoreType.DMA((4,)),
+            pltpu.SemaphoreType.DMA((4,)),
+            pltpu.SemaphoreType.DMA((4,)),
+            pltpu.SemaphoreType.DMA((2,)),
+        ],
+        compiler_params=pltpu.CompilerParams(collective_id=0, has_side_effects=True),
+    )(activations, codes.reshape(1, tokens))
+
+
+def _col_piece_kernel(n_col, x_ref, o_ref, send_sem, recv_sem, lsem):
+    r = lax.axis_index("row")
+    c = lax.axis_index("col")
+    width = o_ref.shape[-1]
+    barrier = pltpu.get_barrier_semaphore()
+    for k in range(1, n_col):
+        pl.semaphore_signal(barrier, 1, device_id=(r, lax.rem(c + k, n_col)), device_id_type=MESH)
+    pl.semaphore_wait(barrier, n_col - 1)
+    own = pltpu.make_async_copy(
+        x_ref.at[:, pl.ds(pl.multiple_of(c * width, width), width)], o_ref.at[c], lsem.at[0])
+    own.start()
+    copies = []
+    for k in range(1, n_col):
+        dst = lax.rem(c + k, n_col)
+        cp = pltpu.make_async_remote_copy(
+            src_ref=x_ref.at[:, pl.ds(pl.multiple_of(dst * width, width), width)],
+            dst_ref=o_ref.at[c],
+            send_sem=send_sem.at[k - 1],
+            recv_sem=recv_sem.at[k - 1],
+            device_id=(r, dst),
+            device_id_type=MESH,
+        )
+        cp.start()
+        copies.append(cp)
+    own.wait()
+    for cp in copies:
+        cp.wait()
+
+
+def _col_piece(activations, n_col):
+    tokens = activations.shape[0]
+    width = activations.shape[1] // n_col
+    any_spec = pl.BlockSpec(memory_space=pl.ANY)
+    return pl.pallas_call(
+        functools.partial(_col_piece_kernel, n_col),
+        out_shape=jax.ShapeDtypeStruct((n_col, tokens, width), activations.dtype),
+        in_specs=[any_spec],
+        out_specs=any_spec,
+        scratch_shapes=[
+            pltpu.SemaphoreType.DMA((n_col - 1,)),
+            pltpu.SemaphoreType.DMA((n_col - 1,)),
+            pltpu.SemaphoreType.DMA((1,)),
+        ],
+        compiler_params=pltpu.CompilerParams(collective_id=1, has_side_effects=True),
+    )(activations)
 
 
 def shards(activations, tenant_ids, concept_labels):
@@ -12,21 +177,19 @@
     width = activations.shape[1]
     row_count = lax.axis_size("row")
     col_count = lax.axis_size("col")
+    n_x = col_count // Z_HI
     groups = TENANTS * LABELS
     codes = tenant_ids * LABELS + concept_labels
-    codes_rows = lax.all_gather(codes, "row", axis=0, tiled=True)
-    row_piece = lax.all_to_all(activations, "row", split_axis=1, concat_axis=0, tiled=True)
-    row_panel, codes_all = (
-        lax.all_gather(row_piece, "col", axis=0, tiled=True),
-        lax.all_gather(codes_rows, "col", axis=0, tiled=True),
-    )
-    total = row_panel.shape[0]
-    row_width = row_panel.shape[1]
-    row_view = row_panel.reshape(col_count, row_count, local_tokens, row_width)
-    col_piece = lax.all_to_all(activations, "col", split_axis=1, concat_axis=0, tiled=True)
+    col_piece = _col_piece(activations, col_count)
+    col_piece = col_piece.reshape(col_count * local_tokens, col_piece.shape[-1])
     col_panel = lax.all_gather(col_piece, "row", axis=0, tiled=True)
-    col_view = col_panel.reshape(row_count, col_count, local_tokens, col_panel.shape[1])
-    gram = jnp.einsum("abtf,batg->fg", row_view, col_view, preferred_element_type=jnp.float32)
+    row_slots, code_slots = _row_panel(activations, codes, row_count, col_count)
+    total = col_panel.shape[0]
+    row_width = row_slots.shape[-1]
+    row_panel = row_slots.reshape(total, row_width)
+    codes_all = code_slots.reshape(total)
+    col_view = col_panel.reshape(row_count, Z_HI, n_x, local_tokens, col_panel.shape[1])
+    gram = jnp.einsum("xhrtf,rhxtg->fg", row_slots, col_view, preferred_element_type=jnp.float32)
     mean_row = jnp.sum(row_panel, axis=0, dtype=jnp.float32) / total
     mean_col = jnp.sum(col_panel, axis=0, dtype=jnp.float32) / total
     covariance = gram / total - mean_row[:, None] * mean_col[None, :]

time: 227 us -> 165 us (0.73)
  Pallas kernels: 0 us -> 114 us
  waiting for transfers between devices: 94.2 us -> 0.02 us
  blocking collectives: 79.3 us -> 0 us
  local copies, waits for them, and re-layouts: 3.72 us -> 0.68 us
    pallas_call x0 -> x2, Pallas kernels: none -> 114 us  [the longest x1 97.3 us: _row_panel(): pl.pallas_call(functools.partial(_row_panel_kernel, n_row, n_x), out_shap...]
    all_gather x1, waiting for transfers between devices: 65.5 us -> 0.01 us  [shards(): col_panel = lax.all_gather(col_piece, 'row', axis=0, tiled=True)]
    all_to_all x2 -> x0, blocking collectives: 42.4 us -> none  [the longest x1 22.4 us: shards(): lax.all_to_all(activations, 'col', split_axis=1, concat_axis=0, tiled=True)]
    all_gather x1 -> x0, waiting for transfers between devices: 28.6 us -> none  [shards(): lax.all_gather(row_piece, 'col', axis=0, tiled=True)]
    all_gather x1 -> x0, blocking collectives: 26.1 us -> none  [shards(): lax.all_gather(codes_rows, 'col', axis=0, tiled=True)]
    unnamed x1 -> x0, blocking collectives: 10.8 us -> none
    all_to_all x2 -> x0, local copies, waits for them, and re-layouts: 2.39 us -> none  [the longest x1 1.2 us: shards(): lax.all_to_all(activations, 'col', split_axis=1, concat_axis=0, tiled=True)]
  transfers between devices with their start and end apart: 2 -> 1, of which waited for: 2 -> 0; matrix products, arithmetic and copies ran while one was open for 5% -> 7% of each run, Pallas kernels for 0% -> 59%
where the time goes in v2:
time: 165 us
  Pallas kernels  114 us (69%)
  matrix products  21.8 us (13%)
  other arithmetic  14.4 us (9%)
  between operations  14.1 us (9%)
    pallas_call x1, Pallas kernels, _row_panel(): pl.pallas_call(functools.partial(_row_panel_kernel, n_row, n_x), out_shap...  97.3 us
    dot_general x1, matrix products, shards(): jnp.einsum('xhrtf,rhxtg->fg', row_slots, col_view, preferred_element_type...  18.9 us
    pallas_call x1, Pallas kernels, _col_piece(): pl.pallas_call(functools.partial(_col_piece_kernel, n_col), out_shape=jax...  16.9 us
    reduce_sum x1, other arithmetic, shards(): mean_col = jnp.sum(col_panel, axis=0, dtype=jnp.float32) / total  6.45 us
    reduce_sum x1, other arithmetic, shards(): mean_row = jnp.sum(row_panel, axis=0, dtype=jnp.float32) / total  3.74 us
  transfers between devices with their start and end apart: 1, of which 0 were waited for; matrix products, arithmetic and copies ran while one was open for 7% of the time, Pallas kernels for 59%

profile of v2, /device:TPU:1, one launch (start us, length us, event | category | flops | bytes accessed | tf_op | source)
XLA Modules:
  0.0 165.2 jit_solution(1489350503578636002)
XLA Ops:
  7.2 0.0 all-gather.2.cloned.1.call-start
  7.2 16.9 %shard_map.51 = bf16[8,24,2048]{2,1,0:T(8,128)(2,1)} custom-call(bf16[24,16384]{1,0:T(8,128)(2,1)} %x_ref.3), custom_call_target="tpu_custom_call" | custom-call | tf_op jit(solution)/shard_map/pallas_call | solution.py:161
  24.1 0.0 all-gather.2.cloned.1.call-update
  24.1 1.2 add_bitcast_fusion.code_ref
  25.3 97.3 %shard_map.50 = (bf16[4,2,16,24,1024]{4,3,2,1,0:T(8,128)(2,1)}, s32[4,2,16,1,24]{4,3,2,1,0:T(1,128)}) custom-call(bf16[24,16384]{1,0:T(8,128)(2,1)} %x_ref.3, s32[1,24]{1,0:T(1,128)} %add_bitcast_fusion.code_ref), custom_call_target="tpu_custom_call" | custom-call | tf_op jit(solution)/shard_map/pallas_call | solution.py:105
  122.7 0.5 broadcast.21
  123.2 1.6 reduce.4
  124.8 0.1 eq.15
  124.9 3.7 %convert_reduce_fusion.1 = f32[1024]{0:T(1024)S(1)} fusion(bf16[4,2,16,24,1024]{4,3,2,1,0:T(8,128)(2,1)} %get-tuple-element.4), kind=kLoop, calls=%fused_computation.3 | loop fusion | flops 6290432 | bytes 6295552 | tf_op jit(solution)/shard_map/reduce_sum | solution.py:193
  128.7 0.1 dynamic_slice.7
  128.7 1.4 convert_reduce_fusion.2
  130.1 2.8 %fusion.10 = f32[128,128]{1,0:T(8,128)} fusion(bf16[3072,1024]{1,0:T(8,128)(2,1)} %bitcast.13, s32[]{:T(128)S(6)} %select_n.4, s32[3072]{0:T(1024)S(1)} %eq.15, f32[128]{0:T(128)S(1)} %dynamic_slice.7, f32[128]{0:T(128)S(1)} %convert_reduce_fusion.2), kind=kOutput, calls=%fused_computation.11 | convolution fusion | flops 101105664 | bytes 865284 | tf_op jit(solution)/shard_map/dot_general | solution.py:203
  132.9 0.0 all-gather.2.cloned.1.call-done
  132.9 6.5 %convert_reduce_fusion = f32[2048]{0:T(1024)S(1)} fusion(bf16[3072,2048]{1,0:T(8,128)(2,1)} %all-gather.2.cloned.1.call-done), kind=kLoop, calls=%fused_computation | loop fusion | flops 12580864 | bytes 12591104 | tf_op jit(solution)/shard_map/reduce_sum | solution.py:194
  139.4 18.9 %fusion.2 = f32[1024,2048]{1,0:T(8,128)} fusion(bf16[16,2,4,24,2048]{4,3,2,1,0:T(8,128)(2,1)} %bitcast.12, bf16[4,2,16,24,1024]{4,3,2,1,0:T(8,128)(2,1)} %get-tuple-element.4, f32[2048]{0:T(1024)S(1)} %broadcast_multiply_fusion, f32[1024]{0:T(1024)S(1)} %broadcast_multiply_fusion.1), kind=kOutput, calls=%fused_computation.5 | convolution fusion | flops 12891193344 | bytes 27275264 | tf_op jit(solution)/shard_map/xhrtf,rhxtg->fg/dot_general | solution.py:192
  (2 shorter events, 0.0 us)
Async XLA Ops:
  7.2 125.8 %all-gather.2.cloned.1.call-start = ((), (), s32[]{:S(2)}) async-start(), calls=%async_computation | async-start | bytes 13369344 | tf_op jit(solution)/shard_map/all_gather | solution.py:185
Sparse Core Ops, SparseCore 0:
  24.2 87.6 all-gather.1

commit v3 on v2

--- a/solution.py
+++ b/solution.py
@@ -20,78 +20,98 @@
     zh = c // n_x
     x = lax.rem(c, n_x)
     width = p_ref.shape[-1]
-    group = Z_HI * n_row
-    me_q = zh * n_row + r
     left = zh * n_x + lax.rem(x + n_x - 1, n_x)
     right = zh * n_x + lax.rem(x + 1, n_x)
-
-    def peer(j):
-        q = lax.rem(me_q + j, group)
-        return q % n_row, (q // n_row) * n_x + x
+    sources = [(dz, dr) for dz in range(Z_HI) for dr in range(n_row) if dz or dr]
+
+    def peer(dz, dr):
+        return lax.rem(r + dr, n_row), lax.rem(zh + dz, Z_HI) * n_x + x
 
     barrier = pltpu.get_barrier_semaphore()
-    for j in range(1, group):
-        pl.semaphore_signal(barrier, 1, device_id=peer(j), device_id_type=MESH)
+    for dz, dr in sources:
+        pl.semaphore_signal(barrier, 1, device_id=peer(dz, dr), device_id_type=MESH)
     pl.semaphore_signal(barrier, 1, device_id=(r, left), device_id_type=MESH)
     pl.semaphore_signal(barrier, 1, device_id=(r, right), device_id_type=MESH)
-    pl.semaphore_wait(barrier, group + 1)
+    pl.semaphore_wait(barrier, len(sources) + 2)
 
     own = pltpu.make_async_copy(
         x_ref.at[:, pl.ds(pl.multiple_of(r * width, width), width)], p_ref.at[x, zh, r], lsem.at[0])
     own_codes = pltpu.make_async_copy(code_ref, pc_ref.at[x, zh, r], lsem.at[1])
     own.start()
     own_codes.start()
-    stage1 = []
-    for j in range(1, group):
-        pr, pc = peer(j)
+    stage1 = {0: [], 1: []}
+    for i, (dz, dr) in enumerate(sources):
+        pr, pc = peer(dz, dr)
         cp = pltpu.make_async_remote_copy(
             src_ref=x_ref.at[:, pl.ds(pl.multiple_of(pr * width, width), width)],
             dst_ref=p_ref.at[x, zh, r],
-            send_sem=s1.at[j - 1],
-            recv_sem=r1.at[j - 1],
+            send_sem=s1.at[i],
+            recv_sem=r1.at[i],
             device_id=(pr, pc),
             device_id_type=MESH,
         )
         cc = pltpu.make_async_remote_copy(
             src_ref=code_ref,
             dst_ref=pc_ref.at[x, zh, r],
-            send_sem=s1c.at[j - 1],
-            recv_sem=r1c.at[j - 1],
+            send_sem=s1c.at[i],
+            recv_sem=r1c.at[i],
             device_id=(pr, pc),
             device_id_type=MESH,
         )
         cp.start()
         cc.start()
-        stage1.append(cp)
-        stage1.append(cc)
-    own.wait()
-    own_codes.wait()
-    for cp in stage1:
-        cp.wait()
+        stage1[min(dz, 1)] += [cp, cc]
 
     def send(src, dst, sems, idx, target):
         return pltpu.make_async_remote_copy(
             src_ref=src, dst_ref=dst, send_sem=sems[0].at[idx], recv_sem=sems[1].at[idx],
             device_id=(r, target), device_id_type=MESH)
 
-    a_right = send(p_ref.at[x], p_ref.at[x], (s2, r2), 0, right)
-    a_left = send(p_ref.at[x], p_ref.at[x], (s2, r2), 1, left)
-    ac_right = send(pc_ref.at[x], pc_ref.at[x], (s2c, r2c), 0, right)
-    ac_left = send(pc_ref.at[x], pc_ref.at[x], (s2c, r2c), 1, left)
-    for cp in (a_right, a_left, ac_right, ac_left):
-        cp.start()
-    for cp in (a_right, a_left, ac_right, ac_left):
-        cp.wait()
+    own.wait()
+    own_codes.wait()
+    halves = []
+    for h, plane in enumerate((zh, 1 - zh)):
+        for cp in stage1[h]:
+            cp.wait_recv()
+        pair = [
+            send(p_ref.at[x, plane], p_ref.at[x, plane], (s2, r2), 2 * h, right),
+            send(p_ref.at[x, plane], p_ref.at[x, plane], (s2, r2), 2 * h + 1, left),
+            send(pc_ref.at[x, plane], pc_ref.at[x, plane], (s2c, r2c), 2 * h, right),
+            send(pc_ref.at[x, plane], pc_ref.at[x, plane], (s2c, r2c), 2 * h + 1, left),
+        ]
+        for cp in pair:
+            cp.start()
+        halves.append(pair)
 
     from_left = lax.rem(x + n_x - 1, n_x)
     from_right = lax.rem(x + 1, n_x)
-    b_right = send(p_ref.at[from_left, 0], p_ref.at[from_left, 0], (s2, r2), 2, right)
-    b_left = send(p_ref.at[from_right, 1], p_ref.at[from_right, 1], (s2, r2), 3, left)
-    bc_right = send(pc_ref.at[from_left, 0], pc_ref.at[from_left, 0], (s2c, r2c), 2, right)
-    bc_left = send(pc_ref.at[from_right, 1], pc_ref.at[from_right, 1], (s2c, r2c), 3, left)
-    for cp in (b_right, b_left, bc_right, bc_left):
-        cp.start()
-    for cp in (b_right, b_left, bc_right, bc_left):
+    halves[0][0].wait_recv()
+    halves[0][2].wait_recv()
+    fwd = [
+        send(p_ref.at[from_left, zh], p_ref.at[from_left, zh], (s2, r2), 4, right),
+        send(pc_ref.at[from_left, zh], pc_ref.at[from_left, zh], (s2c, r2c), 4, right),
+    ]
+    for cp in fwd:
+        cp.start()
+    halves[1][1].wait_recv()
+    halves[1][3].wait_recv()
+    fwd2 = [
+        send(p_ref.at[from_right, 1 - zh], p_ref.at[from_right, 1 - zh], (s2, r2), 5, left),
+        send(pc_ref.at[from_right, 1 - zh], pc_ref.at[from_right, 1 - zh], (s2c, r2c), 5, left),
+    ]
+    for cp in fwd2:
+        cp.start()
+
+    for cp in stage1[0] + stage1[1]:
+        cp.wait_send()
+    for pair in halves:
+        for cp in pair:
+            cp.wait_send()
+    halves[0][1].wait_recv()
+    halves[0][3].wait_recv()
+    halves[1][0].wait_recv()
+    halves[1][2].wait_recv()
+    for cp in fwd + fwd2:
         cp.wait()
 
 
@@ -115,10 +135,10 @@
             pltpu.SemaphoreType.DMA((group - 1,)),
             pltpu.SemaphoreType.DMA((group - 1,)),
             pltpu.SemaphoreType.DMA((group - 1,)),
-            pltpu.SemaphoreType.DMA((4,)),
-            pltpu.SemaphoreType.DMA((4,)),
-            pltpu.SemaphoreType.DMA((4,)),
-            pltpu.SemaphoreType.DMA((4,)),
+            pltpu.SemaphoreType.DMA((6,)),
+            pltpu.SemaphoreType.DMA((6,)),
+            pltpu.SemaphoreType.DMA((6,)),
+            pltpu.SemaphoreType.DMA((6,)),
             pltpu.SemaphoreType.DMA((2,)),
         ],
         compiler_params=pltpu.CompilerParams(collective_id=0, has_side_effects=True),

time: 165 us -> 148 us (0.90)
  Pallas kernels: 114 us -> 96.3 us
    pallas_call x1, Pallas kernels: 97.3 us -> 79.4 us  [_row_panel(): pl.pallas_call(functools.partial(_row_panel_kernel, n_row, n_x), out_shap...]
  transfers between devices with their start and end apart: 1 -> 1, of which waited for: 0 -> 0; matrix products, arithmetic and copies ran while one was open for 7% -> 8% of each run, Pallas kernels for 59% -> 54%
where the time goes in v3:
time: 148 us; the launch traced here: 147 us
  Pallas kernels  96.3 us (65%)
  matrix products  21.8 us (15%)
  other arithmetic  14.5 us (10%)
  between operations  14.1 us (10%)
    pallas_call x1, Pallas kernels, _row_panel(): pl.pallas_call(functools.partial(_row_panel_kernel, n_row, n_x), out_shap...  79.4 us
    dot_general x1, matrix products, shards(): jnp.einsum('xhrtf,rhxtg->fg', row_slots, col_view, preferred_element_type...  18.9 us
    pallas_call x1, Pallas kernels, _col_piece(): pl.pallas_call(functools.partial(_col_piece_kernel, n_col), out_shape=jax...  16.9 us
    reduce_sum x1, other arithmetic, shards(): mean_col = jnp.sum(col_panel, axis=0, dtype=jnp.float32) / total  6.45 us
    reduce_sum x1, other arithmetic, shards(): mean_row = jnp.sum(row_panel, axis=0, dtype=jnp.float32) / total  3.8 us
  transfers between devices with their start and end apart: 1, of which 0 were waited for; matrix products, arithmetic and copies ran while one was open for 8% of the time, Pallas kernels for 54%

profile of v3, /device:TPU:1, one launch (start us, length us, event | category | flops | bytes accessed | tf_op | source)
XLA Modules:
  0.0 147.3 jit_solution(10383689535172723124)
XLA Ops:
  7.2 0.0 all-gather.2.cloned.1.call-start
  7.2 16.9 %shard_map.51 = bf16[8,24,2048]{2,1,0:T(8,128)(2,1)} custom-call(bf16[24,16384]{1,0:T(8,128)(2,1)} %x_ref.3), custom_call_target="tpu_custom_call" | custom-call | tf_op jit(solution)/shard_map/pallas_call | solution.py:181
  24.1 0.0 all-gather.2.cloned.1.call-update
  24.1 1.2 add_bitcast_fusion.code_ref
  25.3 79.4 %shard_map.50 = (bf16[4,2,16,24,1024]{4,3,2,1,0:T(8,128)(2,1)}, s32[4,2,16,1,24]{4,3,2,1,0:T(1,128)}) custom-call(bf16[24,16384]{1,0:T(8,128)(2,1)} %x_ref.3, s32[1,24]{1,0:T(1,128)} %add_bitcast_fusion.code_ref), custom_call_target="tpu_custom_call" | custom-call | tf_op jit(solution)/shard_map/pallas_call | solution.py:125
  104.7 0.5 broadcast.21
  105.2 1.6 %reduce.4 = s32[4,2,16,24]{3,2,1,0:T(8,128)S(1)} reduce(s32[4,2,16,1,24]{4,3,2,1,0:T(1,128)} %get-tuple-element.5, s32[]{:T(128)} %broadcast.21), dimensions={3}, to_apply=%get-tuple-element.5.reduce_sub_computation.3 | reduce | bytes 24580 | tf_op jit(solution)/shard_map/pallas_call | solution.py:125
  106.9 0.1 eq.15
  107.0 3.8 %convert_reduce_fusion.1 = f32[1024]{0:T(1024)S(1)} fusion(bf16[4,2,16,24,1024]{4,3,2,1,0:T(8,128)(2,1)} %get-tuple-element.4), kind=kLoop, calls=%fused_computation.3 | loop fusion | flops 6290432 | bytes 6295552 | tf_op jit(solution)/shard_map/reduce_sum | solution.py:213
  110.8 0.1 dynamic_slice.7
  110.9 1.4 convert_reduce_fusion.2
  112.2 2.8 %fusion.10 = f32[128,128]{1,0:T(8,128)} fusion(bf16[3072,1024]{1,0:T(8,128)(2,1)} %bitcast.13, s32[]{:T(128)S(6)} %select_n.4, s32[3072]{0:T(1024)S(1)} %eq.15, f32[128]{0:T(128)S(1)} %dynamic_slice.7, f32[128]{0:T(128)S(1)} %convert_reduce_fusion.2), kind=kOutput, calls=%fused_computation.11 | convolution fusion | flops 101105664 | bytes 865284 | tf_op jit(solution)/shard_map/dot_general | solution.py:223
  115.1 0.0 all-gather.2.cloned.1.call-done
  115.1 6.5 %convert_reduce_fusion = f32[2048]{0:T(1024)S(1)} fusion(bf16[3072,2048]{1,0:T(8,128)(2,1)} %all-gather.2.cloned.1.call-done), kind=kLoop, calls=%fused_computation | loop fusion | flops 12580864 | bytes 12591104 | tf_op jit(solution)/shard_map/reduce_sum | solution.py:214
  121.5 18.9 %fusion.2 = f32[1024,2048]{1,0:T(8,128)} fusion(bf16[16,2,4,24,2048]{4,3,2,1,0:T(8,128)(2,1)} %bitcast.12, bf16[4,2,16,24,1024]{4,3,2,1,0:T(8,128)(2,1)} %get-tuple-element.4, f32[2048]{0:T(1024)S(1)} %broadcast_multiply_fusion, f32[1024]{0:T(1024)S(1)} %broadcast_multiply_fusion.1), kind=kOutput, calls=%fused_computation.5 | convolution fusion | flops 12891193344 | bytes 27275264 | tf_op jit(solution)/shard_map/xhrtf,rhxtg->fg/dot_general | solution.py:212
  (2 shorter events, 0.0 us)
Async XLA Ops:
  7.2 107.9 %all-gather.2.cloned.1.call-start = ((), (), s32[]{:S(2)}) async-start(), calls=%async_computation | async-start | bytes 13369344 | tf_op jit(solution)/shard_map/all_gather | solution.py:205
Sparse Core Ops, SparseCore 0:
  24.2 87.5 all-gather.1

commit v4 on v3

--- a/solution.py
+++ b/solution.py
@@ -142,10 +142,10 @@
             pltpu.SemaphoreType.DMA((2,)),
         ],
         compiler_params=pltpu.CompilerParams(collective_id=0, has_side_effects=True),
-    )(activations, codes.reshape(1, tokens))
-
-
-def _col_piece_kernel(n_col, x_ref, o_ref, send_sem, recv_sem, lsem):
+    )(activations, codes)
+
+
+def _col_piece_kernel(n_col, x_ref, code_ref, o_ref, code_out, send_sem, recv_sem, lsem):
     r = lax.axis_index("row")
     c = lax.axis_index("col")
     width = o_ref.shape[-1]
@@ -169,27 +169,41 @@
         )
         cp.start()
         copies.append(cp)
+    keep = pltpu.make_async_copy(code_ref, code_out, lsem.at[1])
+    keep.start()
     own.wait()
+    keep.wait()
     for cp in copies:
         cp.wait()
 
 
-def _col_piece(activations, n_col):
+def _col_piece(activations, codes, n_col):
     tokens = activations.shape[0]
     width = activations.shape[1] // n_col
     any_spec = pl.BlockSpec(memory_space=pl.ANY)
     return pl.pallas_call(
         functools.partial(_col_piece_kernel, n_col),
-        out_shape=jax.ShapeDtypeStruct((n_col, tokens, width), activations.dtype),
-        in_specs=[any_spec],
-        out_specs=any_spec,
+        out_shape=(
+            jax.ShapeDtypeStruct((n_col, tokens, width), activations.dtype),
+            jax.ShapeDtypeStruct(codes.shape, codes.dtype),
+        ),
+        in_specs=[any_spec, any_spec],
+        out_specs=(any_spec, any_spec),
         scratch_shapes=[
             pltpu.SemaphoreType.DMA((n_col - 1,)),
             pltpu.SemaphoreType.DMA((n_col - 1,)),
-            pltpu.SemaphoreType.DMA((1,)),
+            pltpu.SemaphoreType.DMA((2,)),
         ],
         compiler_params=pltpu.CompilerParams(collective_id=1, has_side_effects=True),
-    )(activations)
+    )(activations, codes)
+
+
+def _column_sum(panel):
+    rows = panel.shape[0]
+    part = 32 if rows % 32 == 0 else 1
+    first = jnp.sum(panel.reshape(rows // part, part, panel.shape[1]), axis=1, dtype=jnp.float32)
+    first = lax.optimization_barrier(first)
+    return jnp.sum(first, axis=0)
 
 
 def shards(activations, tenant_ids, concept_labels):
@@ -200,30 +214,29 @@
     n_x = col_count // Z_HI
     groups = TENANTS * LABELS
     codes = tenant_ids * LABELS + concept_labels
-    col_piece = _col_piece(activations, col_count)
+    col_piece, codes = _col_piece(activations, codes.reshape(1, local_tokens), col_count)
     col_piece = col_piece.reshape(col_count * local_tokens, col_piece.shape[-1])
     col_panel = lax.all_gather(col_piece, "row", axis=0, tiled=True)
     row_slots, code_slots = _row_panel(activations, codes, row_count, col_count)
     total = col_panel.shape[0]
     row_width = row_slots.shape[-1]
     row_panel = row_slots.reshape(total, row_width)
-    codes_all = code_slots.reshape(total)
     col_view = col_panel.reshape(row_count, Z_HI, n_x, local_tokens, col_panel.shape[1])
     gram = jnp.einsum("xhrtf,rhxtg->fg", row_slots, col_view, preferred_element_type=jnp.float32)
-    mean_row = jnp.sum(row_panel, axis=0, dtype=jnp.float32) / total
-    mean_col = jnp.sum(col_panel, axis=0, dtype=jnp.float32) / total
+    mean_row = _column_sum(row_panel) / total
+    mean_col = _column_sum(col_panel) / total
     covariance = gram / total - mean_row[:, None] * mean_col[None, :]
     slice_width = width // (row_count * col_count)
     slice_start = lax.axis_index("col") * slice_width
     mean_slice = lax.dynamic_slice_in_dim(mean_row, slice_start, slice_width)
     group_ids = jnp.arange(groups, dtype=jnp.int32)
-    onehot_all = codes_all[:, None] == group_ids[None, :]
-    counts = jnp.sum(onehot_all.astype(jnp.float32), axis=0)
-    panel_slice = lax.dynamic_slice_in_dim(row_panel, slice_start, slice_width, 1)
-    sums = lax.dot_general(
+    onehot_all = code_slots[..., None] == group_ids
+    counts = jnp.sum(onehot_all.astype(jnp.float32), axis=(0, 1, 2, 3, 4))
+    panel_slice = lax.dynamic_slice_in_dim(row_slots, slice_start, slice_width, 4)
+    sums = jnp.einsum(
+        "xhrotg,xhrtf->gf",
         onehot_all.astype(jnp.bfloat16),
         panel_slice,
-        (((0,), (0,)), ((), ())),
         preferred_element_type=jnp.float32,
     )
     cross = groups / total * (sums - counts[:, None] * mean_slice[None, :])

time: 148 us -> 150 us (1.014)
  other arithmetic: 14.5 us -> 17 us
    reduce_sum x3 -> x5, other arithmetic: 11.6 us -> 15.8 us  [the longest x2 14.2 us: _column_sum(): jnp.sum(panel.reshape(rows // part, part, panel.shape[1]), axis=1, dtype=...]
    pallas_call x1 -> x0, other arithmetic: 1.65 us -> none  [_row_panel(): pl.pallas_call(functools.partial(_row_panel_kernel, n_row, n_x), out_shap...]
  transfers between devices with their start and end apart: 1 -> 1, of which waited for: 0 -> 0; matrix products, arithmetic and copies ran while one was open for 8% -> 7% of each run, Pallas kernels for 54% -> 53%
where the time goes in v4:
time: 150 us; the launch traced here: 149 us
  Pallas kernels  95.6 us (64%)
  matrix products  21.8 us (15%)
  other arithmetic  17 us (11%)
  between operations  14.1 us (9%)
    pallas_call x1, Pallas kernels, _row_panel(): pl.pallas_call(functools.partial(_row_panel_kernel, n_row, n_x), out_shap...  78.8 us
    dot_general x1, matrix products, shards(): jnp.einsum('xhrtf,rhxtg->fg', row_slots, col_view, preferred_element_type...  18.9 us
    pallas_call x1, Pallas kernels, _col_piece(): pl.pallas_call(functools.partial(_col_piece_kernel, n_col), out_shape=(ja...  16.8 us
    reduce_sum x2, other arithmetic, _column_sum(): jnp.sum(panel.reshape(rows // part, part, panel.shape[1]), axis=1, dtype=...  14.2 us
  transfers between devices with their start and end apart: 1, of which 0 were waited for; matrix products, arithmetic and copies ran while one was open for 7% of the time, Pallas kernels for 53%

profile of v4, /device:TPU:1, one launch (start us, length us, event | category | flops | bytes accessed | tf_op | source)
XLA Modules:
  0.0 149.5 jit_solution(11407389872767686200)
XLA Ops:
  7.2 0.0 all-gather.2.cloned.1.call-start
  7.2 1.2 add_bitcast_fusion.code_ref
  8.4 16.8 %shard_map.50 = (bf16[8,24,2048]{2,1,0:T(8,128)(2,1)}, s32[1,24]{1,0:T(1,128)}) custom-call(bf16[24,16384]{1,0:T(8,128)(2,1)} %x_ref.3, s32[1,24]{1,0:T(1,128)} %add_bitcast_fusion.code_ref), custom_call_target="tpu_custom_call" | custom-call | tf_op jit(solution)/shard_map/pallas_call | solution.py:184
  25.2 0.0 all-gather.2.cloned.1.call-update
  25.2 78.8 %shard_map.51 = (bf16[4,2,16,24,1024]{4,3,2,1,0:T(8,128)(2,1)}, s32[4,2,16,1,24]{4,3,2,1,0:T(1,128)}) custom-call(bf16[24,16384]{1,0:T(8,128)(2,1)} %x_ref.3, s32[1,24]{1,0:T(1,128)} %get-tuple-element.6.code_ref), custom_call_target="tpu_custom_call" | custom-call | tf_op jit(solution)/shard_map/pallas_call | solution.py:125
  104.1 5.1 %convert_reduce_fusion.1 = f32[96,1024]{1,0:T(8,128)S(1)} fusion(bf16[96,32,1024]{2,1,0:T(8,128)(2,1)} %bitcast.25), kind=kLoop, calls=%fused_computation.1 | loop fusion | flops 6193152 | bytes 6684672 | tf_op jit(solution)/shard_map/reduce_sum | solution.py:204
  109.2 0.9 copy.14
  110.1 0.1 dynamic_slice.7
  110.2 1.5 convert_reduce_fusion.2
  111.7 2.8 %fusion.11 = f32[128,128]{1,0:T(8,128)} fusion(s32[4,2,16,24]{3,0,2,1:T(4,128)S(1)} %copy.14, f32[128]{0:T(128)S(1)} %dynamic_slice.7, f32[128]{0:T(128)S(1)} %convert_reduce_fusion.2, bf16[4,2,16,24,1024]{4,3,2,1,0:T(8,128)(2,1)} %get-tuple-element.7, s32[]{:T(128)S(6)} %select_n.4), kind=kOutput, calls=%fused_computation.13 | convolution fusion | flops 101105664 | bytes 865284 | tf_op jit(solution)/shard_map/xhrotg,xhrtf->gf/dot_general | solution.py:236
  114.5 0.0 all-gather.2.cloned.1.call-done
  114.5 9.1 %convert_reduce_fusion = f32[96,2048]{1,0:T(8,128)S(1)} fusion(bf16[96,32,2048]{2,1,0:T(8,128)(2,1)} %bitcast.23), kind=kLoop, calls=%fused_computation | loop fusion | flops 12386304 | bytes 13369344 | tf_op jit(solution)/shard_map/reduce_sum | solution.py:204
  123.7 0.1 reduce_sum.52
  123.7 18.9 %fusion.2 = f32[1024,2048]{1,0:T(8,128)} fusion(bf16[16,2,4,24,2048]{4,3,2,1,0:T(8,128)(2,1)} %bitcast.24, bf16[4,2,16,24,1024]{4,3,2,1,0:T(8,128)(2,1)} %get-tuple-element.7, f32[2048]{0:T(1024)S(1)} %broadcast_multiply_fusion, f32[1024]{0:T(1024)S(1)} %broadcast_multiply_fusion.1), kind=kOutput, calls=%fused_computation.5 | convolution fusion | flops 12891193344 | bytes 27275264 | tf_op jit(solution)/shard_map/xhrtf,rhxtg->fg/dot_general | solution.py:225
  (3 shorter events, 0.0 us)
Async XLA Ops:
  7.2 107.4 %all-gather.2.cloned.1.call-start = ((), (), s32[]{:S(2)}) async-start(), calls=%async_computation | async-start | bytes 13369344 | tf_op jit(solution)/shard_map/all_gather | solution.py:219
Sparse Core Ops, SparseCore 0:
  25.3 86.6 all-gather.1

commit v5 on v4

--- a/solution.py
+++ b/solution.py
@@ -199,11 +199,8 @@
 
 
 def _column_sum(panel):
-    rows = panel.shape[0]
-    part = 32 if rows % 32 == 0 else 1
-    first = jnp.sum(panel.reshape(rows // part, part, panel.shape[1]), axis=1, dtype=jnp.float32)
-    first = lax.optimization_barrier(first)
-    return jnp.sum(first, axis=0)
+    ones = jnp.ones((8, panel.shape[0]), panel.dtype)
+    return jnp.dot(ones, panel, preferred_element_type=jnp.float32)[0]
 
 
 def shards(activations, tenant_ids, concept_labels):

time: 150 us -> 146 us (0.973)
  other arithmetic: 17 us -> 2.53 us
  matrix products: 21.8 us -> 30.7 us
  local copies, waits for them, and re-layouts: 0.97 us -> 2.59 us
    reduce_sum x4 -> x0, other arithmetic: 14.3 us -> none  [the longest x2 14.2 us: _column_sum(): jnp.sum(panel.reshape(rows // part, part, panel.shape[1]), axis=1, dtype=...]
    dot_general x0 -> x2, matrix products: none -> 10.2 us  [_column_sum(): return jnp.dot(ones, panel, preferred_element_type=jnp.float32)[0]]
    unnamed x0 -> x2, local copies, waits for them, and re-layouts: none -> 1.7 us
  transfers between devices with their start and end apart: 1 -> 1, of which waited for: 0 -> 0; matrix products, arithmetic and copies ran while one was open for 7% -> 6% of each run, Pallas kernels for 53% -> 54%
where the time goes in v5:
time: 146 us; the launch traced here: 145 us
  Pallas kernels  95.5 us (65%)
  matrix products  30.7 us (21%)
  between operations  14.1 us (10%)
  local copies, waits for them, and re-layouts  2.59 us (2%)
  other arithmetic  2.53 us (2%)
    pallas_call x1, Pallas kernels, _row_panel(): pl.pallas_call(functools.partial(_row_panel_kernel, n_row, n_x), out_shap...  78.8 us
    dot_general x1, matrix products, shards(): jnp.einsum('xhrtf,rhxtg->fg', row_slots, col_view, preferred_element_type...  17.6 us
    pallas_call x1, Pallas kernels, _col_piece(): pl.pallas_call(functools.partial(_col_piece_kernel, n_col), out_shape=(ja...  16.8 us
    dot_general x2, matrix products, _column_sum(): return jnp.dot(ones, panel, preferred_element_type=jnp.float32)[0]  10.2 us
  transfers between devices with their start and end apart: 1, of which 0 were waited for; matrix products, arithmetic and copies ran while one was open for 6% of the time, Pallas kernels for 54%

profile of v5, /device:TPU:1, one launch (start us, length us, event | category | flops | bytes accessed | tf_op | source)
XLA Modules:
  0.0 145.4 jit_solution(17753515336917131275)
XLA Ops:
  7.2 0.0 all-gather.2.cloned.1.call-start
  7.2 1.2 add_bitcast_fusion.code_ref
  8.4 16.8 %shard_map.50 = (bf16[8,24,2048]{2,1,0:T(8,128)(2,1)}, s32[1,24]{1,0:T(1,128)}) custom-call(bf16[24,16384]{1,0:T(8,128)(2,1)} %x_ref.3, s32[1,24]{1,0:T(1,128)} %add_bitcast_fusion.code_ref), custom_call_target="tpu_custom_call" | custom-call | tf_op jit(solution)/shard_map/pallas_call | solution.py:184
  25.2 0.0 all-gather.2.cloned.1.call-update
  25.2 78.8 %shard_map.51 = (bf16[4,2,16,24,1024]{4,3,2,1,0:T(8,128)(2,1)}, s32[4,2,16,1,24]{4,3,2,1,0:T(1,128)}) custom-call(bf16[24,16384]{1,0:T(8,128)(2,1)} %x_ref.3, s32[1,24]{1,0:T(1,128)} %get-tuple-element.6.code_ref), custom_call_target="tpu_custom_call" | custom-call | tf_op jit(solution)/shard_map/pallas_call | solution.py:125
  104.0 0.9 copy.14
  104.9 3.8 %convolution_multiply_fusion.1 = f32[1,1024]{1,0:T(1,128)S(1)} fusion(bf16[3072,1024]{1,0:T(8,128)(2,1)} %bitcast.27), kind=kOutput, calls=%fused_computation.13 | convolution fusion | flops 6292480 | bytes 6295552 | tf_op jit(solution)/shard_map/dot_general | solution.py:203
  108.6 1.3 convert_reduce_fusion
  110.0 2.8 %fusion.11 = f32[128,128]{1,0:T(8,128)} fusion(s32[4,2,16,24]{3,0,2,1:T(4,128)S(1)} %copy.14, f32[128]{0:T(128)S(1)} %dynamic-slice_bitcast_fusion, f32[128]{0:T(128)S(1)} %convert_reduce_fusion, bf16[4,2,16,24,1024]{4,3,2,1,0:T(8,128)(2,1)} %get-tuple-element.7, s32[]{:T(128)S(6)} %select_n.4), kind=kOutput, calls=%fused_computation.12 | convolution fusion | flops 101105664 | bytes 865284 | tf_op jit(solution)/shard_map/xhrotg,xhrtf->gf/dot_general | solution.py:233
  112.8 0.0 all-gather.2.cloned.1.call-done
  112.8 0.0 copy-start
  112.8 6.5 %convolution_multiply_fusion = f32[1,2048]{1,0:T(1,128)S(1)} fusion(bf16[3072,2048]{1,0:T(8,128)(2,1)} %all-gather.2.cloned.1.call-done), kind=kOutput, calls=%fused_computation.5 | convolution fusion | flops 12584960 | bytes 12591104 | tf_op jit(solution)/shard_map/dot_general | solution.py:203
  119.3 1.7 %copy-done = bf16[3072,2048]{1,0:T(8,128)(2,1)S(1)} copy-done((bf16[3072,2048]{1,0:T(8,128)(2,1)S(1)}, bf16[3072,2048]{1,0:T(8,128)(2,1)}, u32[]{:S(2)}) %copy-start) | copy-done | bytes 12582936
  121.0 17.6 %fusion.2 = f32[1024,2048]{1,0:T(8,128)} fusion(bf16[16,2,4,24,2048]{4,3,2,1,0:T(8,128)(2,1)S(1)} %bitcast.26, bf16[4,2,16,24,1024]{4,3,2,1,0:T(8,128)(2,1)} %get-tuple-element.7, f32[2048]{0:T(1024)S(1)} %bitcast.31, f32[1024]{0:T(1024)S(1)} %bitcast.32), kind=kOutput, calls=%fused_computation.3 | convolution fusion | flops 12891193344 | bytes 27275264 | tf_op jit(solution)/shard_map/xhrtf,rhxtg->fg/dot_general | solution.py:222
  (1 shorter events, 0.0 us)
Async XLA Ops:
  7.2 105.7 %all-gather.2.cloned.1.call-start = ((), (), s32[]{:S(2)}) async-start(), calls=%async_computation | async-start | bytes 13369344 | tf_op jit(solution)/shard_map/all_gather | solution.py:216
  112.8 8.2 %copy-start = (bf16[3072,2048]{1,0:T(8,128)(2,1)S(1)}, bf16[3072,2048]{1,0:T(8,128)(2,1)}, u32[]{:S(2)}) copy-start(bf16[3072,2048]{1,0:T(8,128)(2,1)} %all-gather.2.cloned.1.call-done) | copy-start | bytes 37748740
Sparse Core Ops, SparseCore 0:
  25.3 86.6 all-gather.1

commit v6 on v5

--- a/solution.py
+++ b/solution.py
@@ -13,8 +13,8 @@
 Z_HI = 2
 
 
-def _row_panel_kernel(n_row, n_x, x_ref, code_ref, p_ref, pc_ref,
-                      s1, r1, s1c, r1c, s2, r2, s2c, r2c, lsem):
+def _row_panel_kernel(n_row, n_x, x_ref, code_ref, cs_ref, p_ref, pc_ref, cs_out,
+                      s1, r1, s1c, r1c, s2, r2, s2c, r2c, s3, r3, lsem):
     r = lax.axis_index("row")
     c = lax.axis_index("col")
     zh = c // n_x
@@ -37,9 +37,12 @@
     own = pltpu.make_async_copy(
         x_ref.at[:, pl.ds(pl.multiple_of(r * width, width), width)], p_ref.at[x, zh, r], lsem.at[0])
     own_codes = pltpu.make_async_copy(code_ref, pc_ref.at[x, zh, r], lsem.at[1])
+    own_sum = pltpu.make_async_copy(cs_ref, cs_out.at[r], lsem.at[2])
     own.start()
     own_codes.start()
+    own_sum.start()
     stage1 = {0: [], 1: []}
+    sums = []
     for i, (dz, dr) in enumerate(sources):
         pr, pc = peer(dz, dr)
         cp = pltpu.make_async_remote_copy(
@@ -61,6 +64,17 @@
         cp.start()
         cc.start()
         stage1[min(dz, 1)] += [cp, cc]
+        if dz == 0:
+            cs = pltpu.make_async_remote_copy(
+                src_ref=cs_ref,
+                dst_ref=cs_out.at[r],
+                send_sem=s3.at[dr - 1],
+                recv_sem=r3.at[dr - 1],
+                device_id=(pr, pc),
+                device_id_type=MESH,
+            )
+            cs.start()
+            sums.append(cs)
 
     def send(src, dst, sems, idx, target):
         return pltpu.make_async_remote_copy(
@@ -113,9 +127,12 @@
     halves[1][2].wait_recv()
     for cp in fwd + fwd2:
         cp.wait()
-
-
-def _row_panel(activations, codes, n_row, n_col):
+    own_sum.wait()
+    for cp in sums:
+        cp.wait()
+
+
+def _row_panel(activations, codes, colsum, n_row, n_col):
     tokens = activations.shape[0]
     width = activations.shape[1] // n_row
     n_x = n_col // Z_HI
@@ -127,9 +144,10 @@
         out_shape=(
             jax.ShapeDtypeStruct((n_x, Z_HI, n_row, tokens, width), activations.dtype),
             jax.ShapeDtypeStruct((n_x, Z_HI, n_row, 1, tokens), jnp.int32),
+            jax.ShapeDtypeStruct((n_row,) + colsum.shape, colsum.dtype),
         ),
-        in_specs=[any_spec, any_spec],
-        out_specs=(any_spec, any_spec),
+        in_specs=[any_spec, any_spec, any_spec],
+        out_specs=(any_spec, any_spec, any_spec),
         scratch_shapes=[
             pltpu.SemaphoreType.DMA((group - 1,)),
             pltpu.SemaphoreType.DMA((group - 1,)),
@@ -139,10 +157,12 @@
             pltpu.SemaphoreType.DMA((6,)),
             pltpu.SemaphoreType.DMA((6,)),
             pltpu.SemaphoreType.DMA((6,)),
-            pltpu.SemaphoreType.DMA((2,)),
+            pltpu.SemaphoreType.DMA((n_row - 1,)),
+            pltpu.SemaphoreType.DMA((n_row - 1,)),
+            pltpu.SemaphoreType.DMA((3,)),
         ],
         compiler_params=pltpu.CompilerParams(collective_id=0, has_side_effects=True),
-    )(activations, codes)
+    )(activations, codes, colsum)
 
 
 def _col_piece_kernel(n_col, x_ref, code_ref, o_ref, code_out, send_sem, recv_sem, lsem):
@@ -214,14 +234,16 @@
     col_piece, codes = _col_piece(activations, codes.reshape(1, local_tokens), col_count)
     col_piece = col_piece.reshape(col_count * local_tokens, col_piece.shape[-1])
     col_panel = lax.all_gather(col_piece, "row", axis=0, tiled=True)
-    row_slots, code_slots = _row_panel(activations, codes, row_count, col_count)
+    colsum = jnp.dot(jnp.ones((8, col_piece.shape[0]), col_piece.dtype), col_piece,
+                     preferred_element_type=jnp.float32)[0:1]
+    row_slots, code_slots, col_sums = _row_panel(activations, codes, colsum, row_count, col_count)
     total = col_panel.shape[0]
     row_width = row_slots.shape[-1]
     row_panel = row_slots.reshape(total, row_width)
     col_view = col_panel.reshape(row_count, Z_HI, n_x, local_tokens, col_panel.shape[1])
     gram = jnp.einsum("xhrtf,rhxtg->fg", row_slots, col_view, preferred_element_type=jnp.float32)
     mean_row = _column_sum(row_panel) / total
-    mean_col = _column_sum(col_panel) / total
+    mean_col = jnp.sum(col_sums, axis=(0, 1)) / total
     covariance = gram / total - mean_row[:, None] * mean_col[None, :]
     slice_width = width // (row_count * col_count)
     slice_start = lax.axis_index("col") * slice_width

time: 146 us -> 145 us (level)
  Pallas kernels: 95.5 us -> 99.8 us
  matrix products: 30.7 us -> 27.5 us
  local copies, waits for them, and re-layouts: 2.59 us -> 0.95 us
    dot_general x2 -> x1, matrix products: 10.2 us -> 3.77 us  [_column_sum(): return jnp.dot(ones, panel, preferred_element_type=jnp.float32)[0]]
    pallas_call x1, Pallas kernels: 78.8 us -> 83 us  [_row_panel(): pl.pallas_call(functools.partial(_row_panel_kernel, n_row, n_x), out_shap...]
    dot_general x0 -> x1, matrix products: none -> 1.95 us  [shards(): jnp.dot(jnp.ones((8, col_piece.shape[0]), col_piece.dtype), col_piece, pr...]
    unnamed x2, local copies, waits for them, and re-layouts: 1.7 us -> 0.01 us
  transfers between devices with their start and end apart: 1 -> 1, of which waited for: 0 -> 0; matrix products, arithmetic and copies ran while one was open for 6% -> 8% of each run, Pallas kernels for 54% -> 57%
where the time goes in v6:
time: 145 us
  Pallas kernels  99.8 us (69%)
  matrix products  27.5 us (19%)
  between operations  14.1 us (10%)
  other arithmetic  2.76 us (2%)
    pallas_call x1, Pallas kernels, _row_panel(): pl.pallas_call(functools.partial(_row_panel_kernel, n_row, n_x), out_shap...  83 us
    dot_general x1, matrix products, shards(): jnp.einsum('xhrtf,rhxtg->fg', row_slots, col_view, preferred_element_type...  18.9 us
    pallas_call x1, Pallas kernels, _col_piece(): pl.pallas_call(functools.partial(_col_piece_kernel, n_col), out_shape=(ja...  16.8 us
    dot_general x1, matrix products, _column_sum(): return jnp.dot(ones, panel, preferred_element_type=jnp.float32)[0]  3.77 us
  transfers between devices with their start and end apart: 1, of which 0 were waited for; matrix products, arithmetic and copies ran while one was open for 8% of the time, Pallas kernels for 57%

profile of v6, /device:TPU:1, one launch (start us, length us, event | category | flops | bytes accessed | tf_op | source)
XLA Modules:
  0.0 145.1 jit_solution(2375806286164712501)
XLA Ops:
  7.2 0.0 all-gather.2.cloned.1.call-start
  7.2 1.2 add_bitcast_fusion.code_ref
  8.4 16.8 %shard_map.50 = (bf16[8,24,2048]{2,1,0:T(8,128)(2,1)}, s32[1,24]{1,0:T(1,128)}) custom-call(bf16[24,16384]{1,0:T(8,128)(2,1)} %x_ref.3, s32[1,24]{1,0:T(1,128)} %add_bitcast_fusion.code_ref), custom_call_target="tpu_custom_call" | custom-call | tf_op jit(solution)/shard_map/pallas_call | solution.py:204
  25.2 0.0 all-gather.2.cloned.1.call-update
  25.2 1.9 %fusion.15.cs_ref = f32[1,2048]{1,0:T(1,128)} fusion(bf16[192,2048]{1,0:T(8,128)(2,1)} %bitcast.27), kind=kOutput, calls=%fused_computation.17 | convolution fusion | flops 786432 | bytes 794624 | tf_op jit(solution)/shard_map/dot_general | solution.py:237
  27.2 83.0 %shard_map.51 = (bf16[4,2,16,24,1024]{4,3,2,1,0:T(8,128)(2,1)}, s32[4,2,16,1,24]{4,3,2,1,0:T(1,128)}, f32[16,1,2048]{2,1,0:T(1,128)}) custom-call(bf16[24,16384]{1,0:T(8,128)(2,1)} %x_ref.3, s32[1,24]{1,0:T(1,128)} %get-tuple-element.7.code_ref, f32[1,2048]{1,0:T(1,128)} %fusion.15.cs_ref), custom_call_target="tpu_custom_call" | custom-call | tf_op jit(solution)/shard_map/pallas_call | solution.py:142
  110.2 0.0 copy-start
  110.2 0.9 copy.14
  111.1 1.0 reduce_sum.16
  112.1 3.8 %convolution_multiply_fusion = f32[1,1024]{1,0:T(1,128)S(1)} fusion(bf16[3072,1024]{1,0:T(8,128)(2,1)} %bitcast.25), kind=kOutput, calls=%fused_computation.12 | convolution fusion | flops 6292480 | bytes 6295552 | tf_op jit(solution)/shard_map/dot_general | solution.py:223
  115.9 0.0 copy-done
  115.9 0.6 convert_reduce_fusion
  116.5 2.8 %fusion.11 = f32[128,128]{1,0:T(8,128)} fusion(s32[4,2,16,24]{3,0,2,1:T(4,128)S(1)} %copy.14, f32[128]{0:T(128)S(1)} %dynamic-slice_bitcast_fusion, f32[128]{0:T(128)S(1)} %convert_reduce_fusion, bf16[4,2,16,24,1024]{4,3,2,1,0:T(8,128)(2,1)} %get-tuple-element.9, s32[]{:T(128)S(6)} %select_n.4), kind=kOutput, calls=%fused_computation.11 | convolution fusion | flops 101105664 | bytes 865284 | tf_op jit(solution)/shard_map/xhrotg,xhrtf->gf/dot_general | solution.py:255
  119.3 0.0 all-gather.2.cloned.1.call-done
  119.3 18.9 %fusion.2 = f32[1024,2048]{1,0:T(8,128)} fusion(bf16[16,2,4,24,2048]{4,3,2,1,0:T(8,128)(2,1)} %bitcast.31, bf16[4,2,16,24,1024]{4,3,2,1,0:T(8,128)(2,1)} %get-tuple-element.9, f32[2048]{0:T(1024)S(1)} %broadcast_multiply_fusion, f32[1024]{0:T(1024)S(1)} %bitcast.30), kind=kOutput, calls=%fused_computation.3 | convolution fusion | flops 12891193344 | bytes 27275264 | tf_op jit(solution)/shard_map/xhrtf,rhxtg->fg/dot_general | solution.py:244
  (2 shorter events, 0.0 us)
Async XLA Ops:
  7.2 112.2 %all-gather.2.cloned.1.call-start = ((), (), s32[]{:S(2)}) async-start(), calls=%async_computation | async-start | bytes 13369344 | tf_op jit(solution)/shard_map/all_gather | solution.py:236
  110.2 5.7 %copy-start = (s32[4,2,16,1,24]{4,3,2,1,0:T(1,128)S(1)}, s32[4,2,16,1,24]{4,3,2,1,0:T(1,128)}, u32[]{:S(2)}) copy-start(s32[4,2,16,1,24]{4,3,2,1,0:T(1,128)} %get-tuple-element.11) | copy-start | bytes 36868
Sparse Core Ops, SparseCore 0:
  25.3 89.6 all-gather.1

commit v7 on v5

--- a/solution.py
+++ b/solution.py
@@ -13,46 +13,65 @@
 Z_HI = 2
 
 
-def _row_panel_kernel(n_row, n_x, x_ref, code_ref, p_ref, pc_ref,
-                      s1, r1, s1c, r1c, s2, r2, s2c, r2c, lsem):
+def _row_panel_kernel(n_row, n_x, x_ref, code_ref, p_ref, pc_ref, pair, cpair,
+                      s0, r0, s1, r1, s1c, r1c, s2, r2, s2c, r2c, lsem):
     r = lax.axis_index("row")
     c = lax.axis_index("col")
     zh = c // n_x
     x = lax.rem(c, n_x)
+    core = lax.rem(r, 2)
+    j = r // 2
+    n_j = n_row // 2
+    partner = r + 1 - 2 * core
     width = p_ref.shape[-1]
     left = zh * n_x + lax.rem(x + n_x - 1, n_x)
     right = zh * n_x + lax.rem(x + 1, n_x)
-    sources = [(dz, dr) for dz in range(Z_HI) for dr in range(n_row) if dz or dr]
-
-    def peer(dz, dr):
-        return lax.rem(r + dr, n_row), lax.rem(zh + dz, Z_HI) * n_x + x
+    sources = [(dz, dj) for dz in range(Z_HI) for dj in range(n_j) if dz or dj]
+
+    def peer(dz, dj):
+        return 2 * lax.rem(j + dj, n_j) + core, lax.rem(zh + dz, Z_HI) * n_x + x
 
     barrier = pltpu.get_barrier_semaphore()
-    for dz, dr in sources:
-        pl.semaphore_signal(barrier, 1, device_id=peer(dz, dr), device_id_type=MESH)
+    for dz, dj in sources:
+        pl.semaphore_signal(barrier, 1, device_id=peer(dz, dj), device_id_type=MESH)
+    pl.semaphore_signal(barrier, 1, device_id=(partner, c), device_id_type=MESH)
     pl.semaphore_signal(barrier, 1, device_id=(r, left), device_id_type=MESH)
     pl.semaphore_signal(barrier, 1, device_id=(r, right), device_id_type=MESH)
-    pl.semaphore_wait(barrier, len(sources) + 2)
-
+    pl.semaphore_wait(barrier, len(sources) + 3)
+
+    mine = pltpu.make_async_copy(x_ref, pair.at[core], lsem.at[0])
+    mine_codes = pltpu.make_async_copy(code_ref, cpair.at[core], lsem.at[1])
+    swap = pltpu.make_async_remote_copy(
+        src_ref=x_ref, dst_ref=pair.at[core], send_sem=s0.at[0], recv_sem=r0.at[0],
+        device_id=(partner, c), device_id_type=MESH)
+    swap_codes = pltpu.make_async_remote_copy(
+        src_ref=code_ref, dst_ref=cpair.at[core], send_sem=s0.at[1], recv_sem=r0.at[1],
+        device_id=(partner, c), device_id_type=MESH)
+    for cp in (swap, swap_codes, mine, mine_codes):
+        cp.start()
+    for cp in (swap, swap_codes, mine, mine_codes):
+        cp.wait()
+
+    block = pl.ds(pl.multiple_of(2 * j, 2), 2)
     own = pltpu.make_async_copy(
-        x_ref.at[:, pl.ds(pl.multiple_of(r * width, width), width)], p_ref.at[x, zh, r], lsem.at[0])
-    own_codes = pltpu.make_async_copy(code_ref, pc_ref.at[x, zh, r], lsem.at[1])
+        pair.at[:, :, pl.ds(pl.multiple_of(r * width, width), width)], p_ref.at[x, zh, block], lsem.at[2])
+    own_codes = pltpu.make_async_copy(cpair, pc_ref.at[x, zh, block], lsem.at[3])
     own.start()
     own_codes.start()
     stage1 = {0: [], 1: []}
-    for i, (dz, dr) in enumerate(sources):
-        pr, pc = peer(dz, dr)
+    for i, (dz, dj) in enumerate(sources):
+        pr, pc = peer(dz, dj)
         cp = pltpu.make_async_remote_copy(
-            src_ref=x_ref.at[:, pl.ds(pl.multiple_of(pr * width, width), width)],
-            dst_ref=p_ref.at[x, zh, r],
+            src_ref=pair.at[:, :, pl.ds(pl.multiple_of(pr * width, width), width)],
+            dst_ref=p_ref.at[x, zh, block],
             send_sem=s1.at[i],
             recv_sem=r1.at[i],
             device_id=(pr, pc),
             device_id_type=MESH,
         )
         cc = pltpu.make_async_remote_copy(
-            src_ref=code_ref,
-            dst_ref=pc_ref.at[x, zh, r],
+            src_ref=cpair,
+            dst_ref=pc_ref.at[x, zh, block],
             send_sem=s1c.at[i],
             recv_sem=r1c.at[i],
             device_id=(pr, pc),
@@ -127,19 +146,23 @@
         out_shape=(
             jax.ShapeDtypeStruct((n_x, Z_HI, n_row, tokens, width), activations.dtype),
             jax.ShapeDtypeStruct((n_x, Z_HI, n_row, 1, tokens), jnp.int32),
+            jax.ShapeDtypeStruct((2,) + activations.shape, activations.dtype),
+            jax.ShapeDtypeStruct((2,) + codes.shape, codes.dtype),
         ),
         in_specs=[any_spec, any_spec],
-        out_specs=(any_spec, any_spec),
+        out_specs=(any_spec, any_spec, any_spec, any_spec),
         scratch_shapes=[
-            pltpu.SemaphoreType.DMA((group - 1,)),
-            pltpu.SemaphoreType.DMA((group - 1,)),
-            pltpu.SemaphoreType.DMA((group - 1,)),
-            pltpu.SemaphoreType.DMA((group - 1,)),
-            pltpu.SemaphoreType.DMA((6,)),
-            pltpu.SemaphoreType.DMA((6,)),
-            pltpu.SemaphoreType.DMA((6,)),
-            pltpu.SemaphoreType.DMA((6,)),
             pltpu.SemaphoreType.DMA((2,)),
+            pltpu.SemaphoreType.DMA((2,)),
+            pltpu.SemaphoreType.DMA((group // 2 - 1,)),
+            pltpu.SemaphoreType.DMA((group // 2 - 1,)),
+            pltpu.SemaphoreType.DMA((group // 2 - 1,)),
+            pltpu.SemaphoreType.DMA((group // 2 - 1,)),
+            pltpu.SemaphoreType.DMA((6,)),
+            pltpu.SemaphoreType.DMA((6,)),
+            pltpu.SemaphoreType.DMA((6,)),
+            pltpu.SemaphoreType.DMA((6,)),
+            pltpu.SemaphoreType.DMA((4,)),
         ],
         compiler_params=pltpu.CompilerParams(collective_id=0, has_side_effects=True),
     )(activations, codes)
@@ -214,7 +237,7 @@
     col_piece, codes = _col_piece(activations, codes.reshape(1, local_tokens), col_count)
     col_piece = col_piece.reshape(col_count * local_tokens, col_piece.shape[-1])
     col_panel = lax.all_gather(col_piece, "row", axis=0, tiled=True)
-    row_slots, code_slots = _row_panel(activations, codes, row_count, col_count)
+    row_slots, code_slots, _, _ = _row_panel(activations, codes, row_count, col_count)
     total = col_panel.shape[0]
     row_width = row_slots.shape[-1]
     row_panel = row_slots.reshape(total, row_width)

time: 146 us -> 179 us (1.23)
  Pallas kernels: 95.5 us -> 130 us
    pallas_call x1, Pallas kernels: 78.8 us -> 113 us  [_row_panel(): pl.pallas_call(functools.partial(_row_panel_kernel, n_row, n_x), out_shap...]
  transfers between devices with their start and end apart: 1 -> 1, of which waited for: 0 -> 0; matrix products, arithmetic and copies ran while one was open for 6% -> 5% of each run, Pallas kernels for 54% -> 63%
where the time goes in v7:
time: 179 us
  Pallas kernels  130 us (73%)
  matrix products  30.6 us (17%)
  between operations  14.1 us (8%)
  local copies, waits for them, and re-layouts  2.65 us (1%)
    pallas_call x1, Pallas kernels, _row_panel(): pl.pallas_call(functools.partial(_row_panel_kernel, n_row, n_x), out_shap...  113 us
    dot_general x1, matrix products, shards(): jnp.einsum('xhrtf,rhxtg->fg', row_slots, col_view, preferred_element_type...  17.6 us
    pallas_call x1, Pallas kernels, _col_piece(): pl.pallas_call(functools.partial(_col_piece_kernel, n_col), out_shape=(ja...  16.8 us
    dot_general x2, matrix products, _column_sum(): return jnp.dot(ones, panel, preferred_element_type=jnp.float32)[0]  10.2 us
  transfers between devices with their start and end apart: 1, of which 0 were waited for; matrix products, arithmetic and copies ran while one was open for 5% of the time, Pallas kernels for 63%

profile of v7, /device:TPU:1, one launch (start us, length us, event | category | flops | bytes accessed | tf_op | source)
XLA Modules:
  0.0 179.0 jit_solution(4694884729669099530)
XLA Ops:
  7.2 0.0 all-gather.2.cloned.1.call-start
  7.2 1.2 add_bitcast_fusion.code_ref
  8.4 16.8 %shard_map.50 = (bf16[8,24,2048]{2,1,0:T(8,128)(2,1)}, s32[1,24]{1,0:T(1,128)}) custom-call(bf16[24,16384]{1,0:T(8,128)(2,1)} %x_ref.3, s32[1,24]{1,0:T(1,128)} %add_bitcast_fusion.code_ref), custom_call_target="tpu_custom_call" | custom-call | tf_op jit(solution)/shard_map/pallas_call | solution.py:207
  25.2 0.0 all-gather.2.cloned.1.call-update
  25.2 113.0 %shard_map.51 = (bf16[4,2,16,24,1024]{4,3,2,1,0:T(8,128)(2,1)}, s32[4,2,16,1,24]{4,3,2,1,0:T(1,128)}, bf16[2,24,16384]{2,1,0:T(8,128)(2,1)}, s32[2,1,24]{2,1,0:T(1,128)}) custom-call(bf16[24,16384]{1,0:T(8,128)(2,1)} %x_ref.3, s32[1,24]{1,0:T(1,128)} %get-tuple-element.6.code_ref), custom_call_target="tpu_custom_call" | custom-call | tf_op jit(solution)/shard_map/pallas_call | solution.py:144
  138.3 0.0 copy-start.1
  138.3 0.9 copy.14
  139.2 3.7 %convolution_multiply_fusion.1 = f32[1,1024]{1,0:T(1,128)S(1)} fusion(bf16[3072,1024]{1,0:T(8,128)(2,1)} %bitcast.27), kind=kOutput, calls=%fused_computation.13 | convolution fusion | flops 6292480 | bytes 6295552 | tf_op jit(solution)/shard_map/dot_general | solution.py:226
  142.9 0.0 copy-done.1
  142.9 0.6 convert_reduce_fusion
  143.5 2.8 %fusion.11 = f32[128,128]{1,0:T(8,128)} fusion(s32[4,2,16,24]{3,0,2,1:T(4,128)S(1)} %copy.14, f32[128]{0:T(128)S(1)} %dynamic-slice_bitcast_fusion, f32[128]{0:T(128)S(1)} %convert_reduce_fusion, bf16[4,2,16,24,1024]{4,3,2,1,0:T(8,128)(2,1)} %get-tuple-element.7, s32[]{:T(128)S(6)} %select_n.4), kind=kOutput, calls=%fused_computation.12 | convolution fusion | flops 101105664 | bytes 865284 | tf_op jit(solution)/shard_map/xhrotg,xhrtf->gf/dot_general | solution.py:256
  146.4 0.0 all-gather.2.cloned.1.call-done
  146.4 0.0 copy-start
  146.4 6.5 %convolution_multiply_fusion = f32[1,2048]{1,0:T(1,128)S(1)} fusion(bf16[3072,2048]{1,0:T(8,128)(2,1)} %all-gather.2.cloned.1.call-done), kind=kOutput, calls=%fused_computation.5 | convolution fusion | flops 12584960 | bytes 12591104 | tf_op jit(solution)/shard_map/dot_general | solution.py:226
  152.8 1.7 copy-done
  154.5 17.6 %fusion.2 = f32[1024,2048]{1,0:T(8,128)} fusion(bf16[16,2,4,24,2048]{4,3,2,1,0:T(8,128)(2,1)S(1)} %bitcast.26, bf16[4,2,16,24,1024]{4,3,2,1,0:T(8,128)(2,1)} %get-tuple-element.7, f32[2048]{0:T(1024)S(1)} %bitcast.31, f32[1024]{0:T(1024)S(1)} %bitcast.32), kind=kOutput, calls=%fused_computation.3 | convolution fusion | flops 12891193344 | bytes 27275264 | tf_op jit(solution)/shard_map/xhrtf,rhxtg->fg/dot_general | solution.py:245
  (1 shorter events, 0.0 us)
Async XLA Ops:
  7.2 139.2 %all-gather.2.cloned.1.call-start = ((), (), s32[]{:S(2)}) async-start(), calls=%async_computation | async-start | bytes 13369344 | tf_op jit(solution)/shard_map/all_gather | solution.py:239
  138.3 4.7 %copy-start.1 = (s32[4,2,16,1,24]{4,3,2,1,0:T(1,128)S(1)}, s32[4,2,16,1,24]{4,3,2,1,0:T(1,128)}, u32[]{:S(2)}) copy-start(s32[4,2,16,1,24]{4,3,2,1,0:T(1,128)} %get-tuple-element.9) | copy-start | bytes 36868
  146.4 8.2 %copy-start = (bf16[3072,2048]{1,0:T(8,128)(2,1)S(1)}, bf16[3072,2048]{1,0:T(8,128)(2,1)}, u32[]{:S(2)}) copy-start(bf16[3072,2048]{1,0:T(8,128)(2,1)} %all-gather.2.cloned.1.call-done) | copy-start | bytes 37748740
Sparse Core Ops, SparseCore 0:
  25.3 91.0 all-gather.1

commit v8 on v6

--- a/solution.py
+++ b/solution.py
@@ -234,8 +234,7 @@
     col_piece, codes = _col_piece(activations, codes.reshape(1, local_tokens), col_count)
     col_piece = col_piece.reshape(col_count * local_tokens, col_piece.shape[-1])
     col_panel = lax.all_gather(col_piece, "row", axis=0, tiled=True)
-    colsum = jnp.dot(jnp.ones((8, col_piece.shape[0]), col_piece.dtype), col_piece,
-                     preferred_element_type=jnp.float32)[0:1]
+    colsum = jnp.sum(col_piece, axis=0, dtype=jnp.float32, keepdims=True)
     row_slots, code_slots, col_sums = _row_panel(activations, codes, colsum, row_count, col_count)
     total = col_panel.shape[0]
     row_width = row_slots.shape[-1]

time: 145 us -> 145 us (level)
  matrix products: 27.5 us -> 25.5 us
  other arithmetic: 2.76 us -> 4.62 us
    dot_general x1 -> x0, matrix products: 1.95 us -> none  [shards(): jnp.dot(jnp.ones((8, col_piece.shape[0]), col_piece.dtype), col_piece, pr...]
    reduce_sum x0 -> x1, other arithmetic: none -> 1.86 us  [shards(): colsum = jnp.sum(col_piece, axis=0, dtype=jnp.float32, keepdims=True)]
where the time goes in v8:
time: 145 us
  Pallas kernels  99.5 us (69%)
  matrix products  25.5 us (18%)
  between operations  14.1 us (10%)
  other arithmetic  4.62 us (3%)
    pallas_call x1, Pallas kernels, _row_panel(): pl.pallas_call(functools.partial(_row_panel_kernel, n_row, n_x), out_shap...  82.7 us
    dot_general x1, matrix products, shards(): jnp.einsum('xhrtf,rhxtg->fg', row_slots, col_view, preferred_element_type...  18.9 us
    pallas_call x1, Pallas kernels, _col_piece(): pl.pallas_call(functools.partial(_col_piece_kernel, n_col), out_shape=(ja...  16.8 us
    dot_general x1, matrix products, _column_sum(): return jnp.dot(ones, panel, preferred_element_type=jnp.float32)[0]  3.77 us
  transfers between devices with their start and end apart: 1, of which 0 were waited for; matrix products, arithmetic and copies ran while one was open for 8% of the time, Pallas kernels for 57%

profile of v8, /device:TPU:1, one launch (start us, length us, event | category | flops | bytes accessed | tf_op | source)
XLA Modules:
  0.0 144.7 jit_solution(2088910661177800892)
XLA Ops:
  7.2 0.0 all-gather.2.cloned.1.call-start
  7.2 1.2 add_bitcast_fusion.code_ref
  8.4 16.8 %shard_map.50 = (bf16[8,24,2048]{2,1,0:T(8,128)(2,1)}, s32[1,24]{1,0:T(1,128)}) custom-call(bf16[24,16384]{1,0:T(8,128)(2,1)} %x_ref.3, s32[1,24]{1,0:T(1,128)} %add_bitcast_fusion.code_ref), custom_call_target="tpu_custom_call" | custom-call | tf_op jit(solution)/shard_map/pallas_call | solution.py:204
  25.2 0.0 all-gather.2.cloned.1.call-update
  25.2 1.9 %convert_reduce_fusion.1 = f32[2048]{0:T(1024)} fusion(bf16[8,24,2048]{2,1,0:T(8,128)(2,1)} %get-tuple-element.8), kind=kLoop, calls=%fused_computation.8 | loop fusion | flops 784384 | bytes 794624 | tf_op jit(solution)/shard_map/reduce_sum | solution.py:237
  27.1 82.7 %shard_map.51 = (bf16[4,2,16,24,1024]{4,3,2,1,0:T(8,128)(2,1)}, s32[4,2,16,1,24]{4,3,2,1,0:T(1,128)}, f32[16,1,2048]{2,1,0:T(1,128)}) custom-call(bf16[24,16384]{1,0:T(8,128)(2,1)} %x_ref.3, s32[1,24]{1,0:T(1,128)} %get-tuple-element.7.code_ref, f32[1,2048]{1,0:T(1,128)} %bitcast.29), custom_call_target="tpu_custom_call" | custom-call | tf_op jit(solution)/shard_map/pallas_call | solution.py:142
  109.8 0.0 copy-start
  109.8 0.9 copy.14
  110.8 1.0 reduce_sum.32
  111.8 3.8 %convolution_multiply_fusion = f32[1,1024]{1,0:T(1,128)S(1)} fusion(bf16[3072,1024]{1,0:T(8,128)(2,1)} %bitcast.25), kind=kOutput, calls=%fused_computation.13 | convolution fusion | flops 6292480 | bytes 6295552 | tf_op jit(solution)/shard_map/dot_general | solution.py:223
  115.5 0.0 copy-done
  115.5 0.6 convert_reduce_fusion
  116.1 2.8 %fusion.11 = f32[128,128]{1,0:T(8,128)} fusion(s32[4,2,16,24]{3,0,2,1:T(4,128)S(1)} %copy.14, f32[128]{0:T(128)S(1)} %dynamic-slice_bitcast_fusion, f32[128]{0:T(128)S(1)} %convert_reduce_fusion, bf16[4,2,16,24,1024]{4,3,2,1,0:T(8,128)(2,1)} %get-tuple-element.9, s32[]{:T(128)S(6)} %select_n.4), kind=kOutput, calls=%fused_computation.12 | convolution fusion | flops 101105664 | bytes 865284 | tf_op jit(solution)/shard_map/xhrotg,xhrtf->gf/dot_general | solution.py:254
  119.0 0.0 all-gather.2.cloned.1.call-done
  119.0 18.9 %fusion.2 = f32[1024,2048]{1,0:T(8,128)} fusion(bf16[16,2,4,24,2048]{4,3,2,1,0:T(8,128)(2,1)} %bitcast.31, bf16[4,2,16,24,1024]{4,3,2,1,0:T(8,128)(2,1)} %get-tuple-element.9, f32[2048]{0:T(1024)S(1)} %broadcast_multiply_fusion, f32[1024]{0:T(1024)S(1)} %bitcast.30), kind=kOutput, calls=%fused_computation.3 | convolution fusion | flops 12891193344 | bytes 27275264 | tf_op jit(solution)/shard_map/xhrtf,rhxtg->fg/dot_general | solution.py:243
  (2 shorter events, 0.0 us)
Async XLA Ops:
  7.2 111.8 %all-gather.2.cloned.1.call-start = ((), (), s32[]{:S(2)}) async-start(), calls=%async_computation | async-start | bytes 13369344 | tf_op jit(solution)/shard_map/all_gather | solution.py:236
  109.8 5.7 %copy-start = (s32[4,2,16,1,24]{4,3,2,1,0:T(1,128)S(1)}, s32[4,2,16,1,24]{4,3,2,1,0:T(1,128)}, u32[]{:S(2)}) copy-start(s32[4,2,16,1,24]{4,3,2,1,0:T(1,128)} %get-tuple-element.11) | copy-start | bytes 36868
Sparse Core Ops, SparseCore 0:
  25.3 89.5 all-gather.1

commit v9 on v8

--- a/solution.py
+++ b/solution.py
@@ -13,8 +13,8 @@
 Z_HI = 2
 
 
-def _row_panel_kernel(n_row, n_x, x_ref, code_ref, cs_ref, p_ref, pc_ref, cs_out,
-                      s1, r1, s1c, r1c, s2, r2, s2c, r2c, s3, r3, lsem):
+def _row_panel_kernel(n_row, n_x, x_ref, code_ref, cs_ref, p_ref, pc_ref, cs_out, rs_out,
+                      s1, r1, s1c, r1c, s2, r2, s2c, r2c, s3, r3, lsem, vbuf, vsem):
     r = lax.axis_index("row")
     c = lax.axis_index("col")
     zh = c // n_x
@@ -116,17 +116,34 @@
     for cp in fwd2:
         cp.start()
 
+    rs_out[...] = jnp.zeros_like(rs_out)
+
+    def add_part(slot, xp):
+        load = pltpu.make_async_copy(p_ref.at[xp], vbuf.at[slot], vsem.at[slot])
+        load.start()
+        load.wait()
+
+        def body(i, carry):
+            block = vbuf[slot, i // n_row, lax.rem(i, n_row)].astype(jnp.float32)
+            return carry + jnp.sum(block, axis=0, keepdims=True)
+
+        rs_out[...] += lax.fori_loop(0, Z_HI * n_row, body, jnp.zeros(rs_out.shape, jnp.float32))
+
+    add_part(0, x)
+    halves[0][1].wait_recv()
+    halves[0][3].wait_recv()
+    halves[1][0].wait_recv()
+    halves[1][2].wait_recv()
+    add_part(1, from_left)
+    add_part(2, from_right)
     for cp in stage1[0] + stage1[1]:
         cp.wait_send()
     for pair in halves:
         for cp in pair:
             cp.wait_send()
-    halves[0][1].wait_recv()
-    halves[0][3].wait_recv()
-    halves[1][0].wait_recv()
-    halves[1][2].wait_recv()
     for cp in fwd + fwd2:
         cp.wait()
+    add_part(3, lax.rem(x + 2, n_x))
     own_sum.wait()
     for cp in sums:
         cp.wait()
@@ -145,9 +162,10 @@
             jax.ShapeDtypeStruct((n_x, Z_HI, n_row, tokens, width), activations.dtype),
             jax.ShapeDtypeStruct((n_x, Z_HI, n_row, 1, tokens), jnp.int32),
             jax.ShapeDtypeStruct((n_row,) + colsum.shape, colsum.dtype),
+            jax.ShapeDtypeStruct((1, width), jnp.float32),
         ),
         in_specs=[any_spec, any_spec, any_spec],
-        out_specs=(any_spec, any_spec, any_spec),
+        out_specs=(any_spec, any_spec, any_spec, pl.BlockSpec(memory_space=pltpu.VMEM)),
         scratch_shapes=[
             pltpu.SemaphoreType.DMA((group - 1,)),
             pltpu.SemaphoreType.DMA((group - 1,)),
@@ -160,6 +178,8 @@
             pltpu.SemaphoreType.DMA((n_row - 1,)),
             pltpu.SemaphoreType.DMA((n_row - 1,)),
             pltpu.SemaphoreType.DMA((3,)),
+            pltpu.VMEM((4, Z_HI, n_row, tokens, width), activations.dtype),
+            pltpu.SemaphoreType.DMA((4,)),
         ],
         compiler_params=pltpu.CompilerParams(collective_id=0, has_side_effects=True),
     )(activations, codes, colsum)
@@ -235,13 +255,13 @@
     col_piece = col_piece.reshape(col_count * local_tokens, col_piece.shape[-1])
     col_panel = lax.all_gather(col_piece, "row", axis=0, tiled=True)
     colsum = jnp.sum(col_piece, axis=0, dtype=jnp.float32, keepdims=True)
-    row_slots, code_slots, col_sums = _row_panel(activations, codes, colsum, row_count, col_count)
+    row_slots, code_slots, col_sums, row_sums = _row_panel(activations, codes, colsum, row_count, col_count)
     total = col_panel.shape[0]
     row_width = row_slots.shape[-1]
     row_panel = row_slots.reshape(total, row_width)
     col_view = col_panel.reshape(row_count, Z_HI, n_x, local_tokens, col_panel.shape[1])
     gram = jnp.einsum("xhrtf,rhxtg->fg", row_slots, col_view, preferred_element_type=jnp.float32)
-    mean_row = _column_sum(row_panel) / total
+    mean_row = row_sums[0] / total
     mean_col = jnp.sum(col_sums, axis=(0, 1)) / total
     covariance = gram / total - mean_row[:, None] * mean_col[None, :]
     slice_width = width // (row_count * col_count)

time: 145 us -> 146 us (level)
  matrix products: 25.5 us -> 21.7 us
  Pallas kernels: 99.5 us -> 102 us
  other arithmetic: 4.62 us -> 6.08 us
    dot_general x1 -> x0, matrix products: 3.77 us -> none  [_column_sum(): return jnp.dot(ones, panel, preferred_element_type=jnp.float32)[0]]
    pallas_call x1, Pallas kernels: 82.7 us -> 85.5 us  [_row_panel(): pl.pallas_call(functools.partial(_row_panel_kernel, n_row, n_x), out_shap...]
  transfers between devices with their start and end apart: 1 -> 1, of which waited for: 0 -> 0; matrix products, arithmetic and copies ran while one was open for 8% -> 6% of each run, Pallas kernels for 57% -> 59%
where the time goes in v9:
time: 146 us; the launch traced here: 145 us
  Pallas kernels  102 us (70%)
  matrix products  21.7 us (15%)
  between operations  14.1 us (10%)
  other arithmetic  6.08 us (4%)
    pallas_call x1, Pallas kernels, _row_panel(): pl.pallas_call(functools.partial(_row_panel_kernel, n_row, n_x), out_shap...  85.5 us
    dot_general x1, matrix products, shards(): jnp.einsum('xhrtf,rhxtg->fg', row_slots, col_view, preferred_element_type...  18.9 us
    pallas_call x1, Pallas kernels, _col_piece(): pl.pallas_call(functools.partial(_col_piece_kernel, n_col), out_shape=(ja...  16.8 us
  transfers between devices with their start and end apart: 1, of which 0 were waited for; matrix products, arithmetic and copies ran while one was open for 6% of the time, Pallas kernels for 59%

profile of v9, /device:TPU:1, one launch (start us, length us, event | category | flops | bytes accessed | tf_op | source)
XLA Modules:
  0.0 145.1 jit_solution(14382109175114040195)
XLA Ops:
  7.2 0.0 all-gather.2.cloned.1.call-start
  7.2 1.2 add_bitcast_fusion.code_ref
  8.4 16.8 %shard_map.50 = (bf16[8,24,2048]{2,1,0:T(8,128)(2,1)}, s32[1,24]{1,0:T(1,128)}) custom-call(bf16[24,16384]{1,0:T(8,128)(2,1)} %x_ref.3, s32[1,24]{1,0:T(1,128)} %add_bitcast_fusion.code_ref), custom_call_target="tpu_custom_call" | custom-call | tf_op jit(solution)/shard_map/pallas_call | solution.py:224
  25.2 0.0 all-gather.2.cloned.1.call-update
  25.2 1.9 %convert_reduce_fusion.1 = f32[2048]{0:T(1024)} fusion(bf16[8,24,2048]{2,1,0:T(8,128)(2,1)} %get-tuple-element.9), kind=kLoop, calls=%fused_computation.8 | loop fusion | flops 784384 | bytes 794624 | tf_op jit(solution)/shard_map/reduce_sum | solution.py:257
  27.1 85.5 %shard_map.51 = (bf16[4,2,16,24,1024]{4,3,2,1,0:T(8,128)(2,1)}, s32[4,2,16,1,24]{4,3,2,1,0:T(1,128)}, f32[16,1,2048]{2,1,0:T(1,128)}, f32[1,1024]{1,0:T(1,128)}) custom-call(bf16[24,16384]{1,0:T(8,128)(2,1)} %x_ref.3, s32[1,24]{1,0:T(1,128)} %get-tuple-element.8.code_ref, f32[1,2048]{1,0:T(1,128)} %bitcast.26), custom_call_target="tpu_custom_call" | custom-call | tf_op jit(solution)/shard_map/pallas_call | solution.py:159
  112.6 0.9 copy.14
  113.5 1.0 reduce_sum.32
  114.5 0.7 broadcast_multiply_fusion.1
  115.2 1.3 convert_reduce_fusion
  116.5 2.8 %fusion.11 = f32[128,128]{1,0:T(8,128)} fusion(s32[4,2,16,24]{3,0,2,1:T(4,128)S(1)} %copy.14, f32[128]{0:T(128)S(1)} %dynamic-slice_bitcast_fusion, f32[128]{0:T(128)S(1)} %convert_reduce_fusion, bf16[4,2,16,24,1024]{4,3,2,1,0:T(8,128)(2,1)} %get-tuple-element.10, s32[]{:T(128)S(6)} %select_n.4), kind=kOutput, calls=%fused_computation.12 | convolution fusion | flops 101105664 | bytes 865284 | tf_op jit(solution)/shard_map/xhrotg,xhrtf->gf/dot_general | solution.py:274
  119.4 0.0 all-gather.2.cloned.1.call-done
  119.4 18.9 %fusion.2 = f32[1024,2048]{1,0:T(8,128)} fusion(bf16[16,2,4,24,2048]{4,3,2,1,0:T(8,128)(2,1)} %bitcast.28, bf16[4,2,16,24,1024]{4,3,2,1,0:T(8,128)(2,1)} %get-tuple-element.10, f32[2048]{0:T(1024)S(1)} %broadcast_multiply_fusion, f32[1024]{0:T(1024)S(1)} %bitcast.27), kind=kOutput, calls=%fused_computation.3 | convolution fusion | flops 12891193344 | bytes 27275264 | tf_op jit(solution)/shard_map/xhrtf,rhxtg->fg/dot_general | solution.py:263
  (2 shorter events, 0.0 us)
Async XLA Ops:
  7.2 112.2 %all-gather.2.cloned.1.call-start = ((), (), s32[]{:S(2)}) async-start(), calls=%async_computation | async-start | bytes 13369344 | tf_op jit(solution)/shard_map/all_gather | solution.py:256
Sparse Core Ops, SparseCore 0:
  25.3 89.5 all-gather.1

commit v10 on v8

--- a/solution.py
+++ b/solution.py
@@ -223,6 +223,22 @@
     return jnp.dot(ones, panel, preferred_element_type=jnp.float32)[0]
 
 
+def _col_exchange(activations, n_col):
+    tokens = activations.shape[0]
+    c = lax.axis_index("col")
+    blocks = activations.reshape(tokens, n_col, activations.shape[1] // n_col)
+    order = lax.rem(c + jnp.arange(n_col, dtype=jnp.int32), n_col)
+    outgoing = jnp.take(blocks, order, axis=1)
+    pieces = [outgoing[:, 0]]
+    for k in range(1, n_col):
+        perm = [(i, (i + k) % n_col) for i in range(n_col)]
+        pieces.append(lax.ppermute(outgoing[:, k], "col", perm))
+    stacked = jnp.stack(pieces, axis=0)
+    back = lax.rem(c - jnp.arange(n_col, dtype=jnp.int32) + n_col, n_col)
+    piece = jnp.take(stacked, back, axis=0)
+    return piece.reshape(n_col * tokens, piece.shape[-1])
+
+
 def shards(activations, tenant_ids, concept_labels):
     local_tokens = activations.shape[0]
     width = activations.shape[1]
@@ -231,8 +247,8 @@
     n_x = col_count // Z_HI
     groups = TENANTS * LABELS
     codes = tenant_ids * LABELS + concept_labels
-    col_piece, codes = _col_piece(activations, codes.reshape(1, local_tokens), col_count)
-    col_piece = col_piece.reshape(col_count * local_tokens, col_piece.shape[-1])
+    codes = codes.reshape(1, local_tokens)
+    col_piece = _col_exchange(activations, col_count)
     col_panel = lax.all_gather(col_piece, "row", axis=0, tiled=True)
     colsum = jnp.sum(col_piece, axis=0, dtype=jnp.float32, keepdims=True)
     row_slots, code_slots, col_sums = _row_panel(activations, codes, colsum, row_count, col_count)

time: 145 us -> 151 us (1.041)
  starting transfers between devices: 0.04 us -> 16.6 us
  Pallas kernels: 99.5 us -> 83.7 us
  local copies, waits for them, and re-layouts: 0.95 us -> 3.62 us
  waiting for transfers between devices: 0.02 us -> 2.27 us
    pallas_call x1 -> x0, Pallas kernels: 16.8 us -> none  [_col_piece(): pl.pallas_call(functools.partial(_col_piece_kernel, n_col), out_shape=(ja...]
    ppermute x0 -> x7, starting transfers between devices: none -> 16.6 us  [_col_exchange(): pieces.append(lax.ppermute(outgoing[:, k], 'col', perm))]
    ppermute x0 -> x7, waiting for transfers between devices: none -> 2.26 us  [_col_exchange(): pieces.append(lax.ppermute(outgoing[:, k], 'col', perm))]
  transfers between devices with their start and end apart: 1 -> 8, of which waited for: 0 -> 2; matrix products, arithmetic and copies ran while one was open for 8% -> 7% of each run, Pallas kernels for 57% -> 56%
where the time goes in v10:
time: 151 us; the launch traced here: 150 us
  Pallas kernels  83.7 us (55%)
  matrix products  25.5 us (17%)
  starting transfers between devices  16.6 us (11%)
  between operations  14.2 us (9%)
  other arithmetic  4.25 us (3%)
  local copies, waits for them, and re-layouts  3.62 us (2%)
  waiting for transfers between devices  2.27 us (2%)
    pallas_call x1, Pallas kernels, _row_panel(): pl.pallas_call(functools.partial(_row_panel_kernel, n_row, n_x), out_shap...  83.7 us
    dot_general x1, matrix products, shards(): jnp.einsum('xhrtf,rhxtg->fg', row_slots, col_view, preferred_element_type...  18.9 us
    ppermute x7, starting transfers between devices, _col_exchange(): pieces.append(lax.ppermute(outgoing[:, k], 'col', perm))  16.6 us
    dot_general x1, matrix products, _column_sum(): return jnp.dot(ones, panel, preferred_element_type=jnp.float32)[0]  3.77 us
  transfers between devices with their start and end apart: 8, of which 2 were waited for; matrix products, arithmetic and copies ran while one was open for 7% of the time, Pallas kernels for 56%

profile of v10, /device:TPU:1, one launch (start us, length us, event | category | flops | bytes accessed | tf_op | source)
XLA Modules:
  0.0 150.2 jit_solution(10794212013447910061)
XLA Ops:
  7.2 0.0 all-gather.2.cloned.1.call-start
  7.3 1.2 copy.44
  8.5 0.6 gather_fusion
  9.1 0.1 select_bitcast_fusion
  9.3 2.1 %collective-permute-start = (bf16[24,2048]{1,0:T(8,128)(2,1)S(1)}, bf16[24,2048]{1,0:T(8,128)(2,1)S(1)}, u32[]{:S(2)}, u32[]{:S(2)}) collective-permute-start(bf16[24,2048]{1,0:T(8,128)(2,1)S(1)} %get-tuple-element.14), channel_id=1, source_target_pairs={{0,1},{1,2},{2,3},{3,4},{4,5},{5,6},{6,7},{7,0},{8,9},{9,10},{10,1... | collective-permute-start | bytes 294920 | tf_op jit(solution)/shard_map/ppermute | solution.py:235
  11.4 2.5 %collective-permute-start.1 = (bf16[24,2048]{1,0:T(8,128)(2,1)S(1)}, bf16[24,2048]{1,0:T(8,128)(2,1)S(1)}, u32[]{:S(2)}, u32[]{:S(2)}) collective-permute-start(bf16[24,2048]{1,0:T(8,128)(2,1)S(1)} %get-tuple-element.13), channel_id=1, source_target_pairs={{0,2},{1,3},{2,4},{3,5},{4,6},{5,7},{6,0},{7,1},{8,10},{9,11},{10,... | collective-permute-start | bytes 294920 | tf_op jit(solution)/shard_map/ppermute | solution.py:235
  13.8 4.5 %collective-permute-start.2 = (bf16[24,2048]{1,0:T(8,128)(2,1)S(1)}, bf16[24,2048]{1,0:T(8,128)(2,1)S(1)}, u32[]{:S(2)}, u32[]{:S(2)}) collective-permute-start(bf16[24,2048]{1,0:T(8,128)(2,1)S(1)} %get-tuple-element.12), channel_id=1, source_target_pairs={{0,3},{1,4},{2,5},{3,6},{4,7},{5,0},{6,1},{7,2},{8,11},{9,12},{10,... | collective-permute-start | bytes 294920 | tf_op jit(solution)/shard_map/ppermute | solution.py:235
  18.3 0.0 collective-permute-start.3
  18.3 3.0 %collective-permute-start.4 = (bf16[24,2048]{1,0:T(8,128)(2,1)S(1)}, bf16[24,2048]{1,0:T(8,128)(2,1)S(1)}, u32[]{:S(2)}, u32[]{:S(2)}) collective-permute-start(bf16[24,2048]{1,0:T(8,128)(2,1)S(1)} %get-tuple-element.10), channel_id=1, source_target_pairs={{0,5},{1,6},{2,7},{3,0},{4,1},{5,2},{6,3},{7,4},{8,13},{9,14},{10,... | collective-permute-start | bytes 294920 | tf_op jit(solution)/shard_map/ppermute | solution.py:235
  21.3 0.1 broadcast_in_dim.45
  21.4 0.1 broadcast_in_dim.46
  21.5 0.0 collective-permute-done
  21.5 3.0 %collective-permute-start.5 = (bf16[24,2048]{1,0:T(8,128)(2,1)S(1)}, bf16[24,2048]{1,0:T(8,128)(2,1)S(1)}, u32[]{:S(2)}, u32[]{:S(2)}) collective-permute-start(bf16[24,2048]{1,0:T(8,128)(2,1)S(1)} %get-tuple-element.9), channel_id=1, source_target_pairs={{0,6},{1,7},{2,0},{3,1},{4,2},{5,3},{6,4},{7,5},{8,14},{9,15},{10,... | collective-permute-start | bytes 294920 | tf_op jit(solution)/shard_map/ppermute | solution.py:235
  24.5 0.0 collective-permute-done.1
  24.5 1.5 %collective-permute-start.6 = (bf16[24,2048]{1,0:T(8,128)(2,1)S(1)}, bf16[24,2048]{1,0:T(8,128)(2,1)S(1)}, u32[]{:S(2)}, u32[]{:S(2)}) collective-permute-start(bf16[24,2048]{1,0:T(8,128)(2,1)S(1)} %get-tuple-element.8), channel_id=1, source_target_pairs={{0,7},{1,0},{2,1},{3,2},{4,3},{5,4},{6,5},{7,6},{8,15},{9,8},{10,9... | collective-permute-start | bytes 294920 | tf_op jit(solution)/shard_map/ppermute | solution.py:235
  26.1 0.0 collective-permute-done.2
  26.1 0.0 collective-permute-done.3
  26.1 0.0 collective-permute-done.4
  26.1 1.1 collective-permute-done.5
  27.2 1.2 collective-permute-done.6
  28.4 0.6 gather_fusion.1
  29.0 1.0 bitcast_select_fusion
  30.1 0.0 all-gather.2.cloned.1.call-update
  30.1 0.6 add_bitcast_fusion.code_ref
  30.7 0.8 convert_reduce_fusion.1
  31.5 83.7 %shard_map.50 = (bf16[4,2,16,24,1024]{4,3,2,1,0:T(8,128)(2,1)}, s32[4,2,16,1,24]{4,3,2,1,0:T(1,128)}, f32[16,1,2048]{2,1,0:T(1,128)}) custom-call(bf16[24,16384]{1,0:T(8,128)(2,1)} %x_ref.1, s32[1,24]{1,0:T(1,128)} %add_bitcast_fusion.code_ref, f32[1,2048]{1,0:T(1,128)} %bitcast.73), custom_call_target="tpu_custom_call" | custom-call | tf_op jit(solution)/shard_map/pallas_call | solution.py:142
  115.3 0.9 copy.28
  116.3 1.0 reduce_sum.32
  117.3 3.8 %convolution_multiply_fusion = f32[1,1024]{1,0:T(1,128)S(1)} fusion(bf16[3072,1024]{1,0:T(8,128)(2,1)} %bitcast.68), kind=kOutput, calls=%fused_computation.15 | convolution fusion | flops 6292480 | bytes 6295552 | tf_op jit(solution)/shard_map/dot_general | solution.py:223
  121.0 0.6 convert_reduce_fusion
  121.6 2.8 %fusion.11 = f32[128,128]{1,0:T(8,128)} fusion(s32[4,2,16,24]{3,0,2,1:T(4,128)S(1)} %copy.28, f32[128]{0:T(128)S(1)} %dynamic-slice_bitcast_fusion, f32[128]{0:T(128)S(1)} %convert_reduce_fusion, bf16[4,2,16,24,1024]{4,3,2,1,0:T(8,128)(2,1)} %get-tuple-element.5, s32[]{:T(128)S(6)} %select_n.54), kind=kOutput, calls=%fused_computation.14 | convolution fusion | flops 101105664 | bytes 865284 | tf_op jit(solution)/shard_map/xhrotg,xhrtf->gf/dot_general | solution.py:270
  124.5 18.9 %fusion.2 = f32[1024,2048]{1,0:T(8,128)} fusion(bf16[16,2,4,24,2048]{4,3,2,1,0:T(8,128)(2,1)} %bitcast.75, bf16[4,2,16,24,1024]{4,3,2,1,0:T(8,128)(2,1)} %get-tuple-element.5, f32[2048]{0:T(1024)S(1)} %broadcast_multiply_fusion, f32[1024]{0:T(1024)S(1)} %bitcast.74), kind=kOutput, calls=%fused_computation.5 | convolution fusion | flops 12891193344 | bytes 27275264 | tf_op jit(solution)/shard_map/xhrtf,rhxtg->fg/dot_general | solution.py:259
  (24 shorter events, 0.2 us)
Async XLA Ops:
  7.2 22.9 %copy-start.2 = (s32[24]{0:T(128)S(1)}, s32[24]{0:T(128)}, u32[]{:S(2)}) copy-start(s32[24]{0:T(128)} %param.4) | copy-start | bytes 292
  7.2 22.9 %copy-start.1 = (s32[24]{0:T(128)S(1)}, s32[24]{0:T(128)}, u32[]{:S(2)}) copy-start(s32[24]{0:T(128)} %param.5) | copy-start | bytes 292
  7.2 117.3 %all-gather.2.cloned.1.call-start = ((), (), s32[]{:S(2)}) async-start(), calls=%async_computation | async-start | bytes 13369344 | tf_op jit(solution)/shard_map/all_gather | solution.py:252
  9.3 12.2 %collective-permute-start = (bf16[24,2048]{1,0:T(8,128)(2,1)S(1)}, bf16[24,2048]{1,0:T(8,128)(2,1)S(1)}, u32[]{:S(2)}, u32[]{:S(2)}) collective-permute-start(bf16[24,2048]{1,0:T(8,128)(2,1)S(1)} %get-tuple-element.14), channel_id=1, source_target_pairs={{0,1},{1,2},{2,3},{3,4},{4,5},{5,6},{6,7},{7,0},{8,9},{9,10},{10,1... | collective-permute-start | bytes 294920 | tf_op jit(solution)/shard_map/ppermute | solution.py:235
  11.4 13.1 %collective-permute-start.1 = (bf16[24,2048]{1,0:T(8,128)(2,1)S(1)}, bf16[24,2048]{1,0:T(8,128)(2,1)S(1)}, u32[]{:S(2)}, u32[]{:S(2)}) collective-permute-start(bf16[24,2048]{1,0:T(8,128)(2,1)S(1)} %get-tuple-element.13), channel_id=1, source_target_pairs={{0,2},{1,3},{2,4},{3,5},{4,6},{5,7},{6,0},{7,1},{8,10},{9,11},{10,... | collective-permute-start | bytes 294920 | tf_op jit(solution)/shard_map/ppermute | solution.py:235
  13.8 12.2 %collective-permute-start.2 = (bf16[24,2048]{1,0:T(8,128)(2,1)S(1)}, bf16[24,2048]{1,0:T(8,128)(2,1)S(1)}, u32[]{:S(2)}, u32[]{:S(2)}) collective-permute-start(bf16[24,2048]{1,0:T(8,128)(2,1)S(1)} %get-tuple-element.12), channel_id=1, source_target_pairs={{0,3},{1,4},{2,5},{3,6},{4,7},{5,0},{6,1},{7,2},{8,11},{9,12},{10,... | collective-permute-start | bytes 294920 | tf_op jit(solution)/shard_map/ppermute | solution.py:235
  18.3 7.8 %collective-permute-start.3 = (bf16[24,2048]{1,0:T(8,128)(2,1)S(1)}, bf16[24,2048]{1,0:T(8,128)(2,1)S(1)}, u32[]{:S(2)}, u32[]{:S(2)}) collective-permute-start(bf16[24,2048]{1,0:T(8,128)(2,1)S(1)} %get-tuple-element.11), channel_id=1, source_target_pairs={{0,4},{1,5},{2,6},{3,7},{4,0},{5,1},{6,2},{7,3},{8,12},{9,13},{10,... | collective-permute-start | bytes 294920 | tf_op jit(solution)/shard_map/ppermute | solution.py:235
  18.3 7.8 %collective-permute-start.4 = (bf16[24,2048]{1,0:T(8,128)(2,1)S(1)}, bf16[24,2048]{1,0:T(8,128)(2,1)S(1)}, u32[]{:S(2)}, u32[]{:S(2)}) collective-permute-start(bf16[24,2048]{1,0:T(8,128)(2,1)S(1)} %get-tuple-element.10), channel_id=1, source_target_pairs={{0,5},{1,6},{2,7},{3,0},{4,1},{5,2},{6,3},{7,4},{8,13},{9,14},{10,... | collective-permute-start | bytes 294920 | tf_op jit(solution)/shard_map/ppermute | solution.py:235
  21.5 5.7 %collective-permute-start.5 = (bf16[24,2048]{1,0:T(8,128)(2,1)S(1)}, bf16[24,2048]{1,0:T(8,128)(2,1)S(1)}, u32[]{:S(2)}, u32[]{:S(2)}) collective-permute-start(bf16[24,2048]{1,0:T(8,128)(2,1)S(1)} %get-tuple-element.9), channel_id=1, source_target_pairs={{0,6},{1,7},{2,0},{3,1},{4,2},{5,3},{6,4},{7,5},{8,14},{9,15},{10,... | collective-permute-start | bytes 294920 | tf_op jit(solution)/shard_map/ppermute | solution.py:235
  24.5 3.9 %collective-permute-start.6 = (bf16[24,2048]{1,0:T(8,128)(2,1)S(1)}, bf16[24,2048]{1,0:T(8,128)(2,1)S(1)}, u32[]{:S(2)}, u32[]{:S(2)}) collective-permute-start(bf16[24,2048]{1,0:T(8,128)(2,1)S(1)} %get-tuple-element.8), channel_id=1, source_target_pairs={{0,7},{1,0},{2,1},{3,2},{4,3},{5,4},{6,5},{7,6},{8,15},{9,8},{10,9... | collective-permute-start | bytes 294920 | tf_op jit(solution)/shard_map/ppermute | solution.py:235
  115.3 5.7 %copy-start = (s32[4,2,16,1,24]{4,3,2,1,0:T(1,128)S(1)}, s32[4,2,16,1,24]{4,3,2,1,0:T(1,128)}, u32[]{:S(2)}) copy-start(s32[4,2,16,1,24]{4,3,2,1,0:T(1,128)} %get-tuple-element.7) | copy-start | bytes 36868
Sparse Core Ops, SparseCore 0:
  30.2 89.6 all-gather.1

commit v11 on v5

--- a/solution.py
+++ b/solution.py
@@ -11,6 +11,7 @@
 LABELS = 2
 MESH = pl.DeviceIdType.MESH
 Z_HI = 2
+SIDE_CODES = 128
 
 
 def _row_panel_kernel(n_row, n_x, x_ref, code_ref, p_ref, pc_ref,
@@ -62,6 +63,9 @@
         cc.start()
         stage1[min(dz, 1)] += [cp, cc]
 
+    def lanes(ref):
+        return ref.at[:, :, pl.ds(0, SIDE_CODES)]
+
     def send(src, dst, sems, idx, target):
         return pltpu.make_async_remote_copy(
             src_ref=src, dst_ref=dst, send_sem=sems[0].at[idx], recv_sem=sems[1].at[idx],
@@ -76,8 +80,8 @@
         pair = [
             send(p_ref.at[x, plane], p_ref.at[x, plane], (s2, r2), 2 * h, right),
             send(p_ref.at[x, plane], p_ref.at[x, plane], (s2, r2), 2 * h + 1, left),
-            send(pc_ref.at[x, plane], pc_ref.at[x, plane], (s2c, r2c), 2 * h, right),
-            send(pc_ref.at[x, plane], pc_ref.at[x, plane], (s2c, r2c), 2 * h + 1, left),
+            send(lanes(pc_ref.at[x, plane]), lanes(pc_ref.at[x, plane]), (s2c, r2c), 2 * h, right),
+            send(lanes(pc_ref.at[x, plane]), lanes(pc_ref.at[x, plane]), (s2c, r2c), 2 * h + 1, left),
         ]
         for cp in pair:
             cp.start()
@@ -89,7 +93,7 @@
     halves[0][2].wait_recv()
     fwd = [
         send(p_ref.at[from_left, zh], p_ref.at[from_left, zh], (s2, r2), 4, right),
-        send(pc_ref.at[from_left, zh], pc_ref.at[from_left, zh], (s2c, r2c), 4, right),
+        send(lanes(pc_ref.at[from_left, zh]), lanes(pc_ref.at[from_left, zh]), (s2c, r2c), 4, right),
     ]
     for cp in fwd:
         cp.start()
@@ -97,7 +101,7 @@
     halves[1][3].wait_recv()
     fwd2 = [
         send(p_ref.at[from_right, 1 - zh], p_ref.at[from_right, 1 - zh], (s2, r2), 5, left),
-        send(pc_ref.at[from_right, 1 - zh], pc_ref.at[from_right, 1 - zh], (s2c, r2c), 5, left),
+        send(lanes(pc_ref.at[from_right, 1 - zh]), lanes(pc_ref.at[from_right, 1 - zh]), (s2c, r2c), 5, left),
     ]
     for cp in fwd2:
         cp.start()
@@ -115,7 +119,7 @@
         cp.wait()
 
 
-def _row_panel(activations, codes, n_row, n_col):
+def _row_panel(activations, side, n_row, n_col):
     tokens = activations.shape[0]
     width = activations.shape[1] // n_row
     n_x = n_col // Z_HI
@@ -126,7 +130,7 @@
         functools.partial(_row_panel_kernel, n_row, n_x),
         out_shape=(
             jax.ShapeDtypeStruct((n_x, Z_HI, n_row, tokens, width), activations.dtype),
-            jax.ShapeDtypeStruct((n_x, Z_HI, n_row, 1, tokens), jnp.int32),
+            jax.ShapeDtypeStruct((n_x, Z_HI, n_row) + side.shape, side.dtype),
         ),
         in_specs=[any_spec, any_spec],
         out_specs=(any_spec, any_spec),
@@ -142,7 +146,7 @@
             pltpu.SemaphoreType.DMA((2,)),
         ],
         compiler_params=pltpu.CompilerParams(collective_id=0, has_side_effects=True),
-    )(activations, codes)
+    )(activations, side)
 
 
 def _col_piece_kernel(n_col, x_ref, code_ref, o_ref, code_out, send_sem, recv_sem, lsem):
@@ -214,14 +218,19 @@
     col_piece, codes = _col_piece(activations, codes.reshape(1, local_tokens), col_count)
     col_piece = col_piece.reshape(col_count * local_tokens, col_piece.shape[-1])
     col_panel = lax.all_gather(col_piece, "row", axis=0, tiled=True)
-    row_slots, code_slots = _row_panel(activations, codes, row_count, col_count)
+    colsum = jnp.sum(col_piece, axis=0, dtype=jnp.float32, keepdims=True)
+    side = jnp.concatenate(
+        [jnp.pad(codes.astype(jnp.float32), ((0, 0), (0, SIDE_CODES - local_tokens))), colsum], axis=1)
+    row_slots, side_slots = _row_panel(activations, side, row_count, col_count)
+    code_slots = side_slots[:, :, :, :, :local_tokens].astype(jnp.int32)
+    col_sums = side_slots[lax.rem(lax.axis_index("col"), n_x), lax.axis_index("col") // n_x, :, :, SIDE_CODES:]
     total = col_panel.shape[0]
     row_width = row_slots.shape[-1]
     row_panel = row_slots.reshape(total, row_width)
     col_view = col_panel.reshape(row_count, Z_HI, n_x, local_tokens, col_panel.shape[1])
     gram = jnp.einsum("xhrtf,rhxtg->fg", row_slots, col_view, preferred_element_type=jnp.float32)
     mean_row = _column_sum(row_panel) / total
-    mean_col = _column_sum(col_panel) / total
+    mean_col = jnp.sum(col_sums, axis=(0, 1)) / total
     covariance = gram / total - mean_row[:, None] * mean_col[None, :]
     slice_width = width // (row_count * col_count)
     slice_start = lax.axis_index("col") * slice_width

time: 146 us -> 148 us (1.014)
  Pallas kernels: 95.5 us -> 101 us
  matrix products: 30.7 us -> 25.5 us
  other arithmetic: 2.53 us -> 6.14 us
  local copies, waits for them, and re-layouts: 2.59 us -> 0.05 us
    dot_general x2 -> x1, matrix products: 10.2 us -> 3.77 us  [_column_sum(): return jnp.dot(ones, panel, preferred_element_type=jnp.float32)[0]]
    pallas_call x1, Pallas kernels: 78.8 us -> 84.7 us  [_row_panel(): pl.pallas_call(functools.partial(_row_panel_kernel, n_row, n_x), out_shap...]
    reduce_sum x0 -> x2, other arithmetic: none -> 2.25 us  [the longest x1 1.26 us: shards(): colsum = jnp.sum(col_piece, axis=0, dtype=jnp.float32, keepdims=True)]
    unnamed x2 -> x0, local copies, waits for them, and re-layouts: 1.7 us -> none
    convert_element_type x0 -> x2, other arithmetic: none -> 1.52 us  [the longest x1 0.89 us: shards(): code_slots = side_slots[:, :, :, :, :local_tokens].astype(jnp.int32)]
  transfers between devices with their start and end apart: 1 -> 1, of which waited for: 0 -> 0; matrix products, arithmetic and copies ran while one was open for 6% -> 8% of each run, Pallas kernels for 54% -> 57%
where the time goes in v11:
time: 148 us; the launch traced here: 147 us
  Pallas kernels  101 us (68%)
  matrix products  25.5 us (17%)
  between operations  14.1 us (10%)
  other arithmetic  6.14 us (4%)
    pallas_call x1, Pallas kernels, _row_panel(): pl.pallas_call(functools.partial(_row_panel_kernel, n_row, n_x), out_shap...  84.7 us
    dot_general x1, matrix products, shards(): jnp.einsum('xhrtf,rhxtg->fg', row_slots, col_view, preferred_element_type...  18.9 us
    pallas_call x1, Pallas kernels, _col_piece(): pl.pallas_call(functools.partial(_col_piece_kernel, n_col), out_shape=(ja...  16.8 us
    dot_general x1, matrix products, _column_sum(): return jnp.dot(ones, panel, preferred_element_type=jnp.float32)[0]  3.77 us
  transfers between devices with their start and end apart: 1, of which 0 were waited for; matrix products, arithmetic and copies ran while one was open for 8% of the time, Pallas kernels for 57%

profile of v11, /device:TPU:1, one launch (start us, length us, event | category | flops | bytes accessed | tf_op | source)
XLA Modules:
  0.0 147.4 jit_solution(12608422094361476608)
XLA Ops:
  7.2 0.0 all-gather.2.cloned.1.call-start
  7.2 1.2 add_bitcast_fusion.code_ref
  8.4 16.8 %shard_map.50 = (bf16[8,24,2048]{2,1,0:T(8,128)(2,1)}, s32[1,24]{1,0:T(1,128)}) custom-call(bf16[24,16384]{1,0:T(8,128)(2,1)} %x_ref.3, s32[1,24]{1,0:T(1,128)} %add_bitcast_fusion.code_ref), custom_call_target="tpu_custom_call" | custom-call | tf_op jit(solution)/shard_map/pallas_call | solution.py:188
  25.2 0.0 all-gather.2.cloned.1.call-update
  25.2 0.6 convert_element_type.25
  25.9 1.3 convert_reduce_fusion.1
  27.1 0.6 fusion.14.code_ref
  27.7 84.7 %shard_map.51 = (bf16[4,2,16,24,1024]{4,3,2,1,0:T(8,128)(2,1)}, f32[4,2,16,1,2176]{4,3,2,1,0:T(1,128)}) custom-call(bf16[24,16384]{1,0:T(8,128)(2,1)} %x_ref.3, f32[1,2176]{1,0:T(1,128)} %fusion.14.code_ref), custom_call_target="tpu_custom_call" | custom-call | tf_op jit(solution)/shard_map/pallas_call | solution.py:129
  112.5 0.9 slice_convert_fusion
  113.4 1.0 dynamic-slice_reduce_fusion
  114.4 3.8 %convolution_multiply_fusion = f32[1,1024]{1,0:T(1,128)S(1)} fusion(bf16[3072,1024]{1,0:T(8,128)(2,1)} %bitcast.25), kind=kOutput, calls=%fused_computation.13 | convolution fusion | flops 6292480 | bytes 6295552 | tf_op jit(solution)/shard_map/dot_general | solution.py:207
  118.2 0.6 convert_reduce_fusion
  118.8 2.8 %fusion.11 = f32[128,128]{1,0:T(8,128)} fusion(s32[4,2,16,24]{3,0,2,1:T(4,128)S(1)} %copy.14, f32[128]{0:T(128)S(1)} %fusion.16, f32[128]{0:T(128)S(1)} %convert_reduce_fusion, bf16[4,2,16,24,1024]{4,3,2,1,0:T(8,128)(2,1)} %get-tuple-element.8, s32[]{:T(128)S(6)} %select_n.18), kind=kOutput, calls=%fused_computation.12 | convolution fusion | flops 101105664 | bytes 865284 | tf_op jit(solution)/shard_map/xhrotg,xhrtf->gf/dot_general | solution.py:242
  121.6 0.0 all-gather.2.cloned.1.call-done
  121.6 18.9 %fusion.2 = f32[1024,2048]{1,0:T(8,128)} fusion(bf16[16,2,4,24,2048]{4,3,2,1,0:T(8,128)(2,1)} %bitcast.31, bf16[4,2,16,24,1024]{4,3,2,1,0:T(8,128)(2,1)} %get-tuple-element.8, f32[2048]{0:T(1024)S(1)} %broadcast_multiply_fusion, f32[1024]{0:T(1024)S(1)} %bitcast.30), kind=kOutput, calls=%fused_computation.3 | convolution fusion | flops 12891193344 | bytes 27275264 | tf_op jit(solution)/shard_map/xhrtf,rhxtg->fg/dot_general | solution.py:231
  (3 shorter events, 0.1 us)
Async XLA Ops:
  7.2 114.4 %all-gather.2.cloned.1.call-start = ((), (), s32[]{:S(2)}) async-start(), calls=%async_computation | async-start | bytes 13369344 | tf_op jit(solution)/shard_map/all_gather | solution.py:220
Sparse Core Ops, SparseCore 0:
  25.3 91.5 all-gather.1

commit v12 on v8

--- a/solution.py
+++ b/solution.py
@@ -35,8 +35,8 @@
     pl.semaphore_wait(barrier, len(sources) + 2)
 
     own = pltpu.make_async_copy(
-        x_ref.at[:, pl.ds(pl.multiple_of(r * width, width), width)], p_ref.at[x, zh, r], lsem.at[0])
-    own_codes = pltpu.make_async_copy(code_ref, pc_ref.at[x, zh, r], lsem.at[1])
+        x_ref.at[:, pl.ds(pl.multiple_of(r * width, width), width)], p_ref.at[r, zh, x], lsem.at[0])
+    own_codes = pltpu.make_async_copy(code_ref, pc_ref.at[r, zh, x], lsem.at[1])
     own_sum = pltpu.make_async_copy(cs_ref, cs_out.at[r], lsem.at[2])
     own.start()
     own_codes.start()
@@ -47,7 +47,7 @@
         pr, pc = peer(dz, dr)
         cp = pltpu.make_async_remote_copy(
             src_ref=x_ref.at[:, pl.ds(pl.multiple_of(pr * width, width), width)],
-            dst_ref=p_ref.at[x, zh, r],
+            dst_ref=p_ref.at[r, zh, x],
             send_sem=s1.at[i],
             recv_sem=r1.at[i],
             device_id=(pr, pc),
@@ -55,7 +55,7 @@
         )
         cc = pltpu.make_async_remote_copy(
             src_ref=code_ref,
-            dst_ref=pc_ref.at[x, zh, r],
+            dst_ref=pc_ref.at[r, zh, x],
             send_sem=s1c.at[i],
             recv_sem=r1c.at[i],
             device_id=(pr, pc),
@@ -88,10 +88,10 @@
         for cp in stage1[h]:
             cp.wait_recv()
         pair = [
-            send(p_ref.at[x, plane], p_ref.at[x, plane], (s2, r2), 2 * h, right),
-            send(p_ref.at[x, plane], p_ref.at[x, plane], (s2, r2), 2 * h + 1, left),
-            send(pc_ref.at[x, plane], pc_ref.at[x, plane], (s2c, r2c), 2 * h, right),
-            send(pc_ref.at[x, plane], pc_ref.at[x, plane], (s2c, r2c), 2 * h + 1, left),
+            send(p_ref.at[:, plane, x], p_ref.at[:, plane, x], (s2, r2), 2 * h, right),
+            send(p_ref.at[:, plane, x], p_ref.at[:, plane, x], (s2, r2), 2 * h + 1, left),
+            send(pc_ref.at[:, plane, x], pc_ref.at[:, plane, x], (s2c, r2c), 2 * h, right),
+            send(pc_ref.at[:, plane, x], pc_ref.at[:, plane, x], (s2c, r2c), 2 * h + 1, left),
         ]
         for cp in pair:
             cp.start()
@@ -102,16 +102,16 @@
     halves[0][0].wait_recv()
     halves[0][2].wait_recv()
     fwd = [
-        send(p_ref.at[from_left, zh], p_ref.at[from_left, zh], (s2, r2), 4, right),
-        send(pc_ref.at[from_left, zh], pc_ref.at[from_left, zh], (s2c, r2c), 4, right),
+        send(p_ref.at[:, zh, from_left], p_ref.at[:, zh, from_left], (s2, r2), 4, right),
+        send(pc_ref.at[:, zh, from_left], pc_ref.at[:, zh, from_left], (s2c, r2c), 4, right),
     ]
     for cp in fwd:
         cp.start()
     halves[1][1].wait_recv()
     halves[1][3].wait_recv()
     fwd2 = [
-        send(p_ref.at[from_right, 1 - zh], p_ref.at[from_right, 1 - zh], (s2, r2), 5, left),
-        send(pc_ref.at[from_right, 1 - zh], pc_ref.at[from_right, 1 - zh], (s2c, r2c), 5, left),
+        send(p_ref.at[:, 1 - zh, from_right], p_ref.at[:, 1 - zh, from_right], (s2, r2), 5, left),
+        send(pc_ref.at[:, 1 - zh, from_right], pc_ref.at[:, 1 - zh, from_right], (s2c, r2c), 5, left),
     ]
     for cp in fwd2:
         cp.start()
@@ -142,8 +142,8 @@
     return pl.pallas_call(
         functools.partial(_row_panel_kernel, n_row, n_x),
         out_shape=(
-            jax.ShapeDtypeStruct((n_x, Z_HI, n_row, tokens, width), activations.dtype),
-            jax.ShapeDtypeStruct((n_x, Z_HI, n_row, 1, tokens), jnp.int32),
+            jax.ShapeDtypeStruct((n_row, Z_HI, n_x, tokens, width), activations.dtype),
+            jax.ShapeDtypeStruct((n_row, Z_HI, n_x, 1, tokens), jnp.int32),
             jax.ShapeDtypeStruct((n_row,) + colsum.shape, colsum.dtype),
         ),
         in_specs=[any_spec, any_spec, any_spec],
@@ -239,8 +239,7 @@
     total = col_panel.shape[0]
     row_width = row_slots.shape[-1]
     row_panel = row_slots.reshape(total, row_width)
-    col_view = col_panel.reshape(row_count, Z_HI, n_x, local_tokens, col_panel.shape[1])
-    gram = jnp.einsum("xhrtf,rhxtg->fg", row_slots, col_view, preferred_element_type=jnp.float32)
+    gram = jnp.einsum("tf,tg->fg", row_panel, col_panel, preferred_element_type=jnp.float32)
     mean_row = _column_sum(row_panel) / total
     mean_col = jnp.sum(col_sums, axis=(0, 1)) / total
     covariance = gram / total - mean_row[:, None] * mean_col[None, :]
@@ -252,7 +251,7 @@
     counts = jnp.sum(onehot_all.astype(jnp.float32), axis=(0, 1, 2, 3, 4))
     panel_slice = lax.dynamic_slice_in_dim(row_slots, slice_start, slice_width, 4)
     sums = jnp.einsum(
-        "xhrotg,xhrtf->gf",
+        "rhxotg,rhxtf->gf",
         onehot_all.astype(jnp.bfloat16),
         panel_slice,
         preferred_element_type=jnp.float32,

time: 145 us -> 144 us (level)
  transfers between devices with their start and end apart: 1 -> 1, of which waited for: 0 -> 0; matrix products, arithmetic and copies ran while one was open for 8% -> 7% of each run, Pallas kernels for 57% -> 58%
where the time goes in v12:
time: 144 us
  Pallas kernels  99.8 us (69%)
  matrix products  25.5 us (18%)
  between operations  14.1 us (10%)
  other arithmetic  4.65 us (3%)
    pallas_call x1, Pallas kernels, _row_panel(): pl.pallas_call(functools.partial(_row_panel_kernel, n_row, n_x), out_shap...  83 us
    dot_general x1, matrix products, shards(): jnp.einsum('tf,tg->fg', row_panel, col_panel, preferred_element_type=jnp....  18.9 us
    pallas_call x1, Pallas kernels, _col_piece(): pl.pallas_call(functools.partial(_col_piece_kernel, n_col), out_shape=(ja...  16.8 us
    dot_general x1, matrix products, _column_sum(): return jnp.dot(ones, panel, preferred_element_type=jnp.float32)[0]  3.77 us
  transfers between devices with their start and end apart: 1, of which 0 were waited for; matrix products, arithmetic and copies ran while one was open for 7% of the time, Pallas kernels for 58%

profile of v12, /device:TPU:1, one launch (start us, length us, event | category | flops | bytes accessed | tf_op | source)
XLA Modules:
  0.0 144.1 jit_solution(18156187557005718875)
XLA Ops:
  7.2 0.0 all-gather.2.cloned.1.call-start
  7.2 1.2 add_bitcast_fusion.code_ref
  8.4 16.8 %shard_map.50 = (bf16[8,24,2048]{2,1,0:T(8,128)(2,1)}, s32[1,24]{1,0:T(1,128)}) custom-call(bf16[24,16384]{1,0:T(8,128)(2,1)} %x_ref.3, s32[1,24]{1,0:T(1,128)} %add_bitcast_fusion.code_ref), custom_call_target="tpu_custom_call" | custom-call | tf_op jit(solution)/shard_map/pallas_call | solution.py:204
  25.2 0.0 all-gather.2.cloned.1.call-update
  25.2 1.9 %convert_reduce_fusion.1 = f32[2048]{0:T(1024)} fusion(bf16[8,24,2048]{2,1,0:T(8,128)(2,1)} %get-tuple-element.8), kind=kLoop, calls=%fused_computation.4 | loop fusion | flops 784384 | bytes 794624 | tf_op jit(solution)/shard_map/reduce_sum | solution.py:237
  27.1 83.0 %shard_map.51 = (bf16[16,2,4,24,1024]{4,3,2,1,0:T(8,128)(2,1)}, s32[16,2,4,1,24]{4,3,2,1,0:T(1,128)}, f32[16,1,2048]{2,1,0:T(1,128)}) custom-call(bf16[24,16384]{1,0:T(8,128)(2,1)} %x_ref.3, s32[1,24]{1,0:T(1,128)} %get-tuple-element.7.code_ref, f32[1,2048]{1,0:T(1,128)} %bitcast.25), custom_call_target="tpu_custom_call" | custom-call | tf_op jit(solution)/shard_map/pallas_call | solution.py:142
  110.1 0.0 copy-start
  110.1 1.0 reduce_sum.32
  111.1 3.8 %convolution_multiply_fusion = f32[1,1024]{1,0:T(1,128)S(1)} fusion(bf16[3072,1024]{1,0:T(8,128)(2,1)} %bitcast.20), kind=kOutput, calls=%fused_computation.9 | convolution fusion | flops 6292480 | bytes 6295552 | tf_op jit(solution)/shard_map/dot_general | solution.py:223
  114.9 0.0 copy-done
  114.9 0.6 convert_reduce_fusion
  115.5 2.8 %fusion.3 = f32[128,128]{1,0:T(8,128)} fusion(f32[128]{0:T(128)S(1)} %dynamic-slice_bitcast_fusion, f32[128]{0:T(128)S(1)} %convert_reduce_fusion, bf16[16,2,4,24,1024]{4,3,2,1,0:T(8,128)(2,1)} %get-tuple-element.9, s32[]{:T(128)S(6)} %select_n.4, s32[16,2,4,24]{3,2,1,0:T(4,128)S(1)} %bitcast.24), kind=kOutput, calls=%fused_computation.8 | convolution fusion | flops 101105664 | bytes 865284 | tf_op jit(solution)/shard_map/rhxotg,rhxtf->gf/dot_general | solution.py:253
  118.3 0.0 all-gather.2.cloned.1.call-done
  118.3 18.9 %multiply_subtract_fusion = f32[1024,2048]{1,0:T(8,128)} fusion(bf16[3072,1024]{1,0:T(8,128)(2,1)} %bitcast.21, bf16[3072,2048]{1,0:T(8,128)(2,1)} %all-gather.2.cloned.1.call-done, f32[2048]{0:T(1024)S(1)} %broadcast_multiply_fusion, f32[1024]{0:T(1024)S(1)} %bitcast.26), kind=kOutput, calls=%fused_computation | convolution fusion | flops 12891193344 | bytes 27275264 | tf_op jit(solution)/shard_map/tf,tg->fg/dot_general | solution.py:242
  (2 shorter events, 0.0 us)
Async XLA Ops:
  7.2 111.1 %all-gather.2.cloned.1.call-start = ((), (), s32[]{:S(2)}) async-start(), calls=%async_computation | async-start | bytes 13369344 | tf_op jit(solution)/shard_map/all_gather | solution.py:236
  110.1 4.8 %copy-start = (s32[16,2,4,1,24]{4,3,2,1,0:T(1,128)S(1)}, s32[16,2,4,1,24]{4,3,2,1,0:T(1,128)}, u32[]{:S(2)}) copy-start(s32[16,2,4,1,24]{4,3,2,1,0:T(1,128)} %get-tuple-element.11) | copy-start | bytes 36868
Sparse Core Ops, SparseCore 0:
  25.3 89.5 all-gather.1

commit v13 on v12

--- a/solution.py
+++ b/solution.py
@@ -22,7 +22,7 @@
     width = p_ref.shape[-1]
     left = zh * n_x + lax.rem(x + n_x - 1, n_x)
     right = zh * n_x + lax.rem(x + 1, n_x)
-    sources = [(dz, dr) for dz in range(Z_HI) for dr in range(n_row) if dz or dr]
+    sources = [(dz, dr) for dz in range(Z_HI - 1, -1, -1) for dr in range(n_row) if dz or dr]
 
     def peer(dz, dr):
         return lax.rem(r + dr, n_row), lax.rem(zh + dz, Z_HI) * n_x + x
@@ -63,7 +63,7 @@
         )
         cp.start()
         cc.start()
-        stage1[min(dz, 1)] += [cp, cc]
+        stage1[1 - min(dz, 1)] += [cp, cc]
         if dz == 0:
             cs = pltpu.make_async_remote_copy(
                 src_ref=cs_ref,
@@ -84,7 +84,7 @@
     own.wait()
     own_codes.wait()
     halves = []
-    for h, plane in enumerate((zh, 1 - zh)):
+    for h, plane in enumerate((1 - zh, zh)):
         for cp in stage1[h]:
             cp.wait_recv()
         pair = [
@@ -99,32 +99,32 @@
 
     from_left = lax.rem(x + n_x - 1, n_x)
     from_right = lax.rem(x + 1, n_x)
-    halves[0][0].wait_recv()
-    halves[0][2].wait_recv()
+    halves[0][1].wait_recv()
+    halves[0][3].wait_recv()
+    fwd2 = [
+        send(p_ref.at[:, 1 - zh, from_right], p_ref.at[:, 1 - zh, from_right], (s2, r2), 5, left),
+        send(pc_ref.at[:, 1 - zh, from_right], pc_ref.at[:, 1 - zh, from_right], (s2c, r2c), 5, left),
+    ]
+    for cp in fwd2:
+        cp.start()
+    halves[1][0].wait_recv()
+    halves[1][2].wait_recv()
     fwd = [
         send(p_ref.at[:, zh, from_left], p_ref.at[:, zh, from_left], (s2, r2), 4, right),
         send(pc_ref.at[:, zh, from_left], pc_ref.at[:, zh, from_left], (s2c, r2c), 4, right),
     ]
     for cp in fwd:
         cp.start()
-    halves[1][1].wait_recv()
-    halves[1][3].wait_recv()
-    fwd2 = [
-        send(p_ref.at[:, 1 - zh, from_right], p_ref.at[:, 1 - zh, from_right], (s2, r2), 5, left),
-        send(pc_ref.at[:, 1 - zh, from_right], pc_ref.at[:, 1 - zh, from_right], (s2c, r2c), 5, left),
-    ]
-    for cp in fwd2:
-        cp.start()
 
     for cp in stage1[0] + stage1[1]:
         cp.wait_send()
     for pair in halves:
         for cp in pair:
             cp.wait_send()
-    halves[0][1].wait_recv()
-    halves[0][3].wait_recv()
-    halves[1][0].wait_recv()
-    halves[1][2].wait_recv()
+    halves[0][0].wait_recv()
+    halves[0][2].wait_recv()
+    halves[1][1].wait_recv()
+    halves[1][3].wait_recv()
     for cp in fwd + fwd2:
         cp.wait()
     own_sum.wait()

time: 144 us -> 145 us (level)
  no operation moved by 1% of the time
where the time goes in v13:
time: 145 us
  Pallas kernels  100 us (69%)
  matrix products  25.5 us (18%)
  between operations  14.1 us (10%)
  other arithmetic  4.65 us (3%)
    pallas_call x1, Pallas kernels, _row_panel(): pl.pallas_call(functools.partial(_row_panel_kernel, n_row, n_x), out_shap...  83.5 us
    dot_general x1, matrix products, shards(): jnp.einsum('tf,tg->fg', row_panel, col_panel, preferred_element_type=jnp....  18.9 us
    pallas_call x1, Pallas kernels, _col_piece(): pl.pallas_call(functools.partial(_col_piece_kernel, n_col), out_shape=(ja...  16.8 us
    dot_general x1, matrix products, _column_sum(): return jnp.dot(ones, panel, preferred_element_type=jnp.float32)[0]  3.77 us
  transfers between devices with their start and end apart: 1, of which 0 were waited for; matrix products, arithmetic and copies ran while one was open for 7% of the time, Pallas kernels for 58%

profile of v13, /device:TPU:1, one launch (start us, length us, event | category | flops | bytes accessed | tf_op | source)
XLA Modules:
  0.0 144.6 jit_solution(5751538930680261098)
XLA Ops:
  7.2 0.0 all-gather.2.cloned.1.call-start
  7.2 1.2 add_bitcast_fusion.code_ref
  8.4 16.8 %shard_map.50 = (bf16[8,24,2048]{2,1,0:T(8,128)(2,1)}, s32[1,24]{1,0:T(1,128)}) custom-call(bf16[24,16384]{1,0:T(8,128)(2,1)} %x_ref.3, s32[1,24]{1,0:T(1,128)} %add_bitcast_fusion.code_ref), custom_call_target="tpu_custom_call" | custom-call | tf_op jit(solution)/shard_map/pallas_call | solution.py:204
  25.2 0.0 all-gather.2.cloned.1.call-update
  25.2 1.9 %convert_reduce_fusion.1 = f32[2048]{0:T(1024)} fusion(bf16[8,24,2048]{2,1,0:T(8,128)(2,1)} %get-tuple-element.8), kind=kLoop, calls=%fused_computation.4 | loop fusion | flops 784384 | bytes 794624 | tf_op jit(solution)/shard_map/reduce_sum | solution.py:237
  27.1 83.5 %shard_map.51 = (bf16[16,2,4,24,1024]{4,3,2,1,0:T(8,128)(2,1)}, s32[16,2,4,1,24]{4,3,2,1,0:T(1,128)}, f32[16,1,2048]{2,1,0:T(1,128)}) custom-call(bf16[24,16384]{1,0:T(8,128)(2,1)} %x_ref.3, s32[1,24]{1,0:T(1,128)} %get-tuple-element.7.code_ref, f32[1,2048]{1,0:T(1,128)} %bitcast.25), custom_call_target="tpu_custom_call" | custom-call | tf_op jit(solution)/shard_map/pallas_call | solution.py:142
  110.6 0.0 copy-start
  110.6 1.0 reduce_sum.32
  111.6 3.8 %convolution_multiply_fusion = f32[1,1024]{1,0:T(1,128)S(1)} fusion(bf16[3072,1024]{1,0:T(8,128)(2,1)} %bitcast.20), kind=kOutput, calls=%fused_computation.9 | convolution fusion | flops 6292480 | bytes 6295552 | tf_op jit(solution)/shard_map/dot_general | solution.py:223
  115.4 0.0 copy-done
  115.4 0.6 convert_reduce_fusion
  116.0 2.8 %fusion.3 = f32[128,128]{1,0:T(8,128)} fusion(f32[128]{0:T(128)S(1)} %dynamic-slice_bitcast_fusion, f32[128]{0:T(128)S(1)} %convert_reduce_fusion, bf16[16,2,4,24,1024]{4,3,2,1,0:T(8,128)(2,1)} %get-tuple-element.9, s32[]{:T(128)S(6)} %select_n.4, s32[16,2,4,24]{3,2,1,0:T(4,128)S(1)} %bitcast.24), kind=kOutput, calls=%fused_computation.8 | convolution fusion | flops 101105664 | bytes 865284 | tf_op jit(solution)/shard_map/rhxotg,rhxtf->gf/dot_general | solution.py:253
  118.8 0.0 all-gather.2.cloned.1.call-done
  118.8 18.9 %multiply_subtract_fusion = f32[1024,2048]{1,0:T(8,128)} fusion(bf16[3072,1024]{1,0:T(8,128)(2,1)} %bitcast.21, bf16[3072,2048]{1,0:T(8,128)(2,1)} %all-gather.2.cloned.1.call-done, f32[2048]{0:T(1024)S(1)} %broadcast_multiply_fusion, f32[1024]{0:T(1024)S(1)} %bitcast.26), kind=kOutput, calls=%fused_computation | convolution fusion | flops 12891193344 | bytes 27275264 | tf_op jit(solution)/shard_map/tf,tg->fg/dot_general | solution.py:242
  (2 shorter events, 0.0 us)
Async XLA Ops:
  7.2 111.7 %all-gather.2.cloned.1.call-start = ((), (), s32[]{:S(2)}) async-start(), calls=%async_computation | async-start | bytes 13369344 | tf_op jit(solution)/shard_map/all_gather | solution.py:236
  110.6 4.8 %copy-start = (s32[16,2,4,1,24]{4,3,2,1,0:T(1,128)S(1)}, s32[16,2,4,1,24]{4,3,2,1,0:T(1,128)}, u32[]{:S(2)}) copy-start(s32[16,2,4,1,24]{4,3,2,1,0:T(1,128)} %get-tuple-element.11) | copy-start | bytes 36868
Sparse Core Ops, SparseCore 0:
  25.3 91.1 all-gather.1

commit v14 on v13

--- a/solution.py
+++ b/solution.py
@@ -165,13 +165,14 @@
     )(activations, codes, colsum)
 
 
-def _col_piece_kernel(n_col, x_ref, code_ref, o_ref, code_out, send_sem, recv_sem, lsem):
+def _col_piece_kernel(n_col, x_ref, tenant_ref, label_ref, o_ref, code_out, send_sem, recv_sem, lsem):
     r = lax.axis_index("row")
     c = lax.axis_index("col")
     width = o_ref.shape[-1]
     barrier = pltpu.get_barrier_semaphore()
     for k in range(1, n_col):
         pl.semaphore_signal(barrier, 1, device_id=(r, lax.rem(c + k, n_col)), device_id_type=MESH)
+    code_out[...] = tenant_ref[...] * LABELS + label_ref[...]
     pl.semaphore_wait(barrier, n_col - 1)
     own = pltpu.make_async_copy(
         x_ref.at[:, pl.ds(pl.multiple_of(c * width, width), width)], o_ref.at[c], lsem.at[0])
@@ -189,33 +190,31 @@
         )
         cp.start()
         copies.append(cp)
-    keep = pltpu.make_async_copy(code_ref, code_out, lsem.at[1])
-    keep.start()
     own.wait()
-    keep.wait()
     for cp in copies:
         cp.wait()
 
 
-def _col_piece(activations, codes, n_col):
+def _col_piece(activations, tenant_ids, concept_labels, n_col):
     tokens = activations.shape[0]
     width = activations.shape[1] // n_col
     any_spec = pl.BlockSpec(memory_space=pl.ANY)
+    vmem_spec = pl.BlockSpec(memory_space=pltpu.VMEM)
     return pl.pallas_call(
         functools.partial(_col_piece_kernel, n_col),
         out_shape=(
             jax.ShapeDtypeStruct((n_col, tokens, width), activations.dtype),
-            jax.ShapeDtypeStruct(codes.shape, codes.dtype),
+            jax.ShapeDtypeStruct((1, tokens), jnp.int32),
         ),
-        in_specs=[any_spec, any_spec],
-        out_specs=(any_spec, any_spec),
+        in_specs=[any_spec, vmem_spec, vmem_spec],
+        out_specs=(any_spec, vmem_spec),
         scratch_shapes=[
             pltpu.SemaphoreType.DMA((n_col - 1,)),
             pltpu.SemaphoreType.DMA((n_col - 1,)),
-            pltpu.SemaphoreType.DMA((2,)),
+            pltpu.SemaphoreType.DMA((1,)),
         ],
         compiler_params=pltpu.CompilerParams(collective_id=1, has_side_effects=True),
-    )(activations, codes)
+    )(activations, tenant_ids.reshape(1, tokens), concept_labels.reshape(1, tokens))
 
 
 def _column_sum(panel):
@@ -230,8 +229,7 @@
     col_count = lax.axis_size("col")
     n_x = col_count // Z_HI
     groups = TENANTS * LABELS
-    codes = tenant_ids * LABELS + concept_labels
-    col_piece, codes = _col_piece(activations, codes.reshape(1, local_tokens), col_count)
+    col_piece, codes = _col_piece(activations, tenant_ids, concept_labels, col_count)
     col_piece = col_piece.reshape(col_count * local_tokens, col_piece.shape[-1])
     col_panel = lax.all_gather(col_piece, "row", axis=0, tiled=True)
     colsum = jnp.sum(col_piece, axis=0, dtype=jnp.float32, keepdims=True)

time: 145 us -> 145 us (level)
  Pallas kernels: 100 us -> 102 us
where the time goes in v14:
time: 145 us
  Pallas kernels  102 us (70%)
  matrix products  25.5 us (18%)
  between operations  14.1 us (10%)
  other arithmetic  3.46 us (2%)
    pallas_call x1, Pallas kernels, _row_panel(): pl.pallas_call(functools.partial(_row_panel_kernel, n_row, n_x), out_shap...  83.5 us
    dot_general x1, matrix products, shards(): jnp.einsum('tf,tg->fg', row_panel, col_panel, preferred_element_type=jnp....  18.9 us
    pallas_call x1, Pallas kernels, _col_piece(): pl.pallas_call(functools.partial(_col_piece_kernel, n_col), out_shape=(ja...  18 us
    dot_general x1, matrix products, _column_sum(): return jnp.dot(ones, panel, preferred_element_type=jnp.float32)[0]  3.77 us
  transfers between devices with their start and end apart: 1, of which 0 were waited for; matrix products, arithmetic and copies ran while one was open for 7% of the time, Pallas kernels for 58%

profile of v14, /device:TPU:1, one launch (start us, length us, event | category | flops | bytes accessed | tf_op | source)
XLA Modules:
  0.0 144.7 jit_solution(3995937286125400705)
XLA Ops:
  7.2 0.0 all-gather.2.cloned.1.call-start
  7.2 18.0 %shard_map.50 = (bf16[8,24,2048]{2,1,0:T(8,128)(2,1)}, s32[1,24]{1,0:T(1,128)}) custom-call(bf16[24,16384]{1,0:T(8,128)(2,1)} %x_ref.3, s32[1,24]{1,0:T(1,128)} %bitcast.27, s32[1,24]{1,0:T(1,128)} %bitcast.28), custom_call_target="tpu_custom_call" | custom-call | tf_op jit(solution)/shard_map/pallas_call | solution.py:203
  25.3 0.0 all-gather.2.cloned.1.call-update
  25.3 1.9 %convert_reduce_fusion.1 = f32[2048]{0:T(1024)} fusion(bf16[8,24,2048]{2,1,0:T(8,128)(2,1)} %get-tuple-element.8), kind=kLoop, calls=%fused_computation.4 | loop fusion | flops 784384 | bytes 794624 | tf_op jit(solution)/shard_map/reduce_sum | solution.py:235
  27.1 83.5 %shard_map.51 = (bf16[16,2,4,24,1024]{4,3,2,1,0:T(8,128)(2,1)}, s32[16,2,4,1,24]{4,3,2,1,0:T(1,128)}, f32[16,1,2048]{2,1,0:T(1,128)}) custom-call(bf16[24,16384]{1,0:T(8,128)(2,1)} %x_ref.3, s32[1,24]{1,0:T(1,128)} %get-tuple-element.7.code_ref, f32[1,2048]{1,0:T(1,128)} %bitcast.25), custom_call_target="tpu_custom_call" | custom-call | tf_op jit(solution)/shard_map/pallas_call | solution.py:142
  110.7 0.0 copy-start
  110.7 1.0 reduce_sum.32
  111.7 3.8 %convolution_multiply_fusion = f32[1,1024]{1,0:T(1,128)S(1)} fusion(bf16[3072,1024]{1,0:T(8,128)(2,1)} %bitcast.20), kind=kOutput, calls=%fused_computation.9 | convolution fusion | flops 6292480 | bytes 6295552 | tf_op jit(solution)/shard_map/dot_general | solution.py:222
  115.5 0.0 copy-done
  115.5 0.6 convert_reduce_fusion
  116.1 2.8 %fusion.3 = f32[128,128]{1,0:T(8,128)} fusion(f32[128]{0:T(128)S(1)} %dynamic-slice_bitcast_fusion, f32[128]{0:T(128)S(1)} %convert_reduce_fusion, bf16[16,2,4,24,1024]{4,3,2,1,0:T(8,128)(2,1)} %get-tuple-element.9, s32[]{:T(128)S(6)} %select_n.4, s32[16,2,4,24]{3,2,1,0:T(4,128)S(1)} %bitcast.24), kind=kOutput, calls=%fused_computation.8 | convolution fusion | flops 101105664 | bytes 865284 | tf_op jit(solution)/shard_map/rhxotg,rhxtf->gf/dot_general | solution.py:251
  118.9 0.0 all-gather.2.cloned.1.call-done
  118.9 18.9 %multiply_subtract_fusion = f32[1024,2048]{1,0:T(8,128)} fusion(bf16[3072,1024]{1,0:T(8,128)(2,1)} %bitcast.21, bf16[3072,2048]{1,0:T(8,128)(2,1)} %all-gather.2.cloned.1.call-done, f32[2048]{0:T(1024)S(1)} %broadcast_multiply_fusion, f32[1024]{0:T(1024)S(1)} %bitcast.26), kind=kOutput, calls=%fused_computation | convolution fusion | flops 12891193344 | bytes 27275264 | tf_op jit(solution)/shard_map/tf,tg->fg/dot_general | solution.py:240
  (2 shorter events, 0.0 us)
Async XLA Ops:
  7.2 111.8 %all-gather.2.cloned.1.call-start = ((), (), s32[]{:S(2)}) async-start(), calls=%async_computation | async-start | bytes 13369344 | tf_op jit(solution)/shard_map/all_gather | solution.py:234
  110.7 4.8 %copy-start = (s32[16,2,4,1,24]{4,3,2,1,0:T(1,128)S(1)}, s32[16,2,4,1,24]{4,3,2,1,0:T(1,128)}, u32[]{:S(2)}) copy-start(s32[16,2,4,1,24]{4,3,2,1,0:T(1,128)} %get-tuple-element.11) | copy-start | bytes 36868
Sparse Core Ops, SparseCore 0:
  25.4 91.1 all-gather.1

commit v15 on v13

--- a/solution.py
+++ b/solution.py
@@ -41,7 +41,9 @@
     own.start()
     own_codes.start()
     own_sum.start()
-    stage1 = {0: [], 1: []}
+    group = Z_HI * n_row
+    half_rows = n_row // 2
+    stage1 = []
     sums = []
     for i, (dz, dr) in enumerate(sources):
         pr, pc = peer(dz, dr)
@@ -49,7 +51,7 @@
             src_ref=x_ref.at[:, pl.ds(pl.multiple_of(pr * width, width), width)],
             dst_ref=p_ref.at[r, zh, x],
             send_sem=s1.at[i],
-            recv_sem=r1.at[i],
+            recv_sem=r1.at[zh * n_row + r],
             device_id=(pr, pc),
             device_id_type=MESH,
         )
@@ -57,13 +59,13 @@
             src_ref=code_ref,
             dst_ref=pc_ref.at[r, zh, x],
             send_sem=s1c.at[i],
-            recv_sem=r1c.at[i],
+            recv_sem=r1c.at[zh * n_row + r],
             device_id=(pr, pc),
             device_id_type=MESH,
         )
         cp.start()
         cc.start()
-        stage1[1 - min(dz, 1)] += [cp, cc]
+        stage1 += [cp, cc]
         if dz == 0:
             cs = pltpu.make_async_remote_copy(
                 src_ref=cs_ref,
@@ -81,51 +83,69 @@
             src_ref=src, dst_ref=dst, send_sem=sems[0].at[idx], recv_sem=sems[1].at[idx],
             device_id=(r, target), device_id_type=MESH)
 
+    def arrived(plane, row):
+        for ref, sems in ((p_ref, (s1, r1)), (pc_ref, (s1c, r1c))):
+            pltpu.make_async_remote_copy(
+                src_ref=ref.at[row, plane, x], dst_ref=ref.at[row, plane, x],
+                send_sem=sems[0].at[0], recv_sem=sems[1].at[plane * n_row + row],
+                device_id=(r, right), device_id_type=MESH).wait_recv()
+
     own.wait()
     own_codes.wait()
-    halves = []
-    for h, plane in enumerate((1 - zh, zh)):
-        for cp in stage1[h]:
-            cp.wait_recv()
+    parts = [(1 - zh, 0), (1 - zh, half_rows), (zh, 0), (zh, half_rows)]
+    ring = []
+    for k, (plane, row0) in enumerate(parts):
+        for row in range(row0, row0 + half_rows):
+            if k < 2:
+                arrived(plane, row)
+            else:
+                @pl.when(r != row)
+                def _(row=row, plane=plane):
+                    arrived(plane, row)
+        rows = pl.ds(row0, half_rows)
         pair = [
-            send(p_ref.at[:, plane, x], p_ref.at[:, plane, x], (s2, r2), 2 * h, right),
-            send(p_ref.at[:, plane, x], p_ref.at[:, plane, x], (s2, r2), 2 * h + 1, left),
-            send(pc_ref.at[:, plane, x], pc_ref.at[:, plane, x], (s2c, r2c), 2 * h, right),
-            send(pc_ref.at[:, plane, x], pc_ref.at[:, plane, x], (s2c, r2c), 2 * h + 1, left),
+            send(p_ref.at[rows, plane, x], p_ref.at[rows, plane, x], (s2, r2), 2 * k, right),
+            send(p_ref.at[rows, plane, x], p_ref.at[rows, plane, x], (s2, r2), 2 * k + 1, left),
+            send(pc_ref.at[rows, plane, x], pc_ref.at[rows, plane, x], (s2c, r2c), 2 * k, right),
+            send(pc_ref.at[rows, plane, x], pc_ref.at[rows, plane, x], (s2c, r2c), 2 * k + 1, left),
         ]
         for cp in pair:
             cp.start()
-        halves.append(pair)
+        ring.append(pair)
 
     from_left = lax.rem(x + n_x - 1, n_x)
     from_right = lax.rem(x + 1, n_x)
-    halves[0][1].wait_recv()
-    halves[0][3].wait_recv()
-    fwd2 = [
-        send(p_ref.at[:, 1 - zh, from_right], p_ref.at[:, 1 - zh, from_right], (s2, r2), 5, left),
-        send(pc_ref.at[:, 1 - zh, from_right], pc_ref.at[:, 1 - zh, from_right], (s2c, r2c), 5, left),
-    ]
-    for cp in fwd2:
-        cp.start()
-    halves[1][0].wait_recv()
-    halves[1][2].wait_recv()
-    fwd = [
-        send(p_ref.at[:, zh, from_left], p_ref.at[:, zh, from_left], (s2, r2), 4, right),
-        send(pc_ref.at[:, zh, from_left], pc_ref.at[:, zh, from_left], (s2c, r2c), 4, right),
-    ]
-    for cp in fwd:
-        cp.start()
-
-    for cp in stage1[0] + stage1[1]:
+    fwd = []
+    for k, (plane, row0) in enumerate(parts):
+        rows = pl.ds(row0, half_rows)
+        if k < 2:
+            ring[k][1].wait_recv()
+            ring[k][3].wait_recv()
+            src, target, idx = from_right, left, 8 + k
+        else:
+            ring[k][0].wait_recv()
+            ring[k][2].wait_recv()
+            src, target, idx = from_left, right, 8 + k
+        pair = [
+            send(p_ref.at[rows, plane, src], p_ref.at[rows, plane, src], (s2, r2), idx, target),
+            send(pc_ref.at[rows, plane, src], pc_ref.at[rows, plane, src], (s2c, r2c), idx, target),
+        ]
+        for cp in pair:
+            cp.start()
+        fwd += pair
+
+    for cp in stage1:
         cp.wait_send()
-    for pair in halves:
+    for k, pair in enumerate(ring):
         for cp in pair:
             cp.wait_send()
-    halves[0][0].wait_recv()
-    halves[0][2].wait_recv()
-    halves[1][1].wait_recv()
-    halves[1][3].wait_recv()
-    for cp in fwd + fwd2:
+        if k < 2:
+            pair[0].wait_recv()
+            pair[2].wait_recv()
+        else:
+            pair[1].wait_recv()
+            pair[3].wait_recv()
+    for cp in fwd:
         cp.wait()
     own_sum.wait()
     for cp in sums:
@@ -150,13 +170,13 @@
         out_specs=(any_spec, any_spec, any_spec),
         scratch_shapes=[
             pltpu.SemaphoreType.DMA((group - 1,)),
+            pltpu.SemaphoreType.DMA((group,)),
             pltpu.SemaphoreType.DMA((group - 1,)),
-            pltpu.SemaphoreType.DMA((group - 1,)),
-            pltpu.SemaphoreType.DMA((group - 1,)),
-            pltpu.SemaphoreType.DMA((6,)),
-            pltpu.SemaphoreType.DMA((6,)),
-            pltpu.SemaphoreType.DMA((6,)),
-            pltpu.SemaphoreType.DMA((6,)),
+            pltpu.SemaphoreType.DMA((group,)),
+            pltpu.SemaphoreType.DMA((12,)),
+            pltpu.SemaphoreType.DMA((12,)),
+            pltpu.SemaphoreType.DMA((12,)),
+            pltpu.SemaphoreType.DMA((12,)),
             pltpu.SemaphoreType.DMA((n_row - 1,)),
             pltpu.SemaphoreType.DMA((n_row - 1,)),
             pltpu.SemaphoreType.DMA((3,)),

time: 145 us -> 144 us (level)
  no operation moved by 1% of the time
where the time goes in v15:
time: 144 us
  Pallas kernels  99.5 us (69%)
  matrix products  25.5 us (18%)
  between operations  14.1 us (10%)
  other arithmetic  4.65 us (3%)
    pallas_call x1, Pallas kernels, _row_panel(): pl.pallas_call(functools.partial(_row_panel_kernel, n_row, n_x), out_shap...  82.7 us
    dot_general x1, matrix products, shards(): jnp.einsum('tf,tg->fg', row_panel, col_panel, preferred_element_type=jnp....  18.9 us
    pallas_call x1, Pallas kernels, _col_piece(): pl.pallas_call(functools.partial(_col_piece_kernel, n_col), out_shape=(ja...  16.8 us
    dot_general x1, matrix products, _column_sum(): return jnp.dot(ones, panel, preferred_element_type=jnp.float32)[0]  3.77 us
  transfers between devices with their start and end apart: 1, of which 0 were waited for; matrix products, arithmetic and copies ran while one was open for 7% of the time, Pallas kernels for 58%

profile of v15, /device:TPU:1, one launch (start us, length us, event | category | flops | bytes accessed | tf_op | source)
XLA Modules:
  0.0 143.8 jit_solution(569782947837788055)
XLA Ops:
  7.2 0.0 all-gather.2.cloned.1.call-start
  7.2 1.2 add_bitcast_fusion.code_ref
  8.4 16.8 %shard_map.50 = (bf16[8,24,2048]{2,1,0:T(8,128)(2,1)}, s32[1,24]{1,0:T(1,128)}) custom-call(bf16[24,16384]{1,0:T(8,128)(2,1)} %x_ref.3, s32[1,24]{1,0:T(1,128)} %add_bitcast_fusion.code_ref), custom_call_target="tpu_custom_call" | custom-call | tf_op jit(solution)/shard_map/pallas_call | solution.py:224
  25.2 0.0 all-gather.2.cloned.1.call-update
  25.2 1.9 %convert_reduce_fusion.1 = f32[2048]{0:T(1024)} fusion(bf16[8,24,2048]{2,1,0:T(8,128)(2,1)} %get-tuple-element.8), kind=kLoop, calls=%fused_computation.4 | loop fusion | flops 784384 | bytes 794624 | tf_op jit(solution)/shard_map/reduce_sum | solution.py:257
  27.1 82.7 %shard_map.51 = (bf16[16,2,4,24,1024]{4,3,2,1,0:T(8,128)(2,1)}, s32[16,2,4,1,24]{4,3,2,1,0:T(1,128)}, f32[16,1,2048]{2,1,0:T(1,128)}) custom-call(bf16[24,16384]{1,0:T(8,128)(2,1)} %x_ref.3, s32[1,24]{1,0:T(1,128)} %get-tuple-element.7.code_ref, f32[1,2048]{1,0:T(1,128)} %bitcast.25), custom_call_target="tpu_custom_call" | custom-call | tf_op jit(solution)/shard_map/pallas_call | solution.py:162
  109.8 0.0 copy-start
  109.8 1.0 reduce_sum.32
  110.8 3.8 %convolution_multiply_fusion = f32[1,1024]{1,0:T(1,128)S(1)} fusion(bf16[3072,1024]{1,0:T(8,128)(2,1)} %bitcast.20), kind=kOutput, calls=%fused_computation.9 | convolution fusion | flops 6292480 | bytes 6295552 | tf_op jit(solution)/shard_map/dot_general | solution.py:243
  114.6 0.0 copy-done
  114.6 0.6 convert_reduce_fusion
  115.2 2.9 %fusion.3 = f32[128,128]{1,0:T(8,128)} fusion(f32[128]{0:T(128)S(1)} %dynamic-slice_bitcast_fusion, f32[128]{0:T(128)S(1)} %convert_reduce_fusion, bf16[16,2,4,24,1024]{4,3,2,1,0:T(8,128)(2,1)} %get-tuple-element.9, s32[]{:T(128)S(6)} %select_n.4, s32[16,2,4,24]{3,2,1,0:T(4,128)S(1)} %bitcast.24), kind=kOutput, calls=%fused_computation.8 | convolution fusion | flops 101105664 | bytes 865284 | tf_op jit(solution)/shard_map/rhxotg,rhxtf->gf/dot_general | solution.py:273
  118.1 0.0 all-gather.2.cloned.1.call-done
  118.1 18.9 %multiply_subtract_fusion = f32[1024,2048]{1,0:T(8,128)} fusion(bf16[3072,1024]{1,0:T(8,128)(2,1)} %bitcast.21, bf16[3072,2048]{1,0:T(8,128)(2,1)} %all-gather.2.cloned.1.call-done, f32[2048]{0:T(1024)S(1)} %broadcast_multiply_fusion, f32[1024]{0:T(1024)S(1)} %bitcast.26), kind=kOutput, calls=%fused_computation | convolution fusion | flops 12891193344 | bytes 27275264 | tf_op jit(solution)/shard_map/tf,tg->fg/dot_general | solution.py:262
  (2 shorter events, 0.0 us)
Async XLA Ops:
  7.2 110.9 %all-gather.2.cloned.1.call-start = ((), (), s32[]{:S(2)}) async-start(), calls=%async_computation | async-start | bytes 13369344 | tf_op jit(solution)/shard_map/all_gather | solution.py:256
  109.8 4.8 %copy-start = (s32[16,2,4,1,24]{4,3,2,1,0:T(1,128)S(1)}, s32[16,2,4,1,24]{4,3,2,1,0:T(1,128)}, u32[]{:S(2)}) copy-start(s32[16,2,4,1,24]{4,3,2,1,0:T(1,128)} %get-tuple-element.11) | copy-start | bytes 36868
Sparse Core Ops, SparseCore 0:
  25.3 91.1 all-gather.1

commit v16 on v15

--- a/solution.py
+++ b/solution.py
@@ -13,8 +13,8 @@
 Z_HI = 2
 
 
-def _row_panel_kernel(n_row, n_x, x_ref, code_ref, cs_ref, p_ref, pc_ref, cs_out,
-                      s1, r1, s1c, r1c, s2, r2, s2c, r2c, s3, r3, lsem):
+def _row_panel_kernel(n_row, n_x, x_ref, code_ref, cs_ref, p_ref, pc_ref, cs_out, cs_total,
+                      s1, r1, s1c, r1c, s2, r2, s2c, r2c, s3, r3, lsem, cs_buf):
     r = lax.axis_index("row")
     c = lax.axis_index("col")
     zh = c // n_x
@@ -113,6 +113,14 @@
             cp.start()
         ring.append(pair)
 
+    own_sum.wait()
+    for cp in sums:
+        cp.wait_recv()
+    load = pltpu.make_async_copy(cs_out, cs_buf, lsem.at[3])
+    load.start()
+    load.wait()
+    cs_total[...] = jnp.sum(cs_buf[...], axis=0)
+
     from_left = lax.rem(x + n_x - 1, n_x)
     from_right = lax.rem(x + 1, n_x)
     fwd = []
@@ -147,9 +155,8 @@
             pair[3].wait_recv()
     for cp in fwd:
         cp.wait()
-    own_sum.wait()
     for cp in sums:
-        cp.wait()
+        cp.wait_send()
 
 
 def _row_panel(activations, codes, colsum, n_row, n_col):
@@ -165,9 +172,10 @@
             jax.ShapeDtypeStruct((n_row, Z_HI, n_x, tokens, width), activations.dtype),
             jax.ShapeDtypeStruct((n_row, Z_HI, n_x, 1, tokens), jnp.int32),
             jax.ShapeDtypeStruct((n_row,) + colsum.shape, colsum.dtype),
+            jax.ShapeDtypeStruct(colsum.shape, colsum.dtype),
         ),
         in_specs=[any_spec, any_spec, any_spec],
-        out_specs=(any_spec, any_spec, any_spec),
+        out_specs=(any_spec, any_spec, any_spec, pl.BlockSpec(memory_space=pltpu.VMEM)),
         scratch_shapes=[
             pltpu.SemaphoreType.DMA((group - 1,)),
             pltpu.SemaphoreType.DMA((group,)),
@@ -179,7 +187,8 @@
             pltpu.SemaphoreType.DMA((12,)),
             pltpu.SemaphoreType.DMA((n_row - 1,)),
             pltpu.SemaphoreType.DMA((n_row - 1,)),
-            pltpu.SemaphoreType.DMA((3,)),
+            pltpu.SemaphoreType.DMA((4,)),
+            pltpu.VMEM((n_row,) + colsum.shape, colsum.dtype),
         ],
         compiler_params=pltpu.CompilerParams(collective_id=0, has_side_effects=True),
     )(activations, codes, colsum)
@@ -255,13 +264,13 @@
     col_piece = col_piece.reshape(col_count * local_tokens, col_piece.shape[-1])
     col_panel = lax.all_gather(col_piece, "row", axis=0, tiled=True)
     colsum = jnp.sum(col_piece, axis=0, dtype=jnp.float32, keepdims=True)
-    row_slots, code_slots, col_sums = _row_panel(activations, codes, colsum, row_count, col_count)
+    row_slots, code_slots, _, col_total = _row_panel(activations, codes, colsum, row_count, col_count)
     total = col_panel.shape[0]
     row_width = row_slots.shape[-1]
     row_panel = row_slots.reshape(total, row_width)
     gram = jnp.einsum("tf,tg->fg", row_panel, col_panel, preferred_element_type=jnp.float32)
     mean_row = _column_sum(row_panel) / total
-    mean_col = jnp.sum(col_sums, axis=(0, 1)) / total
+    mean_col = col_total[0] / total
     covariance = gram / total - mean_row[:, None] * mean_col[None, :]
     slice_width = width // (row_count * col_count)
     slice_start = lax.axis_index("col") * slice_width

time: 144 us -> 144 us (level)
  transfers between devices with their start and end apart: 1 -> 1, of which waited for: 0 -> 0; matrix products, arithmetic and copies ran while one was open for 7% -> 6% of each run, Pallas kernels for 58% -> 58%
where the time goes in v16:
time: 144 us; the launch traced here: 143 us
  Pallas kernels  100 us (69%)
  matrix products  25.6 us (18%)
  between operations  14.1 us (10%)
  other arithmetic  3.63 us (3%)
    pallas_call x1, Pallas kernels, _row_panel(): pl.pallas_call(functools.partial(_row_panel_kernel, n_row, n_x), out_shap...  83.3 us
    dot_general x1, matrix products, shards(): jnp.einsum('tf,tg->fg', row_panel, col_panel, preferred_element_type=jnp....  18.9 us
    pallas_call x1, Pallas kernels, _col_piece(): pl.pallas_call(functools.partial(_col_piece_kernel, n_col), out_shape=(ja...  16.8 us
    dot_general x1, matrix products, _column_sum(): return jnp.dot(ones, panel, preferred_element_type=jnp.float32)[0]  3.77 us
  transfers between devices with their start and end apart: 1, of which 0 were waited for; matrix products, arithmetic and copies ran while one was open for 6% of the time, Pallas kernels for 58%

profile of v16, /device:TPU:1, one launch (start us, length us, event | category | flops | bytes accessed | tf_op | source)
XLA Modules:
  0.0 143.5 jit_solution(5263763374699715246)
XLA Ops:
  7.2 0.0 all-gather.2.cloned.1.call-start
  7.2 1.2 add_bitcast_fusion.code_ref
  8.4 16.8 %shard_map.50 = (bf16[8,24,2048]{2,1,0:T(8,128)(2,1)}, s32[1,24]{1,0:T(1,128)}) custom-call(bf16[24,16384]{1,0:T(8,128)(2,1)} %x_ref.3, s32[1,24]{1,0:T(1,128)} %add_bitcast_fusion.code_ref), custom_call_target="tpu_custom_call" | custom-call | tf_op jit(solution)/shard_map/pallas_call | solution.py:233
  25.2 0.0 all-gather.2.cloned.1.call-update
  25.2 1.9 %convert_reduce_fusion.1 = f32[2048]{0:T(1024)} fusion(bf16[8,24,2048]{2,1,0:T(8,128)(2,1)} %get-tuple-element.8), kind=kLoop, calls=%fused_computation.4 | loop fusion | flops 784384 | bytes 794624 | tf_op jit(solution)/shard_map/reduce_sum | solution.py:266
  27.1 83.3 %shard_map.51 = (bf16[16,2,4,24,1024]{4,3,2,1,0:T(8,128)(2,1)}, s32[16,2,4,1,24]{4,3,2,1,0:T(1,128)}, f32[16,1,2048]{2,1,0:T(1,128)}, f32[1,2048]{1,0:T(1,128)}) custom-call(bf16[24,16384]{1,0:T(8,128)(2,1)} %x_ref.3, s32[1,24]{1,0:T(1,128)} %get-tuple-element.7.code_ref, f32[1,2048]{1,0:T(1,128)} %bitcast.26), custom_call_target="tpu_custom_call" | custom-call | tf_op jit(solution)/shard_map/pallas_call | solution.py:169
  110.4 0.0 copy-start
  110.4 0.0 copy-start.1
  110.4 3.8 %convolution_multiply_fusion = f32[1,1024]{1,0:T(1,128)S(1)} fusion(bf16[3072,1024]{1,0:T(8,128)(2,1)} %bitcast.21), kind=kOutput, calls=%fused_computation.9 | convolution fusion | flops 6292480 | bytes 6295552 | tf_op jit(solution)/shard_map/dot_general | solution.py:252
  114.2 0.0 copy-done
  114.2 0.6 convert_reduce_fusion
  114.8 2.8 %fusion.3 = f32[128,128]{1,0:T(8,128)} fusion(f32[128]{0:T(128)S(1)} %dynamic-slice_bitcast_fusion, f32[128]{0:T(128)S(1)} %convert_reduce_fusion, bf16[16,2,4,24,1024]{4,3,2,1,0:T(8,128)(2,1)} %get-tuple-element.9, s32[]{:T(128)S(6)} %select_n.4, s32[16,2,4,24]{3,2,1,0:T(4,128)S(1)} %bitcast.25), kind=kOutput, calls=%fused_computation.8 | convolution fusion | flops 101105664 | bytes 865284 | tf_op jit(solution)/shard_map/rhxotg,rhxtf->gf/dot_general | solution.py:282
  117.6 0.0 copy-done.1
  117.6 0.0 all-gather.2.cloned.1.call-done
  117.7 18.9 %multiply_subtract_fusion = f32[1024,2048]{1,0:T(8,128)} fusion(bf16[3072,1024]{1,0:T(8,128)(2,1)} %bitcast.22, bf16[3072,2048]{1,0:T(8,128)(2,1)} %all-gather.2.cloned.1.call-done, f32[2048]{0:T(1024)S(1)} %bitcast.27, f32[1024]{0:T(1024)S(1)} %bitcast.28), kind=kOutput, calls=%fused_computation | convolution fusion | flops 12891193344 | bytes 27275264 | tf_op jit(solution)/shard_map/tf,tg->fg/dot_general | solution.py:271
  (2 shorter events, 0.0 us)
Async XLA Ops:
  7.2 110.5 %all-gather.2.cloned.1.call-start = ((), (), s32[]{:S(2)}) async-start(), calls=%async_computation | async-start | bytes 13369344 | tf_op jit(solution)/shard_map/all_gather | solution.py:265
  110.4 3.8 %copy-start = (s32[16,2,4,1,24]{4,3,2,1,0:T(1,128)S(1)}, s32[16,2,4,1,24]{4,3,2,1,0:T(1,128)}, u32[]{:S(2)}) copy-start(s32[16,2,4,1,24]{4,3,2,1,0:T(1,128)} %get-tuple-element.11) | copy-start | bytes 36868
  110.4 7.2 %copy-start.1 = (f32[1,2048]{1,0:T(1,128)S(1)}, f32[1,2048]{1,0:T(1,128)}, u32[]{:S(2)}) copy-start(f32[1,2048]{1,0:T(1,128)} %get-tuple-element.10) | copy-start | bytes 24580
Sparse Core Ops, SparseCore 0:
  25.3 91.1 all-gather.1

commit v17 on v16

--- a/solution.py
+++ b/solution.py
@@ -194,7 +194,7 @@
     )(activations, codes, colsum)
 
 
-def _col_piece_kernel(n_col, x_ref, code_ref, o_ref, code_out, send_sem, recv_sem, lsem):
+def _col_piece_kernel(n_col, x_ref, o_ref, send_sem, recv_sem, lsem):
     r = lax.axis_index("row")
     c = lax.axis_index("col")
     width = o_ref.shape[-1]
@@ -218,33 +218,27 @@
         )
         cp.start()
         copies.append(cp)
-    keep = pltpu.make_async_copy(code_ref, code_out, lsem.at[1])
-    keep.start()
     own.wait()
-    keep.wait()
     for cp in copies:
         cp.wait()
 
 
-def _col_piece(activations, codes, n_col):
+def _col_piece(activations, n_col):
     tokens = activations.shape[0]
     width = activations.shape[1] // n_col
     any_spec = pl.BlockSpec(memory_space=pl.ANY)
     return pl.pallas_call(
         functools.partial(_col_piece_kernel, n_col),
-        out_shape=(
-            jax.ShapeDtypeStruct((n_col, tokens, width), activations.dtype),
-            jax.ShapeDtypeStruct(codes.shape, codes.dtype),
-        ),
-        in_specs=[any_spec, any_spec],
-        out_specs=(any_spec, any_spec),
+        out_shape=jax.ShapeDtypeStruct((n_col, tokens, width), activations.dtype),
+        in_specs=[any_spec],
+        out_specs=any_spec,
         scratch_shapes=[
             pltpu.SemaphoreType.DMA((n_col - 1,)),
             pltpu.SemaphoreType.DMA((n_col - 1,)),
             pltpu.SemaphoreType.DMA((2,)),
         ],
         compiler_params=pltpu.CompilerParams(collective_id=1, has_side_effects=True),
-    )(activations, codes)
+    )(activations)
 
 
 def _column_sum(panel):
@@ -260,7 +254,8 @@
     n_x = col_count // Z_HI
     groups = TENANTS * LABELS
     codes = tenant_ids * LABELS + concept_labels
-    col_piece, codes = _col_piece(activations, codes.reshape(1, local_tokens), col_count)
+    codes = codes.reshape(1, local_tokens)
+    col_piece = _col_piece(activations, col_count)
     col_piece = col_piece.reshape(col_count * local_tokens, col_piece.shape[-1])
     col_panel = lax.all_gather(col_piece, "row", axis=0, tiled=True)
     colsum = jnp.sum(col_piece, axis=0, dtype=jnp.float32, keepdims=True)

time: 144 us -> 145 us (level)
  transfers between devices with their start and end apart: 1 -> 1, of which waited for: 0 -> 0; matrix products, arithmetic and copies ran while one was open for 6% -> 7% of each run, Pallas kernels for 58% -> 58%
where the time goes in v17:
time: 145 us; the launch traced here: 144 us
  Pallas kernels  101 us (70%)
  matrix products  25.6 us (18%)
  between operations  14.1 us (10%)
  other arithmetic  3.63 us (3%)
    pallas_call x1, Pallas kernels, _row_panel(): pl.pallas_call(functools.partial(_row_panel_kernel, n_row, n_x), out_shap...  84 us
    dot_general x1, matrix products, shards(): jnp.einsum('tf,tg->fg', row_panel, col_panel, preferred_element_type=jnp....  18.9 us
    pallas_call x1, Pallas kernels, _col_piece(): pl.pallas_call(functools.partial(_col_piece_kernel, n_col), out_shape=jax...  16.9 us
    dot_general x1, matrix products, _column_sum(): return jnp.dot(ones, panel, preferred_element_type=jnp.float32)[0]  3.8 us
  transfers between devices with their start and end apart: 1, of which 0 were waited for; matrix products, arithmetic and copies ran while one was open for 7% of the time, Pallas kernels for 58%

profile of v17, /device:TPU:1, one launch (start us, length us, event | category | flops | bytes accessed | tf_op | source)
XLA Modules:
  0.0 144.3 jit_solution(7092198416813573913)
XLA Ops:
  7.2 0.0 all-gather.2.cloned.1.call-start
  7.2 16.9 %shard_map.50 = bf16[8,24,2048]{2,1,0:T(8,128)(2,1)} custom-call(bf16[24,16384]{1,0:T(8,128)(2,1)} %x_ref.3), custom_call_target="tpu_custom_call" | custom-call | tf_op jit(solution)/shard_map/pallas_call | solution.py:230
  24.1 0.0 all-gather.2.cloned.1.call-update
  24.1 1.9 %convert_reduce_fusion.1 = f32[2048]{0:T(1024)} fusion(bf16[8,24,2048]{2,1,0:T(8,128)(2,1)} %shard_map.50), kind=kLoop, calls=%fused_computation.4 | loop fusion | flops 784384 | bytes 794624 | tf_op jit(solution)/shard_map/reduce_sum | solution.py:261
  26.0 1.2 add_bitcast_fusion.code_ref
  27.2 84.0 %shard_map.51 = (bf16[16,2,4,24,1024]{4,3,2,1,0:T(8,128)(2,1)}, s32[16,2,4,1,24]{4,3,2,1,0:T(1,128)}, f32[16,1,2048]{2,1,0:T(1,128)}, f32[1,2048]{1,0:T(1,128)}) custom-call(bf16[24,16384]{1,0:T(8,128)(2,1)} %x_ref.3, s32[1,24]{1,0:T(1,128)} %add_bitcast_fusion.code_ref, f32[1,2048]{1,0:T(1,128)} %bitcast.26), custom_call_target="tpu_custom_call" | custom-call | tf_op jit(solution)/shard_map/pallas_call | solution.py:169
  111.2 0.0 copy-start
  111.2 0.0 copy-start.1
  111.2 3.8 %convolution_multiply_fusion = f32[1,1024]{1,0:T(1,128)S(1)} fusion(bf16[3072,1024]{1,0:T(8,128)(2,1)} %bitcast.22), kind=kOutput, calls=%fused_computation.9 | convolution fusion | flops 6292480 | bytes 6295552 | tf_op jit(solution)/shard_map/dot_general | solution.py:246
  115.0 0.0 copy-done
  115.0 0.6 convert_reduce_fusion
  115.6 2.8 %fusion.3 = f32[128,128]{1,0:T(8,128)} fusion(f32[128]{0:T(128)S(1)} %dynamic-slice_bitcast_fusion, f32[128]{0:T(128)S(1)} %convert_reduce_fusion, bf16[16,2,4,24,1024]{4,3,2,1,0:T(8,128)(2,1)} %get-tuple-element.5, s32[]{:T(128)S(6)} %select_n.4, s32[16,2,4,24]{3,2,1,0:T(4,128)S(1)} %bitcast.25), kind=kOutput, calls=%fused_computation.8 | convolution fusion | flops 101105664 | bytes 865284 | tf_op jit(solution)/shard_map/rhxotg,rhxtf->gf/dot_general | solution.py:277
  118.5 0.0 copy-done.1
  118.5 0.0 all-gather.2.cloned.1.call-done
  118.5 18.9 %multiply_subtract_fusion = f32[1024,2048]{1,0:T(8,128)} fusion(bf16[3072,1024]{1,0:T(8,128)(2,1)} %bitcast.23, bf16[3072,2048]{1,0:T(8,128)(2,1)} %all-gather.2.cloned.1.call-done, f32[2048]{0:T(1024)S(1)} %bitcast.27, f32[1024]{0:T(1024)S(1)} %bitcast.28), kind=kOutput, calls=%fused_computation | convolution fusion | flops 12891193344 | bytes 27275264 | tf_op jit(solution)/shard_map/tf,tg->fg/dot_general | solution.py:266
  (2 shorter events, 0.0 us)
Async XLA Ops:
  7.2 111.3 %all-gather.2.cloned.1.call-start = ((), (), s32[]{:S(2)}) async-start(), calls=%async_computation | async-start | bytes 13369344 | tf_op jit(solution)/shard_map/all_gather | solution.py:260
  111.2 3.8 %copy-start = (s32[16,2,4,1,24]{4,3,2,1,0:T(1,128)S(1)}, s32[16,2,4,1,24]{4,3,2,1,0:T(1,128)}, u32[]{:S(2)}) copy-start(s32[16,2,4,1,24]{4,3,2,1,0:T(1,128)} %get-tuple-element.7) | copy-start | bytes 36868
  111.2 7.2 %copy-start.1 = (f32[1,2048]{1,0:T(1,128)S(1)}, f32[1,2048]{1,0:T(1,128)}, u32[]{:S(2)}) copy-start(f32[1,2048]{1,0:T(1,128)} %get-tuple-element.6) | copy-start | bytes 24580
Sparse Core Ops, SparseCore 0:
  24.2 91.6 all-gather.1

commit v18 on v16

--- a/solution.py
+++ b/solution.py
@@ -113,14 +113,6 @@
             cp.start()
         ring.append(pair)
 
-    own_sum.wait()
-    for cp in sums:
-        cp.wait_recv()
-    load = pltpu.make_async_copy(cs_out, cs_buf, lsem.at[3])
-    load.start()
-    load.wait()
-    cs_total[...] = jnp.sum(cs_buf[...], axis=0)
-
     from_left = lax.rem(x + n_x - 1, n_x)
     from_right = lax.rem(x + 1, n_x)
     fwd = []
@@ -141,6 +133,14 @@
         for cp in pair:
             cp.start()
         fwd += pair
+
+    own_sum.wait()
+    for cp in sums:
+        cp.wait_recv()
+    load = pltpu.make_async_copy(cs_out, cs_buf, lsem.at[3])
+    load.start()
+    load.wait()
+    cs_total[...] = jnp.sum(cs_buf[...], axis=0)
 
     for cp in stage1:
         cp.wait_send()

time: 144 us -> 144 us (level)
  no operation moved by 1% of the time
where the time goes in v18:
time: 144 us; the launch traced here: 143 us
  Pallas kernels  100 us (69%)
  matrix products  25.6 us (18%)
  between operations  14.1 us (10%)
  other arithmetic  3.63 us (3%)
    pallas_call x1, Pallas kernels, _row_panel(): pl.pallas_call(functools.partial(_row_panel_kernel, n_row, n_x), out_shap...  83.3 us
    dot_general x1, matrix products, shards(): jnp.einsum('tf,tg->fg', row_panel, col_panel, preferred_element_type=jnp....  18.9 us
    pallas_call x1, Pallas kernels, _col_piece(): pl.pallas_call(functools.partial(_col_piece_kernel, n_col), out_shape=(ja...  16.8 us
    dot_general x1, matrix products, _column_sum(): return jnp.dot(ones, panel, preferred_element_type=jnp.float32)[0]  3.77 us
  transfers between devices with their start and end apart: 1, of which 0 were waited for; matrix products, arithmetic and copies ran while one was open for 6% of the time, Pallas kernels for 58%

profile of v18, /device:TPU:1, one launch (start us, length us, event | category | flops | bytes accessed | tf_op | source)
XLA Modules:
  0.0 143.5 jit_solution(4310804307350913960)
XLA Ops:
  7.2 0.0 all-gather.2.cloned.1.call-start
  7.2 1.2 add_bitcast_fusion.code_ref
  8.4 16.8 %shard_map.50 = (bf16[8,24,2048]{2,1,0:T(8,128)(2,1)}, s32[1,24]{1,0:T(1,128)}) custom-call(bf16[24,16384]{1,0:T(8,128)(2,1)} %x_ref.3, s32[1,24]{1,0:T(1,128)} %add_bitcast_fusion.code_ref), custom_call_target="tpu_custom_call" | custom-call | tf_op jit(solution)/shard_map/pallas_call | solution.py:233
  25.2 0.0 all-gather.2.cloned.1.call-update
  25.2 1.9 %convert_reduce_fusion.1 = f32[2048]{0:T(1024)} fusion(bf16[8,24,2048]{2,1,0:T(8,128)(2,1)} %get-tuple-element.8), kind=kLoop, calls=%fused_computation.4 | loop fusion | flops 784384 | bytes 794624 | tf_op jit(solution)/shard_map/reduce_sum | solution.py:266
  27.1 83.3 %shard_map.51 = (bf16[16,2,4,24,1024]{4,3,2,1,0:T(8,128)(2,1)}, s32[16,2,4,1,24]{4,3,2,1,0:T(1,128)}, f32[16,1,2048]{2,1,0:T(1,128)}, f32[1,2048]{1,0:T(1,128)}) custom-call(bf16[24,16384]{1,0:T(8,128)(2,1)} %x_ref.3, s32[1,24]{1,0:T(1,128)} %get-tuple-element.7.code_ref, f32[1,2048]{1,0:T(1,128)} %bitcast.26), custom_call_target="tpu_custom_call" | custom-call | tf_op jit(solution)/shard_map/pallas_call | solution.py:169
  110.4 0.0 copy-start
  110.4 0.0 copy-start.1
  110.4 3.8 %convolution_multiply_fusion = f32[1,1024]{1,0:T(1,128)S(1)} fusion(bf16[3072,1024]{1,0:T(8,128)(2,1)} %bitcast.21), kind=kOutput, calls=%fused_computation.9 | convolution fusion | flops 6292480 | bytes 6295552 | tf_op jit(solution)/shard_map/dot_general | solution.py:252
  114.2 0.0 copy-done
  114.2 0.6 convert_reduce_fusion
  114.8 2.8 %fusion.3 = f32[128,128]{1,0:T(8,128)} fusion(f32[128]{0:T(128)S(1)} %dynamic-slice_bitcast_fusion, f32[128]{0:T(128)S(1)} %convert_reduce_fusion, bf16[16,2,4,24,1024]{4,3,2,1,0:T(8,128)(2,1)} %get-tuple-element.9, s32[]{:T(128)S(6)} %select_n.4, s32[16,2,4,24]{3,2,1,0:T(4,128)S(1)} %bitcast.25), kind=kOutput, calls=%fused_computation.8 | convolution fusion | flops 101105664 | bytes 865284 | tf_op jit(solution)/shard_map/rhxotg,rhxtf->gf/dot_general | solution.py:282
  117.6 0.0 copy-done.1
  117.6 0.0 all-gather.2.cloned.1.call-done
  117.7 18.9 %multiply_subtract_fusion = f32[1024,2048]{1,0:T(8,128)} fusion(bf16[3072,1024]{1,0:T(8,128)(2,1)} %bitcast.22, bf16[3072,2048]{1,0:T(8,128)(2,1)} %all-gather.2.cloned.1.call-done, f32[2048]{0:T(1024)S(1)} %bitcast.27, f32[1024]{0:T(1024)S(1)} %bitcast.28), kind=kOutput, calls=%fused_computation | convolution fusion | flops 12891193344 | bytes 27275264 | tf_op jit(solution)/shard_map/tf,tg->fg/dot_general | solution.py:271
  (2 shorter events, 0.0 us)
Async XLA Ops:
  7.2 110.5 %all-gather.2.cloned.1.call-start = ((), (), s32[]{:S(2)}) async-start(), calls=%async_computation | async-start | bytes 13369344 | tf_op jit(solution)/shard_map/all_gather | solution.py:265
  110.4 3.8 %copy-start = (s32[16,2,4,1,24]{4,3,2,1,0:T(1,128)S(1)}, s32[16,2,4,1,24]{4,3,2,1,0:T(1,128)}, u32[]{:S(2)}) copy-start(s32[16,2,4,1,24]{4,3,2,1,0:T(1,128)} %get-tuple-element.11) | copy-start | bytes 36868
  110.4 7.2 %copy-start.1 = (f32[1,2048]{1,0:T(1,128)S(1)}, f32[1,2048]{1,0:T(1,128)}, u32[]{:S(2)}) copy-start(f32[1,2048]{1,0:T(1,128)} %get-tuple-element.10) | copy-start | bytes 24580
Sparse Core Ops, SparseCore 0:
  25.3 91.1 all-gather.1
